TPU v7x, 32 devices: a whole 2x2x4 slice. The times are simulated.
32 devices in a mesh: cluster: 16 (over z, x, core), blk: 2 (over y).
Axes of the slice: x: 2, y: 2, z: 4, core: 2. Of those that a mesh axis runs over, the one named last changes fastest.
Arguments:
- coeff: bfloat16 [512, 8, 2048], P('cluster', None, 'blk'), may hold values from -0.375 to 0.375
- intersection: int32 [16, 32], replicated, may hold values from 0 to 511, as said below
- basis_vals: bfloat16 [8192, 256], P(('cluster', 'blk')), may hold values from -6 to 6
- coulomb: bfloat16 [8192, 7, 256], P(('cluster', 'blk')), may hold values from -0.125 to 0.125
- reach: int32 [32], P(('cluster', 'blk')), may hold values from 0 to 3, as said below
Outputs:
- exchange_out: bfloat16 [8192, 2048], P(('cluster', 'blk'))
Inputs may be any that keep to these rules, and one draw needn't show every extreme that they name: `intersection`: each row lists 32 distinct atoms; atom a is owned by cluster a // 32; at most 4 atoms of one row have the same owner, and each row c holds exactly 4 atoms owned by cluster c. `reach`: some block reaches 3 and some block reaches 0.
All inputs are finite; a program needn't handle non-finite values.
Results may differ from a plain program's by a relative error of at most 0.0059.
Values may be sent and summed in bfloat16 or wider, within the bound.
No kernel may reach another device: no remote copies, remote signals or barrier semaphores. Data moves between devices by JAX's collectives and lax.ppermute only.
A program may use at most 64 MiB of HBM per device.

v0:
```python
import jax
import jax.numpy as jnp
from jax import lax
from jax.experimental import pallas as pl
from jax.experimental.pallas import tpu as pltpu
from jax.sharding import PartitionSpec as P


VMEM = pl.BlockSpec(memory_space=pltpu.VMEM)
SMEM = pl.BlockSpec(memory_space=pltpu.SMEM)
PARAMS = pltpu.CompilerParams(vmem_limit_bytes=16 * 2**20)


def passed_along(value, axis, steps):
    count = lax.axis_size(axis)
    pairs = [(source, (source + steps) % count) for source in range(count)]
    return lax.ppermute(value, axis, pairs)


def swapped(value, axis, bits):
    count = lax.axis_size(axis)
    return lax.ppermute(value, axis, [(source, source ^ bits) for source in range(count)])


def split_high_low(value):
    high = value.astype(jnp.bfloat16)
    low = (value - high.astype(jnp.float32)).astype(jnp.bfloat16)
    return high, low


def dot_nn(a, b):
    return lax.dot_general(a, b, (((1,), (0,)), ((), ())), preferred_element_type=jnp.float32)


def dot_nt(a, b):
    return lax.dot_general(a, b, (((1,), (1,)), ((), ())), preferred_element_type=jnp.float32)


def stacked(refs):
    values = [ref[...].reshape(-1, ref.shape[-1]) for ref in refs]
    return values[0] if len(values) == 1 else jnp.concatenate(values, axis=0)


def exchange(offsets, sources, factors, gram, parts, width):
    num_sources = len(sources)
    counts = [len(blocks) for blocks in parts]
    points = sources[0].shape[0]

    def kernel(*refs):
        offset_ref = refs[0]
        basis_refs = refs[1 : 1 + num_sources]
        factor_refs = refs[1 + num_sources : 1 + 2 * num_sources]
        rest = list(refs[1 + 2 * num_sources :])
        total = rest.pop(0)[...] if gram is not None else None
        part_values = []
        for count in counts:
            part_values.append(stacked(rest[:count]))
            rest = rest[count:]
        out_ref = rest[0]
        for values in part_values[0 if gram is None else 1 :]:
            term = dot_nt(values, values)
            total = term if total is None else total + term
        gram_high, gram_low = split_high_low(total)
        own = basis_refs[0][...]
        projected = dot_nn(own, gram_high) + dot_nn(own, gram_low)
        proj_high, proj_low = split_high_low(projected)
        mixed = None
        for source in range(num_sources):
            basis = basis_refs[source][...]
            density = dot_nt(proj_high, basis) + dot_nt(proj_low, basis)
            tile = (density * factor_refs[source][...]).astype(jnp.bfloat16)
            term = dot_nn(tile, basis)
            mixed = term if mixed is None else mixed + term
        mixed_high, mixed_low = split_high_low(mixed)
        for part, values in enumerate(part_values):
            columns = values.shape[1]
            result = dot_nn(mixed_high, values) + dot_nn(mixed_low, values)
            start = pl.multiple_of(offset_ref[part] * columns, columns)
            out_ref[:, pl.ds(start, columns)] = result.astype(out_ref.dtype)

    operands = [offsets, *sources, *factors]
    if gram is not None:
        operands.append(gram)
    for blocks in parts:
        operands.extend(blocks)
    return pl.pallas_call(
        kernel,
        out_shape=jax.ShapeDtypeStruct((points, width), jnp.bfloat16),
        in_specs=[SMEM] + [VMEM] * (len(operands) - 1),
        out_specs=VMEM,
        compiler_params=PARAMS,
        name="exchange",
    )(*operands)


def own_gram(blocks):
    rows = sum(block.shape[0] * block.shape[1] for block in blocks)

    def kernel(*refs):
        values = stacked(refs[:-1])
        refs[-1][...] = dot_nt(values, values)

    return pl.pallas_call(
        kernel,
        out_shape=jax.ShapeDtypeStruct((rows, rows), jnp.float32),
        in_specs=[VMEM] * len(blocks),
        out_specs=VMEM,
        compiler_params=PARAMS,
        name="own_gram",
    )(*blocks)


def outgoing_pieces(coeff, intersection, my_cluster, capacity):
    num_clusters, list_len = intersection.shape
    atom_count, num_funcs, columns = coeff.shape
    slots = num_clusters * capacity
    piece_slots = 2 * capacity
    lanes = 128

    def kernel(me_ref, list_ref, coeff_ref, *out_refs):
        me = me_ref[0]
        local = list_ref[...] - me * atom_count
        mine = jnp.logical_and(local >= 0, local < atom_count)
        ks = lax.broadcasted_iota(jnp.int32, (list_len, list_len), 0)
        ls = lax.broadcasted_iota(jnp.int32, (list_len, list_len), 1)
        earlier = jnp.where(ks < ls, 1.0, 0.0).astype(jnp.bfloat16)
        mine_f = jnp.where(mine, 1.0, 0.0)
        rank = dot_nn(mine_f.astype(jnp.bfloat16), earlier)
        local_f = local.astype(jnp.float32)
        lane = lax.broadcasted_iota(jnp.int32, (num_clusters, lanes), 1)
        source = jnp.zeros((num_clusters, lanes), jnp.float32)
        for slot in range(capacity):
            chosen = jnp.where(jnp.logical_and(mine, rank == slot), local_f, 0.0)
            source = jnp.where(lane == slot, jnp.sum(chosen, axis=1, keepdims=True), source)
        rows = slots * num_funcs
        row = lax.broadcasted_iota(jnp.int32, (rows, num_clusters), 0)
        cluster = lax.broadcasted_iota(jnp.int32, (rows, num_clusters), 1)
        pick = jnp.where(cluster == jnp.bitwise_xor(row // (capacity * num_funcs), me), 1.0, 0.0)
        spread = dot_nn(pick.astype(jnp.bfloat16), source.astype(jnp.bfloat16))
        row = lax.broadcasted_iota(jnp.int32, (rows, lanes), 0)
        lane = lax.broadcasted_iota(jnp.int32, (rows, lanes), 1)
        spread = jnp.where(lane == (row // num_funcs) % capacity, spread, 0.0)
        held = atom_count * num_funcs
        atom = dot_nn(spread.astype(jnp.bfloat16), jnp.ones((lanes, held), jnp.bfloat16))
        row = lax.broadcasted_iota(jnp.int32, (rows, held), 0)
        column = lax.broadcasted_iota(jnp.int32, (rows, held), 1)
        hit = atom.astype(jnp.int32) * num_funcs + row % num_funcs == column
        select = jnp.where(hit, 1.0, 0.0).astype(jnp.bfloat16)
        values = coeff_ref[...].reshape(held, columns)
        step = piece_slots * num_funcs
        for piece, out_ref in enumerate(out_refs):
            result = dot_nn(select[piece * step : (piece + 1) * step], values)
            out_ref[...] = result.astype(jnp.bfloat16).reshape(piece_slots, num_funcs, columns)

    count = num_clusters // 2
    return pl.pallas_call(
        kernel,
        out_shape=[jax.ShapeDtypeStruct((piece_slots, num_funcs, columns), coeff.dtype)] * count,
        in_specs=[SMEM, VMEM, VMEM],
        out_specs=[VMEM] * count,
        compiler_params=PARAMS,
        name="outgoing",
    )(my_cluster.reshape(1), intersection, coeff)


def packed(places, capacity, pieces, direct, relayed, half, carried=None):
    num_funcs, columns = relayed[0].shape[1:]
    count = len(pieces)
    shape = jax.ShapeDtypeStruct((half, num_funcs, columns), relayed[0].dtype)

    def kernel(*refs):
        place_ref = refs[0]
        direct_refs = refs[1 : 1 + count]
        relayed_refs = refs[1 + count : 1 + 2 * count]
        outs = refs[-1:] if carried is not None else refs[-2:]
        for at, piece in enumerate(pieces):
            for core in range(2):
                for slot in range(capacity):
                    place = place_ref[(2 * piece + core) * capacity + slot]
                    from_ref = direct_refs[at] if core == 0 else relayed_refs[at]

                    if carried is None:

                        @pl.when(place < half)
                        def _(place=place, from_ref=from_ref, slot=slot):
                            outs[0][place] = from_ref[slot]

                    @pl.when(jnp.logical_and(place >= half, place < 2 * half))
                    def _(place=place, from_ref=from_ref, slot=slot):
                        outs[-1][place - half] = from_ref[slot]

    operands = [places, *direct, *relayed]
    aliases = {}
    if carried is not None:
        operands.append(carried)
        aliases = {len(operands) - 1: 0}
    return pl.pallas_call(
        kernel,
        out_shape=shape if carried is not None else [shape, shape],
        in_specs=[SMEM] + [VMEM] * (len(operands) - 1),
        out_specs=VMEM if carried is not None else [VMEM, VMEM],
        input_output_aliases=aliases,
        compiler_params=PARAMS,
        name="packed",
    )(*operands)


def screened_factors(coulomb, reach, by_step, norm_factor):
    half_stops = (coulomb.shape[1] - 1) // 2
    points = coulomb.shape[0]
    my_reach = reach[0]
    factors = []
    for step in sorted(by_step):
        total = jnp.zeros((points, coulomb.shape[2]), jnp.float32)
        for offset in by_step[step]:
            tile = coulomb[:, offset + half_stops, :].astype(jnp.float32)
            total = total + jnp.where(abs(offset) <= my_reach, tile, jnp.float32(0.0))
        factors.append(total * norm_factor)
    return factors


def two_blocks(coeff, intersection, basis_vals, factors, capacity):
    num_clusters, list_len = intersection.shape
    atom_count, num_funcs, columns = coeff.shape
    my_cluster = lax.axis_index("cluster")
    my_block = lax.axis_index("blk")
    half = list_len // 2
    pieces = outgoing_pieces(coeff, intersection, my_cluster, capacity)
    count = len(pieces)
    first = list(range(3 * count // 4))
    last = list(range(3 * count // 4, count))
    arrived = [pieces[0]]
    for m in range(1, count):
        arrived.append(swapped(pieces[m], "cluster", 2 * m))

    later, _ = lax.optimization_barrier((intersection, pieces[0]))
    my_row = lax.dynamic_index_in_dim(later, my_cluster, 0, keepdims=False)
    turn = jnp.bitwise_xor(my_row // atom_count, my_cluster)
    key = turn * list_len + jnp.arange(list_len)
    place = jnp.sum((key[None, :] < key[:, None]).astype(jnp.int32), axis=1)
    func = jnp.arange(list_len * num_funcs) % num_funcs
    target = jnp.repeat(place, num_funcs) * num_funcs + func
    order = (target[:, None] == jnp.arange(list_len * num_funcs)[None, :]).astype(jnp.bfloat16)
    mine = dot_nn(basis_vals, order).astype(jnp.bfloat16)

    turns = jnp.arange(num_clusters)
    begin = jnp.sum((turn[None, :] < turns[:, None]).astype(jnp.int32), axis=1)
    end = jnp.sum((turn[None, :] <= turns[:, None]).astype(jnp.int32), axis=1)
    places = begin[:, None] + jnp.arange(capacity)[None, :]
    places = jnp.where(places < end[:, None], places, list_len).reshape(-1)

    sources = [mine, swapped(mine, "blk", 1)]

    relayed = []
    for m in range(count):
        relayed.append(swapped(arrived[m][capacity:], "cluster", 1))

    def group(values, at):
        return [values[m] for m in at]

    low, high = packed(places, capacity, first, group(arrived, first), group(relayed, first), half)
    low_other = swapped(low, "blk", 1)
    high = packed(places, capacity, last, group(arrived, last), group(relayed, last), half, high)
    high_other = swapped(high, "blk", 1)
    gram = own_gram([low, high])
    offsets = jnp.stack([my_block, 1 - my_block])
    return exchange(offsets, sources, factors, gram, [[low, high], [low_other, high_other]], 2 * columns)


def many_blocks(coeff, intersection, basis_vals, factors, capacity, steps):
    num_clusters, list_len = intersection.shape
    atom_count, num_funcs, columns = coeff.shape
    my_cluster = lax.axis_index("cluster")
    num_blocks = lax.axis_size("blk")
    local_atom = intersection - my_cluster * atom_count
    mine = jnp.logical_and(local_atom >= 0, local_atom < atom_count)
    earlier = jnp.arange(list_len)[:, None] < jnp.arange(list_len)[None, :]
    rank = dot_nn(mine.astype(jnp.bfloat16), earlier.astype(jnp.bfloat16)).astype(jnp.int32)
    matches = jnp.logical_and(mine[:, None, :], rank[:, None, :] == jnp.arange(capacity)[None, :, None])
    source_rows = jnp.sum(jnp.where(matches, local_atom[:, None, :], 0), axis=2)
    outgoing = coeff.at[source_rows.reshape(-1)].get(mode="promise_in_bounds")
    outgoing = outgoing.reshape(num_clusters, capacity, num_funcs, columns)
    incoming = lax.all_to_all(outgoing, "cluster", split_axis=0, concat_axis=0, tiled=True)
    my_row = lax.dynamic_index_in_dim(intersection, my_cluster, 0, keepdims=False)
    my_owners = my_row // atom_count
    same = jnp.logical_and(my_owners[:, None] == my_owners[None, :], earlier.T)
    positions = my_owners * capacity + jnp.sum(same.astype(jnp.int32), axis=1)
    needed = incoming.reshape(num_clusters * capacity, num_funcs, columns)
    needed = needed.at[positions].get(mode="promise_in_bounds")
    needed = needed.reshape(list_len * num_funcs, columns)
    all_columns = lax.all_gather(needed, "blk", axis=1, tiled=True)
    sources = [basis_vals if step == 0 else passed_along(basis_vals, "blk", -step) for step in steps]
    offsets = jnp.zeros((1,), jnp.int32)
    return exchange(offsets, sources, factors, None, [[all_columns]], num_blocks * columns)


def on_device(coeff, intersection, basis_vals, coulomb, reach):
    num_clusters = lax.axis_size("cluster")
    num_blocks = lax.axis_size("blk")
    list_len = intersection.shape[1]
    capacity = 2 * list_len // num_clusters
    half_stops = (coulomb.shape[1] - 1) // 2
    by_step = {}
    for offset in range(-half_stops, half_stops + 1):
        by_step.setdefault(offset % num_blocks, []).append(offset)
    factors = screened_factors(coulomb, reach, by_step, (coeff.shape[2] * num_blocks) ** (-0.5))
    if takes_two_blocks(num_clusters, num_blocks):
        return two_blocks(coeff, intersection, basis_vals, factors, capacity)
    return many_blocks(coeff, intersection, basis_vals, factors, capacity, sorted(by_step))


def takes_two_blocks(num_clusters, num_blocks):
    return num_blocks == 2 and num_clusters >= 16 and num_clusters & (num_clusters - 1) == 0


def solution(mesh):
    return jax.shard_map(
        on_device,
        mesh=mesh,
        in_specs=(
            P("cluster", None, "blk"),
            P(),
            P(("cluster", "blk"), None),
            P(("cluster", "blk"), None, None),
            P(("cluster", "blk")),
        ),
        out_specs=P(("cluster", "blk"), None),
        check_vma=False,
    )
```

profile of v0, /device:TPU:16, one launch (start us, length us, event | category | flops | bytes accessed | tf_op | source)
XLA Modules:
  0.0 54.8 jit_solution(6069864154197752031)
XLA Ops:
  0.0 0.0 copy-start
  0.0 0.0 copy-start.2
  0.0 0.7 %copy-done.2 = s32[16,32]{1,0:T(8,128)S(1)} copy-done((s32[16,32]{1,0:T(8,128)S(1)}, s32[16,32]{1,0:T(8,128)}, u32[]{:S(2)}) %copy-start.2) | copy-done | bytes 2072
  0.7 0.0 copy-start.1
  0.7 1.0 %copy-done.1 = bf16[32,8,1024]{2,1,0:T(8,128)(2,1)S(1)} copy-done((bf16[32,8,1024]{2,1,0:T(8,128)(2,1)S(1)}, bf16[32,8,1024]{2,1,0:T(8,128)(2,1)}, u32[]{:S(2)}) %copy-start.1) | copy-done | bytes 524312
  1.8 1.1 %outgoing.1 = (bf16[8,8,1024]{2,1,0:T(8,128)(2,1)S(1)}, bf16[8,8,1024]{2,1,0:T(8,128)(2,1)S(1)}, bf16[8,8,1024]{2,1,0:T(8,128)(2,1)S(1)}, bf16[8,8,1024]{2,1,0:T...) custom-call(s32[1]{0:T(128)} %bitcast.2.me_ref, ...), custom_call_target="tpu_custom_call" | custom-call | tf_op jit(solution)/shard_map/outgoing/pallas_call | solution.py:156
  2.9 1.6 %collective-permute-start.1 = (bf16[8,8,1024]{2,1,0:T(8,128)(2,1)S(1)}, bf16[8,8,1024]{2,1,0:T(8,128)(2,1)S(1)}, u32[]{:S(2)}, u32[]{:S(2)}) collective-permute-start(bf16[8,8,1024]{2,1,0:T(8,128)(2,1)S(1)} %get-tuple-element.18), channel_id=1, source_target_pairs={{0,4},{2,6},{4,0},{6,2},{8,12},{10,14},{12,8},{14,10},{16,20},{18,... | collective-permute-start | bytes 393224 | tf_op jit(solution)/shard_map/ppermute | solution.py:22
  4.5 1.6 %collective-permute-start.2 = (bf16[8,8,1024]{2,1,0:T(8,128)(2,1)S(1)}, bf16[8,8,1024]{2,1,0:T(8,128)(2,1)S(1)}, u32[]{:S(2)}, u32[]{:S(2)}) collective-permute-start(bf16[8,8,1024]{2,1,0:T(8,128)(2,1)S(1)} %get-tuple-element.19), channel_id=1, source_target_pairs={{0,8},{2,10},{4,12},{6,14},{8,0},{10,2},{12,4},{14,6},{16,24},{18,... | collective-permute-start | bytes 393224 | tf_op jit(solution)/shard_map/ppermute | solution.py:22
  6.0 0.4 collective-permute-start.3
  6.5 0.0 collective-permute-start.4
  6.5 3.9 %collective-permute-start.5 = (bf16[8,8,1024]{2,1,0:T(8,128)(2,1)S(1)}, bf16[8,8,1024]{2,1,0:T(8,128)(2,1)S(1)}, u32[]{:S(2)}, u32[]{:S(2)}) collective-permute-start(bf16[8,8,1024]{2,1,0:T(8,128)(2,1)S(1)} %get-tuple-element.22), channel_id=1, source_target_pairs={{0,20},{2,22},{4,16},{6,18},{8,28},{10,30},{12,24},{14,26},{16,4},... | collective-permute-start | bytes 393224 | tf_op jit(solution)/shard_map/ppermute | solution.py:22
  10.4 0.2 convert_reduce_fusion
  10.5 0.1 broadcast_in_dim.28
  10.6 0.1 mul.37
  10.7 0.0 copy-done
  10.7 0.3 fusion.refs_1_
  11.0 0.1 convert_reduce_fusion.1
  11.1 0.0 collective-permute-done.1.refs_2_
  11.1 0.1 collective-permute-start.6
  11.2 1.8 %collective-permute-done.2.refs_3_ = bf16[8,8,1024]{2,1,0:T(8,128)(2,1)S(1)} collective-permute-done((bf16[8,8,1024]{2,1,0:T(8,128)(2,1)S(1)}, bf16[8,8,1024]{2,1,0:T(8,128)(2,1)S(1)}, u32[]{:S(2)}, u32[]{:S(2)}) %collective-permute-start.2) | collective-permute-done | bytes 131104 | tf_op jit(solution)/shard_map/ppermute | solution.py:22
  13.1 0.8 %collective-permute-start.12 = (bf16[8,8,1024]{2,1,0:T(8,128)(2,1)S(1)}, bf16[8,8,1024]{2,1,0:T(8,128)(2,1)S(1)}, u32[]{:S(2)}, u32[]{:S(2)}) collective-permute-start(bf16[8,8,1024]{2,1,0:T(8,128)(2,1)S(1)} %get-tuple-element.24), channel_id=1, source_target_pairs={{0,24},{2,26},{4,28},{6,30},{8,16},{10,18},{12,20},{14,22},{16,8},... | collective-permute-start | bytes 393224 | tf_op jit(solution)/shard_map/ppermute | solution.py:22
  13.9 0.5 collective-permute-done.3.refs_4_
  14.4 0.6 %collective-permute-start.13 = (bf16[8,8,1024]{2,1,0:T(8,128)(2,1)S(1)}, bf16[8,8,1024]{2,1,0:T(8,128)(2,1)S(1)}, u32[]{:S(2)}, u32[]{:S(2)}) collective-permute-start(bf16[8,8,1024]{2,1,0:T(8,128)(2,1)S(1)} %get-tuple-element.25), channel_id=1, source_target_pairs={{0,28},{2,30},{4,24},{6,26},{8,20},{10,22},{12,16},{14,18},{16,12}... | collective-permute-start | bytes 393224 | tf_op jit(solution)/shard_map/ppermute | solution.py:22
  15.0 1.4 %collective-permute-done.4.refs_5_ = bf16[8,8,1024]{2,1,0:T(8,128)(2,1)S(1)} collective-permute-done((bf16[8,8,1024]{2,1,0:T(8,128)(2,1)S(1)}, bf16[8,8,1024]{2,1,0:T(8,128)(2,1)S(1)}, u32[]{:S(2)}, u32[]{:S(2)}) %collective-permute-start.4) | collective-permute-done | bytes 131104 | tf_op jit(solution)/shard_map/ppermute | solution.py:22
  16.4 0.0 collective-permute-start.7
  16.4 7.7 %collective-permute-done.5.refs_6_ = bf16[8,8,1024]{2,1,0:T(8,128)(2,1)S(1)} collective-permute-done((bf16[8,8,1024]{2,1,0:T(8,128)(2,1)S(1)}, bf16[8,8,1024]{2,1,0:T(8,128)(2,1)S(1)}, u32[]{:S(2)}, u32[]{:S(2)}) %collective-permute-start.5) | collective-permute-done | bytes 131104 | tf_op jit(solution)/shard_map/ppermute | solution.py:22
  24.2 0.0 collective-permute-start.8
  24.2 0.1 iota_add_fusion
  24.2 0.1 lt.64
  24.3 0.1 lt.65
  24.4 0.1 add.93
  24.5 5.6 %collective-permute-done.12.refs_1_ = bf16[8,8,1024]{2,1,0:T(8,128)(2,1)S(1)} collective-permute-done((bf16[8,8,1024]{2,1,0:T(8,128)(2,1)S(1)}, bf16[8,8,1024]{2,1,0:T(8,128)(2,1)S(1)}, u32[]{:S(2)}, u32[]{:S(2)}) %collective-permute-start.12) | collective-permute-done | bytes 131104 | tf_op jit(solution)/shard_map/ppermute | solution.py:22
  30.2 0.0 collective-permute-start.9
  30.2 2.3 %collective-permute-done.13.refs_2_ = bf16[8,8,1024]{2,1,0:T(8,128)(2,1)S(1)} collective-permute-done((bf16[8,8,1024]{2,1,0:T(8,128)(2,1)S(1)}, bf16[8,8,1024]{2,1,0:T(8,128)(2,1)S(1)}, u32[]{:S(2)}, u32[]{:S(2)}) %collective-permute-start.13) | collective-permute-done | bytes 131104 | tf_op jit(solution)/shard_map/ppermute | solution.py:22
  32.5 0.0 collective-permute-start.10
  32.5 0.0 collective-permute-done.6.refs_7_
  32.5 0.6 %collective-permute-start.11 = (bf16[4,8,1024]{2,1,0:T(8,128)(2,1)S(1)}, bf16[4,8,1024]{2,1,0:T(8,128)(2,1)S(1)}, u32[]{:S(2)}, u32[]{:S(2)}) collective-permute-start(bf16[4,8,1024]{2,1,0:T(8,128)(2,1)S(1)} %slice.64), channel_id=1, source_target_pairs={{0,2},{2,0},{4,6},{6,4},{8,10},{10,8},{12,14},{14,12},{16,18},{18,... | collective-permute-start | bytes 196616 | tf_op jit(solution)/shard_map/ppermute | solution.py:22
  33.1 0.0 collective-permute-done.7.refs_8_
  33.1 0.1 collective-permute-start.14
  33.1 0.0 collective-permute-done.8.refs_9_
  33.1 0.4 collective-permute-start.15
  34.2 0.0 copy-start.3
  34.2 0.0 collective-permute-done.9.refs_10_
  34.3 1.6 %collective-permute-start = (bf16[256,256]{1,0:T(8,128)(2,1)S(1)}, bf16[256,256]{1,0:T(8,128)(2,1)S(1)}, u32[]{:S(2)}, u32[]{:S(2)}) collective-permute-start(bf16[256,256]{1,0:T(8,128)(2,1)S(1)} %fusion.refs_1_), channel_id=1, source_target_pairs={{0,1},{1,0},{2,3},{3,2},{4,5},{5,4},{6,7},{7,6},{8,9},{9,8},{10,11... | collective-permute-start | bytes 393224 | tf_op jit(solution)/shard_map/ppermute | solution.py:22
  35.8 0.0 collective-permute-done.10.refs_11_
  35.8 0.0 collective-permute-done.11.refs_12_
  35.8 1.2 %packed.2 = (bf16[16,8,1024]{2,1,0:T(8,128)(2,1)S(1)}, bf16[16,8,1024]{2,1,0:T(8,128)(2,1)S(1)}) custom-call(s32[64]{0:T(128)S(1)} %compare_select_fusion.refs_0_, bf16[8,8,1024]{2,1,0:T(8,128)(2,1)S(1)} %get-tuple-element.16.refs_1_, bf16[8,8,1024]{2,1,0:T(8,128)(2,1)S(1)} %collective-permute-done.1.refs_2_, ...), custom_call_target="tpu_custom_call" | custom-call | tf_op jit(solution)/shard_map/packed/pallas_call | solution.py:197
  37.0 0.0 collective-permute-done.14.refs_3_
  37.1 0.0 collective-permute-done.15.refs_4_
  37.1 0.7 %packed.3.refs_1_.refs_7_ = bf16[16,8,1024]{2,1,0:T(8,128)(2,1)S(1)} custom-call(s32[64]{0:T(128)S(1)} %compare_select_fusion.refs_0_, bf16[8,8,1024]{2,1,0:T(8,128)(2,1)S(1)} %collective-permute-done.12.refs_1_, bf16[8,8,1024]{2,1,0:T(8,128)(2,1)S(1)} %collective-permute-done.13.refs_2_, ...), custom_call_target="tpu_custom_call", output_to_operand_aliasing={{}: (5, {})} | custom-call | tf_op jit(solution)/shard_map/packed/pallas_call | solution.py:197
  37.8 0.6 %collective-permute-start.17 = (bf16[16,8,1024]{2,1,0:T(8,128)(2,1)S(1)}, bf16[16,8,1024]{2,1,0:T(8,128)(2,1)S(1)}, u32[]{:S(2)}, u32[]{:S(2)}) collective-permute-start(bf16[16,8,1024]{2,1,0:T(8,128)(2,1)S(1)} %packed.3.refs_1_.refs_7_), channel_id=1, source_target_pairs={{0,1},{1,0},{2,3},{3,2},{4,5},{5,4},{6,7},{7,6},{8,9},{9,8},{10,11... | collective-permute-start | bytes 786440 | tf_op jit(solution)/shard_map/ppermute | solution.py:22
  38.3 1.5 %collective-permute-start.16 = (bf16[16,8,1024]{2,1,0:T(8,128)(2,1)S(1)}, bf16[16,8,1024]{2,1,0:T(8,128)(2,1)S(1)}, u32[]{:S(2)}, u32[]{:S(2)}) collective-permute-start(bf16[16,8,1024]{2,1,0:T(8,128)(2,1)S(1)} %get-tuple-element.23.refs_0_.refs_6_), channel_id=1, source_target_pairs={{0,1},{1,0},{2,3},{3,2},{4,5},{5,4},{6,7},{7,6},{8,9},{9,8},{10,11... | collective-permute-start | bytes 786440 | tf_op jit(solution)/shard_map/ppermute | solution.py:22
  39.8 0.0 copy-done.3
  39.8 0.2 multiply_bitcast_fusion
  40.0 0.1 pad_add_fusion.refs_0_
  40.1 0.3 own_gram.1.refs_5_
  40.5 0.0 collective-permute-done.refs_2_
  40.5 6.5 %collective-permute-done.17.refs_9_ = bf16[16,8,1024]{2,1,0:T(8,128)(2,1)S(1)} collective-permute-done((bf16[16,8,1024]{2,1,0:T(8,128)(2,1)S(1)}, bf16[16,8,1024]{2,1,0:T(8,128)(2,1)S(1)}, u32[]{:S(2)}, u32[]{:S(2)}) %collective-permute-start.17) | collective-permute-done | bytes 262176 | tf_op jit(solution)/shard_map/ppermute | solution.py:22
  47.0 4.5 %collective-permute-done.16.refs_8_ = bf16[16,8,1024]{2,1,0:T(8,128)(2,1)S(1)} collective-permute-done((bf16[16,8,1024]{2,1,0:T(8,128)(2,1)S(1)}, bf16[16,8,1024]{2,1,0:T(8,128)(2,1)S(1)}, u32[]{:S(2)}, u32[]{:S(2)}) %collective-permute-start.16) | collective-permute-done | bytes 262176 | tf_op jit(solution)/shard_map/ppermute | solution.py:22
  51.5 3.4 %exchange.1 = bf16[256,2048]{1,0:T(8,128)(2,1)} custom-call(s32[2]{0:T(128)S(1)} %pad_add_fusion.refs_0_, bf16[256,256]{1,0:T(8,128)(2,1)S(1)} %fusion.refs_1_, bf16[256,256]{1,0:T(8,128)(2,1)S(1)} %collective-permute-done.refs_2_, f32[256,256]{1,0:T(8,128)S(1)} %get-tuple-element.32.refs_3_, f32[256,256]{1,0:T(8,128)S(1)} %get-tuple-element.31.refs_4_, ...), custom_call_target="tpu_custom_call" | custom-call | tf_op jit(solution)/shard_map/exchange/pallas_call | solution.py:86
  (13 shorter events, 0.1 us)
Async XLA Ops:
  0.0 10.7 %copy-start = (bf16[256,256]{1,0:T(8,128)(2,1)S(1)}, bf16[256,256]{1,0:T(8,128)(2,1)}, u32[]{:S(2)}) copy-start(bf16[256,256]{1,0:T(8,128)(2,1)} %param.7) | copy-start | bytes 393220
  0.0 0.7 %copy-start.2 = (s32[16,32]{1,0:T(8,128)S(1)}, s32[16,32]{1,0:T(8,128)}, u32[]{:S(2)}) copy-start(s32[16,32]{1,0:T(8,128)} %list_ref.1) | copy-start | bytes 6148
  0.7 1.0 %copy-start.1 = (bf16[32,8,1024]{2,1,0:T(8,128)(2,1)S(1)}, bf16[32,8,1024]{2,1,0:T(8,128)(2,1)}, u32[]{:S(2)}) copy-start(bf16[32,8,1024]{2,1,0:T(8,128)(2,1)} %coeff_ref.1) | copy-start | bytes 1572868
  2.9 8.2 %collective-permute-start.1 = (bf16[8,8,1024]{2,1,0:T(8,128)(2,1)S(1)}, bf16[8,8,1024]{2,1,0:T(8,128)(2,1)S(1)}, u32[]{:S(2)}, u32[]{:S(2)}) collective-permute-start(bf16[8,8,1024]{2,1,0:T(8,128)(2,1)S(1)} %get-tuple-element.18), channel_id=1, source_target_pairs={{0,4},{2,6},{4,0},{6,2},{8,12},{10,14},{12,8},{14,10},{16,20},{18,... | collective-permute-start | bytes 393224 | tf_op jit(solution)/shard_map/ppermute | solution.py:22
  4.5 8.6 %collective-permute-start.2 = (bf16[8,8,1024]{2,1,0:T(8,128)(2,1)S(1)}, bf16[8,8,1024]{2,1,0:T(8,128)(2,1)S(1)}, u32[]{:S(2)}, u32[]{:S(2)}) collective-permute-start(bf16[8,8,1024]{2,1,0:T(8,128)(2,1)S(1)} %get-tuple-element.19), channel_id=1, source_target_pairs={{0,8},{2,10},{4,12},{6,14},{8,0},{10,2},{12,4},{14,6},{16,24},{18,... | collective-permute-start | bytes 393224 | tf_op jit(solution)/shard_map/ppermute | solution.py:22
  6.0 8.4 %collective-permute-start.3 = (bf16[8,8,1024]{2,1,0:T(8,128)(2,1)S(1)}, bf16[8,8,1024]{2,1,0:T(8,128)(2,1)S(1)}, u32[]{:S(2)}, u32[]{:S(2)}) collective-permute-start(bf16[8,8,1024]{2,1,0:T(8,128)(2,1)S(1)} %get-tuple-element.20), channel_id=1, source_target_pairs={{0,12},{2,14},{4,8},{6,10},{8,4},{10,6},{12,0},{14,2},{16,28},{18,... | collective-permute-start | bytes 393224 | tf_op jit(solution)/shard_map/ppermute | solution.py:22
  6.5 10.0 %collective-permute-start.4 = (bf16[8,8,1024]{2,1,0:T(8,128)(2,1)S(1)}, bf16[8,8,1024]{2,1,0:T(8,128)(2,1)S(1)}, u32[]{:S(2)}, u32[]{:S(2)}) collective-permute-start(bf16[8,8,1024]{2,1,0:T(8,128)(2,1)S(1)} %get-tuple-element.21), channel_id=1, source_target_pairs={{0,16},{2,18},{4,20},{6,22},{8,24},{10,26},{12,28},{14,30},{16,0},... | collective-permute-start | bytes 393224 | tf_op jit(solution)/shard_map/ppermute | solution.py:22
  6.5 17.7 %collective-permute-start.5 = (bf16[8,8,1024]{2,1,0:T(8,128)(2,1)S(1)}, bf16[8,8,1024]{2,1,0:T(8,128)(2,1)S(1)}, u32[]{:S(2)}, u32[]{:S(2)}) collective-permute-start(bf16[8,8,1024]{2,1,0:T(8,128)(2,1)S(1)} %get-tuple-element.22), channel_id=1, source_target_pairs={{0,20},{2,22},{4,16},{6,18},{8,28},{10,30},{12,24},{14,26},{16,4},... | collective-permute-start | bytes 393224 | tf_op jit(solution)/shard_map/ppermute | solution.py:22
  11.1 21.3 %collective-permute-start.6 = (bf16[4,8,1024]{2,1,0:T(8,128)(2,1)S(1)}, bf16[4,8,1024]{2,1,0:T(8,128)(2,1)S(1)}, u32[]{:S(2)}, u32[]{:S(2)}) collective-permute-start(bf16[4,8,1024]{2,1,0:T(8,128)(2,1)S(1)} %slice.52), channel_id=1, source_target_pairs={{0,2},{2,0},{4,6},{6,4},{8,10},{10,8},{12,14},{14,12},{16,18},{18,... | collective-permute-start | bytes 196616 | tf_op jit(solution)/shard_map/ppermute | solution.py:22
  13.1 17.1 %collective-permute-start.12 = (bf16[8,8,1024]{2,1,0:T(8,128)(2,1)S(1)}, bf16[8,8,1024]{2,1,0:T(8,128)(2,1)S(1)}, u32[]{:S(2)}, u32[]{:S(2)}) collective-permute-start(bf16[8,8,1024]{2,1,0:T(8,128)(2,1)S(1)} %get-tuple-element.24), channel_id=1, source_target_pairs={{0,24},{2,26},{4,28},{6,30},{8,16},{10,18},{12,20},{14,22},{16,8},... | collective-permute-start | bytes 393224 | tf_op jit(solution)/shard_map/ppermute | solution.py:22
  14.4 18.0 %collective-permute-start.13 = (bf16[8,8,1024]{2,1,0:T(8,128)(2,1)S(1)}, bf16[8,8,1024]{2,1,0:T(8,128)(2,1)S(1)}, u32[]{:S(2)}, u32[]{:S(2)}) collective-permute-start(bf16[8,8,1024]{2,1,0:T(8,128)(2,1)S(1)} %get-tuple-element.25), channel_id=1, source_target_pairs={{0,28},{2,30},{4,24},{6,26},{8,20},{10,22},{12,16},{14,18},{16,12}... | collective-permute-start | bytes 393224 | tf_op jit(solution)/shard_map/ppermute | solution.py:22
  16.4 16.6 %collective-permute-start.7 = (bf16[4,8,1024]{2,1,0:T(8,128)(2,1)S(1)}, bf16[4,8,1024]{2,1,0:T(8,128)(2,1)S(1)}, u32[]{:S(2)}, u32[]{:S(2)}) collective-permute-start(bf16[4,8,1024]{2,1,0:T(8,128)(2,1)S(1)} %slice.60), channel_id=1, source_target_pairs={{0,2},{2,0},{4,6},{6,4},{8,10},{10,8},{12,14},{14,12},{16,18},{18,... | collective-permute-start | bytes 196616 | tf_op jit(solution)/shard_map/ppermute | solution.py:22
  24.2 9.0 %collective-permute-start.8 = (bf16[4,8,1024]{2,1,0:T(8,128)(2,1)S(1)}, bf16[4,8,1024]{2,1,0:T(8,128)(2,1)S(1)}, u32[]{:S(2)}, u32[]{:S(2)}) collective-permute-start(bf16[4,8,1024]{2,1,0:T(8,128)(2,1)S(1)} %slice.61), channel_id=1, source_target_pairs={{0,2},{2,0},{4,6},{6,4},{8,10},{10,8},{12,14},{14,12},{16,18},{18,... | collective-permute-start | bytes 196616 | tf_op jit(solution)/shard_map/ppermute | solution.py:22
  30.2 4.1 %collective-permute-start.9 = (bf16[4,8,1024]{2,1,0:T(8,128)(2,1)S(1)}, bf16[4,8,1024]{2,1,0:T(8,128)(2,1)S(1)}, u32[]{:S(2)}, u32[]{:S(2)}) collective-permute-start(bf16[4,8,1024]{2,1,0:T(8,128)(2,1)S(1)} %slice.62), channel_id=1, source_target_pairs={{0,2},{2,0},{4,6},{6,4},{8,10},{10,8},{12,14},{14,12},{16,18},{18,... | collective-permute-start | bytes 196616 | tf_op jit(solution)/shard_map/ppermute | solution.py:22
  32.5 3.4 %collective-permute-start.10 = (bf16[4,8,1024]{2,1,0:T(8,128)(2,1)S(1)}, bf16[4,8,1024]{2,1,0:T(8,128)(2,1)S(1)}, u32[]{:S(2)}, u32[]{:S(2)}) collective-permute-start(bf16[4,8,1024]{2,1,0:T(8,128)(2,1)S(1)} %slice.63), channel_id=1, source_target_pairs={{0,2},{2,0},{4,6},{6,4},{8,10},{10,8},{12,14},{14,12},{16,18},{18,... | collective-permute-start | bytes 196616 | tf_op jit(solution)/shard_map/ppermute | solution.py:22
  32.5 3.4 %collective-permute-start.11 = (bf16[4,8,1024]{2,1,0:T(8,128)(2,1)S(1)}, bf16[4,8,1024]{2,1,0:T(8,128)(2,1)S(1)}, u32[]{:S(2)}, u32[]{:S(2)}) collective-permute-start(bf16[4,8,1024]{2,1,0:T(8,128)(2,1)S(1)} %slice.64), channel_id=1, source_target_pairs={{0,2},{2,0},{4,6},{6,4},{8,10},{10,8},{12,14},{14,12},{16,18},{18,... | collective-permute-start | bytes 196616 | tf_op jit(solution)/shard_map/ppermute | solution.py:22
  33.1 4.0 %collective-permute-start.14 = (bf16[4,8,1024]{2,1,0:T(8,128)(2,1)S(1)}, bf16[4,8,1024]{2,1,0:T(8,128)(2,1)S(1)}, u32[]{:S(2)}, u32[]{:S(2)}) collective-permute-start(bf16[4,8,1024]{2,1,0:T(8,128)(2,1)S(1)} %slice.65), channel_id=1, source_target_pairs={{0,2},{2,0},{4,6},{6,4},{8,10},{10,8},{12,14},{14,12},{16,18},{18,... | collective-permute-start | bytes 196616 | tf_op jit(solution)/shard_map/ppermute | solution.py:22
  33.1 3.9 %collective-permute-start.15 = (bf16[4,8,1024]{2,1,0:T(8,128)(2,1)S(1)}, bf16[4,8,1024]{2,1,0:T(8,128)(2,1)S(1)}, u32[]{:S(2)}, u32[]{:S(2)}) collective-permute-start(bf16[4,8,1024]{2,1,0:T(8,128)(2,1)S(1)} %slice.66), channel_id=1, source_target_pairs={{0,2},{2,0},{4,6},{6,4},{8,10},{10,8},{12,14},{14,12},{16,18},{18,... | collective-permute-start | bytes 196616 | tf_op jit(solution)/shard_map/ppermute | solution.py:22
  34.2 5.6 %copy-start.3 = (bf16[256,7,256]{2,0,1:T(8,128)(2,1)S(1)}, bf16[256,7,256]{2,0,1:T(8,128)(2,1)}, u32[]{:S(2)}) copy-start(bf16[256,7,256]{2,0,1:T(8,128)(2,1)} %param.8) | copy-start | bytes 2752516
  34.3 6.2 %collective-permute-start = (bf16[256,256]{1,0:T(8,128)(2,1)S(1)}, bf16[256,256]{1,0:T(8,128)(2,1)S(1)}, u32[]{:S(2)}, u32[]{:S(2)}) collective-permute-start(bf16[256,256]{1,0:T(8,128)(2,1)S(1)} %fusion.refs_1_), channel_id=1, source_target_pairs={{0,1},{1,0},{2,3},{3,2},{4,5},{5,4},{6,7},{7,6},{8,9},{9,8},{10,11... | collective-permute-start | bytes 393224 | tf_op jit(solution)/shard_map/ppermute | solution.py:22
  37.8 9.2 %collective-permute-start.17 = (bf16[16,8,1024]{2,1,0:T(8,128)(2,1)S(1)}, bf16[16,8,1024]{2,1,0:T(8,128)(2,1)S(1)}, u32[]{:S(2)}, u32[]{:S(2)}) collective-permute-start(bf16[16,8,1024]{2,1,0:T(8,128)(2,1)S(1)} %packed.3.refs_1_.refs_7_), channel_id=1, source_target_pairs={{0,1},{1,0},{2,3},{3,2},{4,5},{5,4},{6,7},{7,6},{8,9},{9,8},{10,11... | collective-permute-start | bytes 786440 | tf_op jit(solution)/shard_map/ppermute | solution.py:22
  38.3 13.1 %collective-permute-start.16 = (bf16[16,8,1024]{2,1,0:T(8,128)(2,1)S(1)}, bf16[16,8,1024]{2,1,0:T(8,128)(2,1)S(1)}, u32[]{:S(2)}, u32[]{:S(2)}) collective-permute-start(bf16[16,8,1024]{2,1,0:T(8,128)(2,1)S(1)} %get-tuple-element.23.refs_0_.refs_6_), channel_id=1, source_target_pairs={{0,1},{1,0},{2,3},{3,2},{4,5},{5,4},{6,7},{7,6},{8,9},{9,8},{10,11... | collective-permute-start | bytes 786440 | tf_op jit(solution)/shard_map/ppermute | solution.py:22
where the time goes:
time: 55 us; the launch traced here: 54.8 us
  waiting for transfers between devices  30.5 us (55%)
  starting transfers between devices  13.6 us (25%)
  Pallas kernels  6.7 us (12%)
  local copies, waits for them, and re-layouts  2.25 us (4%)
  between operations  0.86 us (2%)
  other arithmetic  0.67 us (1%)
    ppermute x18, waiting for transfers between devices, swapped(): lax.ppermute(value, axis, [(source, source ^ bits) for source in range(co...  30.5 us
    ppermute x18, starting transfers between devices, swapped(): lax.ppermute(value, axis, [(source, source ^ bits) for source in range(co...  13.6 us
    pallas_call x1, Pallas kernels, exchange(): pl.pallas_call(kernel, out_shape=jax.ShapeDtypeStruct((points, width), jn...  3.38 us
    pallas_call x2, Pallas kernels, packed(): pl.pallas_call(kernel, out_shape=shape if carried is not None else [shape...  1.87 us
    unnamed x8, local copies, waits for them, and re-layouts  1.78 us
    pallas_call x1, Pallas kernels, outgoing_pieces(): pl.pallas_call(kernel, out_shape=[jax.ShapeDtypeStruct((piece_slots, num_...  1.12 us
  transfers between devices with their start and end apart: 18, of which 8 were waited for; matrix products, arithmetic and copies ran while one was open for 3% of the time, Pallas kernels for 4%

commit v1 on v0

v1 whole, which is shorter than its diff:
```python
import jax
import jax.numpy as jnp
from jax import lax
from jax.experimental import pallas as pl
from jax.experimental.pallas import tpu as pltpu
from jax.sharding import PartitionSpec as P


EARLY_PARTS = 5

VMEM = pl.BlockSpec(memory_space=pltpu.VMEM)
SMEM = pl.BlockSpec(memory_space=pltpu.SMEM)
ANY = pl.BlockSpec(memory_space=pl.ANY)
PARAMS = pltpu.CompilerParams(vmem_limit_bytes=16 * 2**20)


def passed_along(value, axis, steps):
    count = lax.axis_size(axis)
    pairs = [(source, (source + steps) % count) for source in range(count)]
    return lax.ppermute(value, axis, pairs)


def swapped(value, axis, bits):
    count = lax.axis_size(axis)
    return lax.ppermute(value, axis, [(source, source ^ bits) for source in range(count)])


def split_high_low(value):
    high = value.astype(jnp.bfloat16)
    low = (value - high.astype(jnp.float32)).astype(jnp.bfloat16)
    return high, low


def dot_nn(a, b):
    return lax.dot_general(a, b, (((1,), (0,)), ((), ())), preferred_element_type=jnp.float32)


def dot_nt(a, b):
    return lax.dot_general(a, b, (((1,), (1,)), ((), ())), preferred_element_type=jnp.float32)


def exchange(starts, sources, factors, gram, known, parts, width):
    num_sources = len(sources)
    num_parts = len(parts)
    points = sources[0].shape[0]
    widths = [part.shape[1] for part in parts]

    def kernel(*refs):
        start_ref = refs[0]
        basis_refs = refs[1 : 1 + num_sources]
        factor_refs = refs[1 + num_sources : 1 + 2 * num_sources]
        rest = list(refs[1 + 2 * num_sources :])
        total = rest.pop(0)[...] if gram is not None else None
        part_refs = rest[:num_parts]
        out_ref = rest[num_parts]
        held_refs = rest[num_parts + 1 : 2 * num_parts + 1]
        sems = rest[-1]
        for part in range(known, num_parts):
            values = part_refs[part][...]
            term = dot_nt(values, values)
            total = term if total is None else total + term
        gram_high, gram_low = split_high_low(total)
        own = basis_refs[0][...]
        projected = dot_nn(own, gram_high) + dot_nn(own, gram_low)
        proj_high, proj_low = split_high_low(projected)
        mixed = None
        for source in range(num_sources):
            basis = basis_refs[source][...]
            density = dot_nt(proj_high, basis) + dot_nt(proj_low, basis)
            tile = (density * factor_refs[source][...]).astype(jnp.bfloat16)
            term = dot_nn(tile, basis)
            mixed = term if mixed is None else mixed + term
        mixed_high, mixed_low = split_high_low(mixed)
        copies = []
        for part in range(num_parts):
            values = part_refs[part][...]
            result = dot_nn(mixed_high, values) + dot_nn(mixed_low, values)
            held_refs[part][...] = result.astype(out_ref.dtype)
            start = pl.multiple_of(start_ref[part] * 128, 128)
            copy = pltpu.make_async_copy(held_refs[part], out_ref.at[:, pl.ds(start, widths[part])], sems.at[part])
            copy.start()
            copies.append(copy)
        for copy in copies:
            copy.wait()

    operands = [starts, *sources, *factors]
    if gram is not None:
        operands.append(gram)
    operands.extend(parts)
    return pl.pallas_call(
        kernel,
        out_shape=jax.ShapeDtypeStruct((points, width), jnp.bfloat16),
        in_specs=[SMEM] + [VMEM] * (len(operands) - 1),
        out_specs=ANY,
        scratch_shapes=[pltpu.VMEM((points, columns), jnp.bfloat16) for columns in widths]
        + [pltpu.SemaphoreType.DMA((num_parts,))],
        compiler_params=PARAMS,
        name="exchange",
    )(*operands)


def gram_of(values, carried=None):
    rows = values.shape[0]

    def kernel(*refs):
        block = refs[0][...]
        total = dot_nt(block, block)
        refs[-1][...] = total if carried is None else total + refs[1][...]

    operands = [values] if carried is None else [values, carried]
    return pl.pallas_call(
        kernel,
        out_shape=jax.ShapeDtypeStruct((rows, rows), jnp.float32),
        in_specs=[VMEM] * len(operands),
        out_specs=VMEM,
        compiler_params=PARAMS,
        name="gram_of",
    )(*operands)


def outgoing(coeff, intersection, my_cluster, capacity, split):
    num_clusters, list_len = intersection.shape
    atom_count, num_funcs, columns = coeff.shape
    slots = num_clusters * capacity
    held = atom_count * num_funcs
    lanes = 128

    def kernel(me_ref, list_ref, coeff_ref, early_ref, *rest):
        late_refs = rest[: num_clusters // 2]
        list_held, coeff_held, late_held, sems = rest[num_clusters // 2 :]
        coeff_copy = pltpu.make_async_copy(coeff_ref, coeff_held, sems.at[0])
        list_copy = pltpu.make_async_copy(list_ref, list_held, sems.at[1])
        list_copy.start()
        coeff_copy.start()
        me = me_ref[0]
        list_copy.wait()
        local = list_held[...] - me * atom_count
        mine = jnp.logical_and(local >= 0, local < atom_count)
        ks = lax.broadcasted_iota(jnp.int32, (list_len, list_len), 0)
        ls = lax.broadcasted_iota(jnp.int32, (list_len, list_len), 1)
        earlier = jnp.where(ks < ls, 1.0, 0.0).astype(jnp.bfloat16)
        mine_f = jnp.where(mine, 1.0, 0.0)
        rank = dot_nn(mine_f.astype(jnp.bfloat16), earlier)
        local_f = local.astype(jnp.float32)
        lane = lax.broadcasted_iota(jnp.int32, (num_clusters, lanes), 1)
        source = jnp.zeros((num_clusters, lanes), jnp.float32)
        for slot in range(capacity):
            chosen = jnp.where(jnp.logical_and(mine, rank == slot), local_f, 0.0)
            source = jnp.where(lane == slot, jnp.sum(chosen, axis=1, keepdims=True), source)
        rows = slots * num_funcs
        row = lax.broadcasted_iota(jnp.int32, (rows, num_clusters), 0)
        cluster = lax.broadcasted_iota(jnp.int32, (rows, num_clusters), 1)
        pick = jnp.where(cluster == row // (capacity * num_funcs), 1.0, 0.0)
        spread = dot_nn(pick.astype(jnp.bfloat16), source.astype(jnp.bfloat16))
        row = lax.broadcasted_iota(jnp.int32, (rows, lanes), 0)
        lane = lax.broadcasted_iota(jnp.int32, (rows, lanes), 1)
        spread = jnp.where(lane == (row // num_funcs) % capacity, spread, 0.0)
        atom = dot_nn(spread.astype(jnp.bfloat16), jnp.ones((lanes, held), jnp.bfloat16))
        row = lax.broadcasted_iota(jnp.int32, (rows, held), 0)
        column = lax.broadcasted_iota(jnp.int32, (rows, held), 1)
        hit = atom.astype(jnp.int32) * num_funcs + row % num_funcs == column
        select = jnp.where(hit, 1.0, 0.0).astype(jnp.bfloat16)
        coeff_copy.wait()
        values = coeff_held[...].reshape(held, columns)
        result = dot_nn(select, values[:, :split]).astype(jnp.bfloat16)
        early_ref[...] = result.reshape(slots, num_funcs, split)
        result = dot_nn(select, values[:, split:]).astype(jnp.bfloat16)
        late_held[...] = result.reshape(slots, num_funcs, columns - split)
        for turn in range(num_clusters):
            target = jnp.bitwise_xor(me, turn) * capacity
            side = turn % 2 * capacity
            late_refs[turn // 2][side : side + capacity] = late_held[pl.ds(target, capacity)]

    count = num_clusters // 2
    late = jax.ShapeDtypeStruct((2 * capacity, num_funcs, columns - split), coeff.dtype)
    return pl.pallas_call(
        kernel,
        out_shape=[jax.ShapeDtypeStruct((slots, num_funcs, split), coeff.dtype)] + [late] * count,
        in_specs=[SMEM, ANY, ANY],
        out_specs=[VMEM] * (count + 1),
        scratch_shapes=[
            pltpu.VMEM((num_clusters, list_len), jnp.int32),
            pltpu.VMEM(coeff.shape, coeff.dtype),
            pltpu.VMEM((slots, num_funcs, columns - split), coeff.dtype),
            pltpu.SemaphoreType.DMA((2,)),
        ],
        compiler_params=PARAMS,
        name="outgoing",
    )(my_cluster.reshape(1), intersection, coeff)


def packed(positions, blocks):
    list_len = positions.shape[0]
    num_funcs, columns = blocks[0].shape[1:]
    slots = sum(block.shape[0] for block in blocks)

    def kernel(position_ref, *rest):
        block_refs = rest[: len(blocks)]
        out_ref = rest[len(blocks)]
        if len(blocks) > 1:
            held_ref = rest[-1]
            begin = 0
            for ref in block_refs:
                held_ref[begin : begin + ref.shape[0]] = ref[...]
                begin += ref.shape[0]
        else:
            held_ref = block_refs[0]
        for k in range(list_len):
            out_ref[k] = held_ref[position_ref[k]]

    return pl.pallas_call(
        kernel,
        out_shape=jax.ShapeDtypeStruct((list_len, num_funcs, columns), blocks[0].dtype),
        in_specs=[SMEM] + [VMEM] * len(blocks),
        out_specs=VMEM,
        scratch_shapes=[pltpu.VMEM((slots, num_funcs, columns), blocks[0].dtype)] if len(blocks) > 1 else [],
        compiler_params=PARAMS,
        name="packed",
    )(positions, *blocks).reshape(list_len * num_funcs, columns)


def screened_factors(coulomb, reach, by_step, norm_factor):
    half_stops = (coulomb.shape[1] - 1) // 2
    points = coulomb.shape[0]
    my_reach = reach[0]
    factors = []
    for step in sorted(by_step):
        total = jnp.zeros((points, coulomb.shape[2]), jnp.float32)
        for offset in by_step[step]:
            tile = coulomb[:, offset + half_stops, :].astype(jnp.float32)
            total = total + jnp.where(abs(offset) <= my_reach, tile, jnp.float32(0.0))
        factors.append(total * norm_factor)
    return factors


def two_blocks(coeff, intersection, basis_vals, factors, capacity):
    num_clusters, list_len = intersection.shape
    atom_count, num_funcs, columns = coeff.shape
    my_cluster = lax.axis_index("cluster")
    my_block = lax.axis_index("blk")
    split = max(columns * EARLY_PARTS // 8 // 128, 1) * 128
    early, *pieces = outgoing(coeff, intersection, my_cluster, capacity, split)
    early = early.reshape(num_clusters, capacity, num_funcs, split)
    early = lax.all_to_all(early, "cluster", split_axis=0, concat_axis=0, tiled=True)
    early = early.reshape(num_clusters * capacity, num_funcs, split)
    arrived = [pieces[0]]
    for m in range(1, len(pieces)):
        arrived.append(swapped(pieces[m], "cluster", 2 * m))
    relayed = []
    for m in range(len(pieces)):
        relayed.append(swapped(arrived[m][capacity:], "cluster", 1))
    sources = [basis_vals, swapped(basis_vals, "blk", 1)]

    later, _ = lax.optimization_barrier((intersection, pieces[0]))
    my_row = lax.dynamic_index_in_dim(later, my_cluster, 0, keepdims=False)
    owner = my_row // atom_count
    same = jnp.logical_and(owner[:, None] == owner[None, :], jnp.arange(list_len)[:, None] > jnp.arange(list_len)[None, :])
    rank = jnp.sum(same.astype(jnp.int32), axis=1)
    turn = jnp.bitwise_xor(owner, my_cluster)
    early_at = owner * capacity + rank
    late_at = turn // 2 * capacity + rank + jnp.where(turn % 2 == 1, num_clusters // 2 * capacity, 0)

    early = packed(early_at, [early])
    early_other = swapped(early, "blk", 1)
    gram = gram_of(early)
    late = packed(late_at, [piece[:capacity] for piece in arrived] + relayed)
    late_other = swapped(late, "blk", 1)
    gram = gram_of(late, gram)
    gram = gram_of(early_other, gram)
    lanes = columns // 128
    begin = jnp.stack([my_block * lanes, (1 - my_block) * lanes])
    starts = (begin[None, :] + jnp.array([0, split // 128])[:, None]).reshape(-1)
    return exchange(starts, sources, factors, gram, 3, [early, early_other, late, late_other], 2 * columns)


def many_blocks(coeff, intersection, basis_vals, factors, capacity, steps):
    num_clusters, list_len = intersection.shape
    atom_count, num_funcs, columns = coeff.shape
    my_cluster = lax.axis_index("cluster")
    num_blocks = lax.axis_size("blk")
    local_atom = intersection - my_cluster * atom_count
    mine = jnp.logical_and(local_atom >= 0, local_atom < atom_count)
    earlier = jnp.arange(list_len)[:, None] < jnp.arange(list_len)[None, :]
    rank = dot_nn(mine.astype(jnp.bfloat16), earlier.astype(jnp.bfloat16)).astype(jnp.int32)
    matches = jnp.logical_and(mine[:, None, :], rank[:, None, :] == jnp.arange(capacity)[None, :, None])
    source_rows = jnp.sum(jnp.where(matches, local_atom[:, None, :], 0), axis=2)
    outgoing = coeff.at[source_rows.reshape(-1)].get(mode="promise_in_bounds")
    outgoing = outgoing.reshape(num_clusters, capacity, num_funcs, columns)
    incoming = lax.all_to_all(outgoing, "cluster", split_axis=0, concat_axis=0, tiled=True)
    my_row = lax.dynamic_index_in_dim(intersection, my_cluster, 0, keepdims=False)
    my_owners = my_row // atom_count
    same = jnp.logical_and(my_owners[:, None] == my_owners[None, :], earlier.T)
    positions = my_owners * capacity + jnp.sum(same.astype(jnp.int32), axis=1)
    needed = incoming.reshape(num_clusters * capacity, num_funcs, columns)
    needed = needed.at[positions].get(mode="promise_in_bounds")
    needed = needed.reshape(list_len * num_funcs, columns)
    all_columns = lax.all_gather(needed, "blk", axis=1, tiled=True)
    sources = [basis_vals if step == 0 else passed_along(basis_vals, "blk", -step) for step in steps]
    starts = jnp.zeros((1,), jnp.int32)
    return exchange(starts, sources, factors, None, 0, [all_columns], num_blocks * columns)


def on_device(coeff, intersection, basis_vals, coulomb, reach):
    num_clusters = lax.axis_size("cluster")
    num_blocks = lax.axis_size("blk")
    list_len = intersection.shape[1]
    capacity = 2 * list_len // num_clusters
    half_stops = (coulomb.shape[1] - 1) // 2
    by_step = {}
    for offset in range(-half_stops, half_stops + 1):
        by_step.setdefault(offset % num_blocks, []).append(offset)
    factors = screened_factors(coulomb, reach, by_step, (coeff.shape[2] * num_blocks) ** (-0.5))
    if takes_two_blocks(num_clusters, num_blocks):
        return two_blocks(coeff, intersection, basis_vals, factors, capacity)
    return many_blocks(coeff, intersection, basis_vals, factors, capacity, sorted(by_step))


def takes_two_blocks(num_clusters, num_blocks):
    return num_blocks == 2 and num_clusters >= 16 and num_clusters & (num_clusters - 1) == 0


def solution(mesh):
    return jax.shard_map(
        on_device,
        mesh=mesh,
        in_specs=(
            P("cluster", None, "blk"),
            P(),
            P(("cluster", "blk"), None),
            P(("cluster", "blk"), None, None),
            P(("cluster", "blk")),
        ),
        out_specs=P(("cluster", "blk"), None),
        check_vma=False,
    )
```

time: 55 us -> 59.4 us (1.080)
  the two profiles are of different devices: /device:TPU:16 before, /device:TPU:0 now
where the time goes in v1:
time: 59.4 us; the launch traced here: 59.1 us
  starting transfers between devices  26.4 us (44%)
  waiting for transfers between devices  22.5 us (38%)
  Pallas kernels  6.98 us (12%)
  local copies, waits for them, and re-layouts  1.88 us (3%)
  between operations  0.82 us (1%)
    ppermute x18, waiting for transfers between devices, swapped(): lax.ppermute(value, axis, [(source, source ^ bits) for source in range(co...  22.5 us
    ppermute x18, starting transfers between devices, swapped(): lax.ppermute(value, axis, [(source, source ^ bits) for source in range(co...  19 us
    all_to_all x1, starting transfers between devices, two_blocks(): lax.all_to_all(early, 'cluster', split_axis=0, concat_axis=0, tiled=True)  7.4 us
    pallas_call x1, Pallas kernels, exchange(): pl.pallas_call(kernel, out_shape=jax.ShapeDtypeStruct((points, width), jn...  3.03 us
    pallas_call x1, Pallas kernels, outgoing(): pl.pallas_call(kernel, out_shape=[jax.ShapeDtypeStruct((slots, num_funcs,...  1.91 us
    unnamed x8, local copies, waits for them, and re-layouts  1.75 us
    pallas_call x2, Pallas kernels, packed(): pl.pallas_call(kernel, out_shape=jax.ShapeDtypeStruct((list_len, num_func...  1.19 us
  transfers between devices with their start and end apart: 19, of which 7 were waited for; matrix products, arithmetic and copies ran while one was open for 1% of the time, Pallas kernels for 3%

profile of v1, /device:TPU:0, one launch (start us, length us, event | category | flops | bytes accessed | tf_op | source)
XLA Modules:
  0.0 59.1 jit_solution(9558445762022372879)
XLA Ops:
  0.0 0.0 copy-start.2
  0.0 0.7 %copy-done.2 = s32[16,32]{1,0:T(8,128)S(1)} copy-done((s32[16,32]{1,0:T(8,128)S(1)}, s32[16,32]{1,0:T(8,128)}, u32[]{:S(2)}) %copy-start.2) | copy-done | bytes 2072
  0.7 0.0 copy-start
  0.7 1.0 %copy-done = bf16[32,8,1024]{2,1,0:T(8,128)(2,1)S(1)} copy-done((bf16[32,8,1024]{2,1,0:T(8,128)(2,1)S(1)}, bf16[32,8,1024]{2,1,0:T(8,128)(2,1)}, u32[]{:S(2)}) %copy-start) | copy-done | bytes 524312
  1.7 1.9 %outgoing.1 = (bf16[64,8,640]{2,1,0:T(8,128)(2,1)}, bf16[8,8,384]{2,1,0:T(8,128)(2,1)S(1)}, bf16[8,8,384]{2,1,0:T(8,128)(2,1)S(1)}, bf16[8,8,384]{2,1,0:T(8,128)...) custom-call(s32[1]{0:T(128)} %bitcast.8.me_ref, ...), custom_call_target="tpu_custom_call" | custom-call | tf_op jit(solution)/shard_map/outgoing/pallas_call | solution.py:176
  3.7 7.4 %all-to-all-start = ((bf16[16,4,8,640]{3,2,1,0:T(8,128)(2,1)}), bf16[16,4,8,640]{3,2,1,0:T(8,128)(2,1)S(1)}, u32[]{:S(2)}, u32[]{:S(2)}) async-start(bf16[16,4,8,640]{3,2,1,0:T(8,128)(2,1)} %bitcast.11), calls=%async_computation | async-start | bytes 1310720 | tf_op jit(solution)/shard_map/all_to_all | solution.py:244
  11.1 0.5 collective-permute-start.9
  11.5 1.6 %collective-permute-start.2 = (bf16[8,8,384]{2,1,0:T(8,128)(2,1)S(1)}, bf16[8,8,384]{2,1,0:T(8,128)(2,1)S(1)}, u32[]{:S(2)}, u32[]{:S(2)}) collective-permute-start(bf16[8,8,384]{2,1,0:T(8,128)(2,1)S(1)} %get-tuple-element.18), channel_id=1, source_target_pairs={{0,4},{2,6},{4,0},{6,2},{8,12},{10,14},{12,8},{14,10},{16,20},{18,... | collective-permute-start | bytes 147464 | tf_op jit(solution)/shard_map/ppermute | solution.py:25
  13.2 1.5 %collective-permute-start.3 = (bf16[8,8,384]{2,1,0:T(8,128)(2,1)S(1)}, bf16[8,8,384]{2,1,0:T(8,128)(2,1)S(1)}, u32[]{:S(2)}, u32[]{:S(2)}) collective-permute-start(bf16[8,8,384]{2,1,0:T(8,128)(2,1)S(1)} %get-tuple-element.19), channel_id=1, source_target_pairs={{0,8},{2,10},{4,12},{6,14},{8,0},{10,2},{12,4},{14,6},{16,24},{18,... | collective-permute-start | bytes 147464 | tf_op jit(solution)/shard_map/ppermute | solution.py:25
  14.6 0.4 collective-permute-start.4
  15.0 2.5 %collective-permute-start.5 = (bf16[8,8,384]{2,1,0:T(8,128)(2,1)S(1)}, bf16[8,8,384]{2,1,0:T(8,128)(2,1)S(1)}, u32[]{:S(2)}, u32[]{:S(2)}) collective-permute-start(bf16[8,8,384]{2,1,0:T(8,128)(2,1)S(1)} %get-tuple-element.21), channel_id=1, source_target_pairs={{0,16},{2,18},{4,20},{6,22},{8,24},{10,26},{12,28},{14,30},{16,0},... | collective-permute-start | bytes 147464 | tf_op jit(solution)/shard_map/ppermute | solution.py:25
  17.6 0.2 convert_reduce_fusion
  17.8 0.1 pad_add_fusion
  17.9 1.0 %collective-permute-done.2 = bf16[8,8,384]{2,1,0:T(8,128)(2,1)S(1)} collective-permute-done((bf16[8,8,384]{2,1,0:T(8,128)(2,1)S(1)}, bf16[8,8,384]{2,1,0:T(8,128)(2,1)S(1)}, u32[]{:S(2)}, u32[]{:S(2)}) %collective-permute-start.2) | collective-permute-done | bytes 49184 | tf_op jit(solution)/shard_map/ppermute | solution.py:25
  18.9 1.9 %collective-permute-start.6 = (bf16[8,8,384]{2,1,0:T(8,128)(2,1)S(1)}, bf16[8,8,384]{2,1,0:T(8,128)(2,1)S(1)}, u32[]{:S(2)}, u32[]{:S(2)}) collective-permute-start(bf16[8,8,384]{2,1,0:T(8,128)(2,1)S(1)} %get-tuple-element.22), channel_id=1, source_target_pairs={{0,20},{2,22},{4,16},{6,18},{8,28},{10,30},{12,24},{14,26},{16,4},... | collective-permute-start | bytes 147464 | tf_op jit(solution)/shard_map/ppermute | solution.py:25
  20.8 3.7 %collective-permute-done.3 = bf16[8,8,384]{2,1,0:T(8,128)(2,1)S(1)} collective-permute-done((bf16[8,8,384]{2,1,0:T(8,128)(2,1)S(1)}, bf16[8,8,384]{2,1,0:T(8,128)(2,1)S(1)}, u32[]{:S(2)}, u32[]{:S(2)}) %collective-permute-start.3) | collective-permute-done | bytes 49184 | tf_op jit(solution)/shard_map/ppermute | solution.py:25
  24.5 3.3 %collective-permute-start.7 = (bf16[8,8,384]{2,1,0:T(8,128)(2,1)S(1)}, bf16[8,8,384]{2,1,0:T(8,128)(2,1)S(1)}, u32[]{:S(2)}, u32[]{:S(2)}) collective-permute-start(bf16[8,8,384]{2,1,0:T(8,128)(2,1)S(1)} %get-tuple-element.23), channel_id=1, source_target_pairs={{0,24},{2,26},{4,28},{6,30},{8,16},{10,18},{12,20},{14,22},{16,8},... | collective-permute-start | bytes 147464 | tf_op jit(solution)/shard_map/ppermute | solution.py:25
  27.8 0.0 collective-permute-done.4
  27.8 1.9 %collective-permute-start.8 = (bf16[8,8,384]{2,1,0:T(8,128)(2,1)S(1)}, bf16[8,8,384]{2,1,0:T(8,128)(2,1)S(1)}, u32[]{:S(2)}, u32[]{:S(2)}) collective-permute-start(bf16[8,8,384]{2,1,0:T(8,128)(2,1)S(1)} %get-tuple-element.24), channel_id=1, source_target_pairs={{0,28},{2,30},{4,24},{6,26},{8,20},{10,22},{12,16},{14,18},{16,12}... | collective-permute-start | bytes 147464 | tf_op jit(solution)/shard_map/ppermute | solution.py:25
  29.8 5.2 %collective-permute-done.5 = bf16[8,8,384]{2,1,0:T(8,128)(2,1)S(1)} collective-permute-done((bf16[8,8,384]{2,1,0:T(8,128)(2,1)S(1)}, bf16[8,8,384]{2,1,0:T(8,128)(2,1)S(1)}, u32[]{:S(2)}, u32[]{:S(2)}) %collective-permute-start.5) | collective-permute-done | bytes 49184 | tf_op jit(solution)/shard_map/ppermute | solution.py:25
  35.0 0.0 collective-permute-start.10
  35.0 1.9 %collective-permute-done.6 = bf16[8,8,384]{2,1,0:T(8,128)(2,1)S(1)} collective-permute-done((bf16[8,8,384]{2,1,0:T(8,128)(2,1)S(1)}, bf16[8,8,384]{2,1,0:T(8,128)(2,1)S(1)}, u32[]{:S(2)}, u32[]{:S(2)}) %collective-permute-start.6) | collective-permute-done | bytes 49184 | tf_op jit(solution)/shard_map/ppermute | solution.py:25
  36.9 0.0 collective-permute-start.11
  37.0 0.0 copy-start.3
  37.0 0.0 collective-permute-done.7
  37.0 0.6 collective-permute-start.12
  37.5 0.0 collective-permute-done.8
  37.5 0.1 collective-permute-start.13
  37.6 0.0 all-to-all-done
  37.7 0.0 copy-start.1
  37.7 0.6 packed.2
  38.2 0.0 collective-permute-done.9.rest_8_
  38.3 0.5 collective-permute-start.14
  38.8 0.0 collective-permute-done.10.rest_9_
  38.8 0.1 collective-permute-start.15
  38.9 0.0 collective-permute-done.11.rest_10_
  38.9 0.4 collective-permute-start.16
  39.3 0.0 collective-permute-done.12.rest_11_
  39.3 1.5 %collective-permute-start.1 = (bf16[256,640]{1,0:T(8,128)(2,1)S(1)}, bf16[256,640]{1,0:T(8,128)(2,1)S(1)}, u32[]{:S(2)}, u32[]{:S(2)}) collective-permute-start(bf16[256,640]{1,0:T(8,128)(2,1)S(1)} %bitcast.27), channel_id=1, source_target_pairs={{0,1},{1,0},{2,3},{3,2},{4,5},{5,4},{6,7},{7,6},{8,9},{9,8},{10,11... | collective-permute-start | bytes 983048 | tf_op jit(solution)/shard_map/ppermute | solution.py:25
  40.9 0.1 broadcast_add_fusion
  41.6 0.1 add.69.refs_0_
  41.7 0.0 collective-permute-done.13.rest_12_
  41.7 0.0 copy-done.1
  41.7 0.5 collective-permute-start
  42.2 0.0 collective-permute-done.14.rest_13_
  42.2 0.0 collective-permute-done.15.rest_14_
  42.2 0.0 collective-permute-done.16.rest_15_
  42.2 0.6 %packed.3 = bf16[32,8,384]{2,1,0:T(8,128)(2,1)S(1)} custom-call(s32[32]{0:T(128)S(1)} %get-tuple-element.43.position_ref, bf16[4,8,384]{2,1,0:T(8,128)(2,1)S(1)} %get-tuple-element.42.rest_0_, bf16[4,8,384]{2,1,0:T(8,128)(2,1)S(1)} %get-tuple-element.40.rest_1_, bf16[4,8,384]{2,1,0:T(8,128)(2,1)S(1)} %get-tuple-element.38.rest_2_, ...), custom_call_target="tpu_custom_call" | custom-call | tf_op jit(solution)/shard_map/packed/pallas_call | solution.py:211
  42.8 1.6 %collective-permute-start.17 = (bf16[256,384]{1,0:T(8,128)(2,1)S(1)}, bf16[256,384]{1,0:T(8,128)(2,1)S(1)}, u32[]{:S(2)}, u32[]{:S(2)}) collective-permute-start(bf16[256,384]{1,0:T(8,128)(2,1)S(1)} %bitcast.31), channel_id=1, source_target_pairs={{0,1},{1,0},{2,3},{3,2},{4,5},{5,4},{6,7},{7,6},{8,9},{9,8},{10,11... | collective-permute-start | bytes 589832 | tf_op jit(solution)/shard_map/ppermute | solution.py:25
  44.4 0.0 copy-done.3
  44.4 0.2 multiply_bitcast_fusion
  44.6 0.3 gram_of.3.refs_1_
  44.9 0.3 gram_of.4.refs_1_
  45.2 4.7 %collective-permute-done.1.refs_0_.refs_7_ = bf16[256,640]{1,0:T(8,128)(2,1)S(1)} collective-permute-done((bf16[256,640]{1,0:T(8,128)(2,1)S(1)}, bf16[256,640]{1,0:T(8,128)(2,1)S(1)}, u32[]{:S(2)}, u32[]{:S(2)}) %collective-permute-start.1) | collective-permute-done | bytes 327712 | tf_op jit(solution)/shard_map/ppermute | solution.py:25
  49.9 0.3 gram_of.5.refs_5_
  50.2 2.5 %collective-permute-done.refs_2_ = bf16[256,256]{1,0:T(8,128)(2,1)S(1)} collective-permute-done((bf16[256,256]{1,0:T(8,128)(2,1)S(1)}, bf16[256,256]{1,0:T(8,128)(2,1)S(1)}, u32[]{:S(2)}, u32[]{:S(2)}) %collective-permute-start) | collective-permute-done | bytes 131104 | tf_op jit(solution)/shard_map/ppermute | solution.py:25
  52.7 3.3 %collective-permute-done.17.refs_9_ = bf16[256,384]{1,0:T(8,128)(2,1)S(1)} collective-permute-done((bf16[256,384]{1,0:T(8,128)(2,1)S(1)}, bf16[256,384]{1,0:T(8,128)(2,1)S(1)}, u32[]{:S(2)}, u32[]{:S(2)}) %collective-permute-start.17) | collective-permute-done | bytes 196640 | tf_op jit(solution)/shard_map/ppermute | solution.py:25
  56.1 3.0 %exchange.1 = bf16[256,2048]{1,0:T(8,128)(2,1)} custom-call(s32[4]{0:T(128)S(1)} %add.69.refs_0_, bf16[256,256]{1,0:T(8,128)(2,1)S(1)} %copy-done.1, bf16[256,256]{1,0:T(8,128)(2,1)S(1)} %collective-permute-done.refs_2_, f32[256,256]{1,0:T(8,128)S(1)} %get-tuple-element.26.refs_3_, f32[256,256]{1,0:T(8,128)S(1)} %get-tuple-element.25.refs_4_, ...), custom_call_target="tpu_custom_call" | custom-call | tf_op jit(solution)/shard_map/exchange/pallas_call | solution.py:90
  (11 shorter events, 0.1 us)
Async XLA Ops:
  0.0 0.7 %copy-start.2 = (s32[16,32]{1,0:T(8,128)S(1)}, s32[16,32]{1,0:T(8,128)}, u32[]{:S(2)}) copy-start(s32[16,32]{1,0:T(8,128)} %list_ref.1) | copy-start | bytes 6148
  0.7 1.0 %copy-start = (bf16[32,8,1024]{2,1,0:T(8,128)(2,1)S(1)}, bf16[32,8,1024]{2,1,0:T(8,128)(2,1)}, u32[]{:S(2)}) copy-start(bf16[32,8,1024]{2,1,0:T(8,128)(2,1)} %coeff_ref.1) | copy-start | bytes 1572868
  3.7 34.0 %all-to-all-start = ((bf16[16,4,8,640]{3,2,1,0:T(8,128)(2,1)}), bf16[16,4,8,640]{3,2,1,0:T(8,128)(2,1)S(1)}, u32[]{:S(2)}, u32[]{:S(2)}) async-start(bf16[16,4,8,640]{3,2,1,0:T(8,128)(2,1)} %bitcast.11), calls=%async_computation | async-start | bytes 1310720 | tf_op jit(solution)/shard_map/all_to_all | solution.py:244
  11.1 27.2 %collective-permute-start.9 = (bf16[4,8,384]{2,1,0:T(8,128)(2,1)S(1)}, bf16[4,8,384]{2,1,0:T(8,128)(2,1)S(1)}, u32[]{:S(2)}, u32[]{:S(2)}) collective-permute-start(bf16[4,8,384]{2,1,0:T(8,128)(2,1)S(1)} %get-tuple-element.41), channel_id=1, source_target_pairs={{0,2},{2,0},{4,6},{6,4},{8,10},{10,8},{12,14},{14,12},{16,18},{18,... | collective-permute-start | bytes 73736 | tf_op jit(solution)/shard_map/ppermute | solution.py:25
  11.5 7.3 %collective-permute-start.2 = (bf16[8,8,384]{2,1,0:T(8,128)(2,1)S(1)}, bf16[8,8,384]{2,1,0:T(8,128)(2,1)S(1)}, u32[]{:S(2)}, u32[]{:S(2)}) collective-permute-start(bf16[8,8,384]{2,1,0:T(8,128)(2,1)S(1)} %get-tuple-element.18), channel_id=1, source_target_pairs={{0,4},{2,6},{4,0},{6,2},{8,12},{10,14},{12,8},{14,10},{16,20},{18,... | collective-permute-start | bytes 147464 | tf_op jit(solution)/shard_map/ppermute | solution.py:25
  13.2 11.3 %collective-permute-start.3 = (bf16[8,8,384]{2,1,0:T(8,128)(2,1)S(1)}, bf16[8,8,384]{2,1,0:T(8,128)(2,1)S(1)}, u32[]{:S(2)}, u32[]{:S(2)}) collective-permute-start(bf16[8,8,384]{2,1,0:T(8,128)(2,1)S(1)} %get-tuple-element.19), channel_id=1, source_target_pairs={{0,8},{2,10},{4,12},{6,14},{8,0},{10,2},{12,4},{14,6},{16,24},{18,... | collective-permute-start | bytes 147464 | tf_op jit(solution)/shard_map/ppermute | solution.py:25
  14.6 13.2 %collective-permute-start.4 = (bf16[8,8,384]{2,1,0:T(8,128)(2,1)S(1)}, bf16[8,8,384]{2,1,0:T(8,128)(2,1)S(1)}, u32[]{:S(2)}, u32[]{:S(2)}) collective-permute-start(bf16[8,8,384]{2,1,0:T(8,128)(2,1)S(1)} %get-tuple-element.20), channel_id=1, source_target_pairs={{0,12},{2,14},{4,8},{6,10},{8,4},{10,6},{12,0},{14,2},{16,28},{18,... | collective-permute-start | bytes 147464 | tf_op jit(solution)/shard_map/ppermute | solution.py:25
  15.0 20.0 %collective-permute-start.5 = (bf16[8,8,384]{2,1,0:T(8,128)(2,1)S(1)}, bf16[8,8,384]{2,1,0:T(8,128)(2,1)S(1)}, u32[]{:S(2)}, u32[]{:S(2)}) collective-permute-start(bf16[8,8,384]{2,1,0:T(8,128)(2,1)S(1)} %get-tuple-element.21), channel_id=1, source_target_pairs={{0,16},{2,18},{4,20},{6,22},{8,24},{10,26},{12,28},{14,30},{16,0},... | collective-permute-start | bytes 147464 | tf_op jit(solution)/shard_map/ppermute | solution.py:25
  18.9 18.1 %collective-permute-start.6 = (bf16[8,8,384]{2,1,0:T(8,128)(2,1)S(1)}, bf16[8,8,384]{2,1,0:T(8,128)(2,1)S(1)}, u32[]{:S(2)}, u32[]{:S(2)}) collective-permute-start(bf16[8,8,384]{2,1,0:T(8,128)(2,1)S(1)} %get-tuple-element.22), channel_id=1, source_target_pairs={{0,20},{2,22},{4,16},{6,18},{8,28},{10,30},{12,24},{14,26},{16,4},... | collective-permute-start | bytes 147464 | tf_op jit(solution)/shard_map/ppermute | solution.py:25
  24.5 12.5 %collective-permute-start.7 = (bf16[8,8,384]{2,1,0:T(8,128)(2,1)S(1)}, bf16[8,8,384]{2,1,0:T(8,128)(2,1)S(1)}, u32[]{:S(2)}, u32[]{:S(2)}) collective-permute-start(bf16[8,8,384]{2,1,0:T(8,128)(2,1)S(1)} %get-tuple-element.23), channel_id=1, source_target_pairs={{0,24},{2,26},{4,28},{6,30},{8,16},{10,18},{12,20},{14,22},{16,8},... | collective-permute-start | bytes 147464 | tf_op jit(solution)/shard_map/ppermute | solution.py:25
  27.8 9.7 %collective-permute-start.8 = (bf16[8,8,384]{2,1,0:T(8,128)(2,1)S(1)}, bf16[8,8,384]{2,1,0:T(8,128)(2,1)S(1)}, u32[]{:S(2)}, u32[]{:S(2)}) collective-permute-start(bf16[8,8,384]{2,1,0:T(8,128)(2,1)S(1)} %get-tuple-element.24), channel_id=1, source_target_pairs={{0,28},{2,30},{4,24},{6,26},{8,20},{10,22},{12,16},{14,18},{16,12}... | collective-permute-start | bytes 147464 | tf_op jit(solution)/shard_map/ppermute | solution.py:25
  35.0 3.8 %collective-permute-start.10 = (bf16[4,8,384]{2,1,0:T(8,128)(2,1)S(1)}, bf16[4,8,384]{2,1,0:T(8,128)(2,1)S(1)}, u32[]{:S(2)}, u32[]{:S(2)}) collective-permute-start(bf16[4,8,384]{2,1,0:T(8,128)(2,1)S(1)} %get-tuple-element.39), channel_id=1, source_target_pairs={{0,2},{2,0},{4,6},{6,4},{8,10},{10,8},{12,14},{14,12},{16,18},{18,... | collective-permute-start | bytes 73736 | tf_op jit(solution)/shard_map/ppermute | solution.py:25
  36.9 2.0 %collective-permute-start.11 = (bf16[4,8,384]{2,1,0:T(8,128)(2,1)S(1)}, bf16[4,8,384]{2,1,0:T(8,128)(2,1)S(1)}, u32[]{:S(2)}, u32[]{:S(2)}) collective-permute-start(bf16[4,8,384]{2,1,0:T(8,128)(2,1)S(1)} %get-tuple-element.37), channel_id=1, source_target_pairs={{0,2},{2,0},{4,6},{6,4},{8,10},{10,8},{12,14},{14,12},{16,18},{18,... | collective-permute-start | bytes 73736 | tf_op jit(solution)/shard_map/ppermute | solution.py:25
  37.0 7.5 %copy-start.3 = (bf16[256,7,256]{2,0,1:T(8,128)(2,1)S(1)}, bf16[256,7,256]{2,0,1:T(8,128)(2,1)}, u32[]{:S(2)}) copy-start(bf16[256,7,256]{2,0,1:T(8,128)(2,1)} %param.9) | copy-start | bytes 2752516
  37.0 2.4 %collective-permute-start.12 = (bf16[4,8,384]{2,1,0:T(8,128)(2,1)S(1)}, bf16[4,8,384]{2,1,0:T(8,128)(2,1)S(1)}, u32[]{:S(2)}, u32[]{:S(2)}) collective-permute-start(bf16[4,8,384]{2,1,0:T(8,128)(2,1)S(1)} %get-tuple-element.35), channel_id=1, source_target_pairs={{0,2},{2,0},{4,6},{6,4},{8,10},{10,8},{12,14},{14,12},{16,18},{18,... | collective-permute-start | bytes 73736 | tf_op jit(solution)/shard_map/ppermute | solution.py:25
  37.5 4.1 %collective-permute-start.13 = (bf16[4,8,384]{2,1,0:T(8,128)(2,1)S(1)}, bf16[4,8,384]{2,1,0:T(8,128)(2,1)S(1)}, u32[]{:S(2)}, u32[]{:S(2)}) collective-permute-start(bf16[4,8,384]{2,1,0:T(8,128)(2,1)S(1)} %get-tuple-element.33), channel_id=1, source_target_pairs={{0,2},{2,0},{4,6},{6,4},{8,10},{10,8},{12,14},{14,12},{16,18},{18,... | collective-permute-start | bytes 73736 | tf_op jit(solution)/shard_map/ppermute | solution.py:25
  37.7 4.0 %copy-start.1 = (bf16[256,256]{1,0:T(8,128)(2,1)S(1)}, bf16[256,256]{1,0:T(8,128)(2,1)}, u32[]{:S(2)}) copy-start(bf16[256,256]{1,0:T(8,128)(2,1)} %refs_1_.1) | copy-start | bytes 393220
  38.3 3.9 %collective-permute-start.14 = (bf16[4,8,384]{2,1,0:T(8,128)(2,1)S(1)}, bf16[4,8,384]{2,1,0:T(8,128)(2,1)S(1)}, u32[]{:S(2)}, u32[]{:S(2)}) collective-permute-start(bf16[4,8,384]{2,1,0:T(8,128)(2,1)S(1)} %get-tuple-element.31), channel_id=1, source_target_pairs={{0,2},{2,0},{4,6},{6,4},{8,10},{10,8},{12,14},{14,12},{16,18},{18,... | collective-permute-start | bytes 73736 | tf_op jit(solution)/shard_map/ppermute | solution.py:25
  38.8 3.4 %collective-permute-start.15 = (bf16[4,8,384]{2,1,0:T(8,128)(2,1)S(1)}, bf16[4,8,384]{2,1,0:T(8,128)(2,1)S(1)}, u32[]{:S(2)}, u32[]{:S(2)}) collective-permute-start(bf16[4,8,384]{2,1,0:T(8,128)(2,1)S(1)} %get-tuple-element.29), channel_id=1, source_target_pairs={{0,2},{2,0},{4,6},{6,4},{8,10},{10,8},{12,14},{14,12},{16,18},{18,... | collective-permute-start | bytes 73736 | tf_op jit(solution)/shard_map/ppermute | solution.py:25
  38.9 3.3 %collective-permute-start.16 = (bf16[4,8,384]{2,1,0:T(8,128)(2,1)S(1)}, bf16[4,8,384]{2,1,0:T(8,128)(2,1)S(1)}, u32[]{:S(2)}, u32[]{:S(2)}) collective-permute-start(bf16[4,8,384]{2,1,0:T(8,128)(2,1)S(1)} %get-tuple-element.27), channel_id=1, source_target_pairs={{0,2},{2,0},{4,6},{6,4},{8,10},{10,8},{12,14},{14,12},{16,18},{18,... | collective-permute-start | bytes 73736 | tf_op jit(solution)/shard_map/ppermute | solution.py:25
  39.3 10.6 %collective-permute-start.1 = (bf16[256,640]{1,0:T(8,128)(2,1)S(1)}, bf16[256,640]{1,0:T(8,128)(2,1)S(1)}, u32[]{:S(2)}, u32[]{:S(2)}) collective-permute-start(bf16[256,640]{1,0:T(8,128)(2,1)S(1)} %bitcast.27), channel_id=1, source_target_pairs={{0,1},{1,0},{2,3},{3,2},{4,5},{5,4},{6,7},{7,6},{8,9},{9,8},{10,11... | collective-permute-start | bytes 983048 | tf_op jit(solution)/shard_map/ppermute | solution.py:25
  41.7 11.1 %collective-permute-start = (bf16[256,256]{1,0:T(8,128)(2,1)S(1)}, bf16[256,256]{1,0:T(8,128)(2,1)S(1)}, u32[]{:S(2)}, u32[]{:S(2)}) collective-permute-start(bf16[256,256]{1,0:T(8,128)(2,1)S(1)} %copy-done.1), channel_id=1, source_target_pairs={{0,1},{1,0},{2,3},{3,2},{4,5},{5,4},{6,7},{7,6},{8,9},{9,8},{10,11... | collective-permute-start | bytes 393224 | tf_op jit(solution)/shard_map/ppermute | solution.py:25
  42.8 13.2 %collective-permute-start.17 = (bf16[256,384]{1,0:T(8,128)(2,1)S(1)}, bf16[256,384]{1,0:T(8,128)(2,1)S(1)}, u32[]{:S(2)}, u32[]{:S(2)}) collective-permute-start(bf16[256,384]{1,0:T(8,128)(2,1)S(1)} %bitcast.31), channel_id=1, source_target_pairs={{0,1},{1,0},{2,3},{3,2},{4,5},{5,4},{6,7},{7,6},{8,9},{9,8},{10,11... | collective-permute-start | bytes 589832 | tf_op jit(solution)/shard_map/ppermute | solution.py:25

commit v2 on v1

--- a/solution.py
+++ b/solution.py
@@ -10,8 +10,8 @@
 
 VMEM = pl.BlockSpec(memory_space=pltpu.VMEM)
 SMEM = pl.BlockSpec(memory_space=pltpu.SMEM)
-ANY = pl.BlockSpec(memory_space=pl.ANY)
-PARAMS = pltpu.CompilerParams(vmem_limit_bytes=16 * 2**20)
+HBM = pl.BlockSpec(memory_space=pltpu.HBM)
+PARAMS = pltpu.CompilerParams(vmem_limit_bytes=12 * 2**20)
 
 
 def passed_along(value, axis, steps):
@@ -91,7 +91,7 @@
         kernel,
         out_shape=jax.ShapeDtypeStruct((points, width), jnp.bfloat16),
         in_specs=[SMEM] + [VMEM] * (len(operands) - 1),
-        out_specs=ANY,
+        out_specs=HBM,
         scratch_shapes=[pltpu.VMEM((points, columns), jnp.bfloat16) for columns in widths]
         + [pltpu.SemaphoreType.DMA((num_parts,))],
         compiler_params=PARAMS,
@@ -125,9 +125,9 @@
     held = atom_count * num_funcs
     lanes = 128
 
-    def kernel(me_ref, list_ref, coeff_ref, early_ref, *rest):
-        late_refs = rest[: num_clusters // 2]
-        list_held, coeff_held, late_held, sems = rest[num_clusters // 2 :]
+    def kernel(me_ref, list_ref, coeff_ref, list_held, late_ref, *rest):
+        early_refs = rest[: num_clusters // 2]
+        coeff_held, early_held, sems = rest[num_clusters // 2 :]
         coeff_copy = pltpu.make_async_copy(coeff_ref, coeff_held, sems.at[0])
         list_copy = pltpu.make_async_copy(list_ref, list_held, sems.at[1])
         list_copy.start()
@@ -163,60 +163,60 @@
         coeff_copy.wait()
         values = coeff_held[...].reshape(held, columns)
         result = dot_nn(select, values[:, :split]).astype(jnp.bfloat16)
-        early_ref[...] = result.reshape(slots, num_funcs, split)
-        result = dot_nn(select, values[:, split:]).astype(jnp.bfloat16)
-        late_held[...] = result.reshape(slots, num_funcs, columns - split)
+        early_held[...] = result.reshape(slots, num_funcs, split)
         for turn in range(num_clusters):
             target = jnp.bitwise_xor(me, turn) * capacity
             side = turn % 2 * capacity
-            late_refs[turn // 2][side : side + capacity] = late_held[pl.ds(target, capacity)]
+            early_refs[turn // 2][side : side + capacity] = early_held[pl.ds(target, capacity)]
+        result = dot_nn(select, values[:, split:]).astype(jnp.bfloat16)
+        late_ref[...] = result.reshape(slots, num_funcs, columns - split)
 
     count = num_clusters // 2
-    late = jax.ShapeDtypeStruct((2 * capacity, num_funcs, columns - split), coeff.dtype)
+    late = jax.ShapeDtypeStruct((slots, num_funcs, columns - split), coeff.dtype)
+    early = jax.ShapeDtypeStruct((2 * capacity, num_funcs, split), coeff.dtype)
     return pl.pallas_call(
         kernel,
-        out_shape=[jax.ShapeDtypeStruct((slots, num_funcs, split), coeff.dtype)] + [late] * count,
-        in_specs=[SMEM, ANY, ANY],
-        out_specs=[VMEM] * (count + 1),
+        out_shape=[jax.ShapeDtypeStruct(intersection.shape, jnp.int32), late] + [early] * count,
+        in_specs=[SMEM, HBM, HBM],
+        out_specs=[VMEM] * (count + 2),
         scratch_shapes=[
-            pltpu.VMEM((num_clusters, list_len), jnp.int32),
             pltpu.VMEM(coeff.shape, coeff.dtype),
-            pltpu.VMEM((slots, num_funcs, columns - split), coeff.dtype),
+            pltpu.VMEM((slots, num_funcs, split), coeff.dtype),
             pltpu.SemaphoreType.DMA((2,)),
         ],
         compiler_params=PARAMS,
         name="outgoing",
-    )(my_cluster.reshape(1), intersection, coeff)
-
-
-def packed(positions, blocks):
+    )(
+        my_cluster.reshape(1),
+        pltpu.with_memory_space_constraint(intersection, pltpu.HBM),
+        pltpu.with_memory_space_constraint(coeff, pltpu.HBM),
+    )
+
+
+def packed(positions, blocks, taken, last):
     list_len = positions.shape[0]
-    num_funcs, columns = blocks[0].shape[1:]
-    slots = sum(block.shape[0] for block in blocks)
+    num_funcs, columns = last.shape[1:]
+    slots = len(blocks) * taken + last.shape[0]
 
     def kernel(position_ref, *rest):
-        block_refs = rest[: len(blocks)]
-        out_ref = rest[len(blocks)]
-        if len(blocks) > 1:
-            held_ref = rest[-1]
-            begin = 0
-            for ref in block_refs:
-                held_ref[begin : begin + ref.shape[0]] = ref[...]
-                begin += ref.shape[0]
-        else:
-            held_ref = block_refs[0]
+        last_ref, out_ref = rest[len(blocks) : len(blocks) + 2]
+        held_ref = rest[-1] if blocks else last_ref
+        if blocks:
+            for at, ref in enumerate(rest[: len(blocks)]):
+                held_ref[at * taken : (at + 1) * taken] = ref[:taken]
+            held_ref[len(blocks) * taken :] = last_ref[...]
         for k in range(list_len):
             out_ref[k] = held_ref[position_ref[k]]
 
     return pl.pallas_call(
         kernel,
-        out_shape=jax.ShapeDtypeStruct((list_len, num_funcs, columns), blocks[0].dtype),
-        in_specs=[SMEM] + [VMEM] * len(blocks),
+        out_shape=jax.ShapeDtypeStruct((list_len, num_funcs, columns), last.dtype),
+        in_specs=[SMEM] + [VMEM] * (len(blocks) + 1),
         out_specs=VMEM,
-        scratch_shapes=[pltpu.VMEM((slots, num_funcs, columns), blocks[0].dtype)] if len(blocks) > 1 else [],
+        scratch_shapes=[pltpu.VMEM((slots, num_funcs, columns), last.dtype)] if blocks else [],
         compiler_params=PARAMS,
         name="packed",
-    )(positions, *blocks).reshape(list_len * num_funcs, columns)
+    )(positions, *blocks, last).reshape(list_len * num_funcs, columns)
 
 
 def screened_factors(coulomb, reach, by_step, norm_factor):
@@ -239,31 +239,28 @@
     my_cluster = lax.axis_index("cluster")
     my_block = lax.axis_index("blk")
     split = max(columns * EARLY_PARTS // 8 // 128, 1) * 128
-    early, *pieces = outgoing(coeff, intersection, my_cluster, capacity, split)
-    early = early.reshape(num_clusters, capacity, num_funcs, split)
-    early = lax.all_to_all(early, "cluster", split_axis=0, concat_axis=0, tiled=True)
-    early = early.reshape(num_clusters * capacity, num_funcs, split)
+    listed, late, *pieces = outgoing(coeff, intersection, my_cluster, capacity, split)
     arrived = [pieces[0]]
     for m in range(1, len(pieces)):
         arrived.append(swapped(pieces[m], "cluster", 2 * m))
-    relayed = []
-    for m in range(len(pieces)):
-        relayed.append(swapped(arrived[m][capacity:], "cluster", 1))
+    late = late.reshape(num_clusters, capacity, num_funcs, columns - split)
+    late = lax.all_to_all(late, "cluster", split_axis=0, concat_axis=0, tiled=True)
+    late = late.reshape(num_clusters * capacity, num_funcs, columns - split)
+    relayed = swapped(jnp.concatenate([piece[capacity:] for piece in arrived], axis=0), "cluster", 1)
     sources = [basis_vals, swapped(basis_vals, "blk", 1)]
 
-    later, _ = lax.optimization_barrier((intersection, pieces[0]))
-    my_row = lax.dynamic_index_in_dim(later, my_cluster, 0, keepdims=False)
+    my_row = lax.dynamic_index_in_dim(listed, my_cluster, 0, keepdims=False)
     owner = my_row // atom_count
     same = jnp.logical_and(owner[:, None] == owner[None, :], jnp.arange(list_len)[:, None] > jnp.arange(list_len)[None, :])
     rank = jnp.sum(same.astype(jnp.int32), axis=1)
     turn = jnp.bitwise_xor(owner, my_cluster)
-    early_at = owner * capacity + rank
-    late_at = turn // 2 * capacity + rank + jnp.where(turn % 2 == 1, num_clusters // 2 * capacity, 0)
-
-    early = packed(early_at, [early])
+    early_at = turn // 2 * capacity + rank + jnp.where(turn % 2 == 1, num_clusters // 2 * capacity, 0)
+    late_at = owner * capacity + rank
+
+    early = packed(early_at, arrived, capacity, relayed)
     early_other = swapped(early, "blk", 1)
     gram = gram_of(early)
-    late = packed(late_at, [piece[:capacity] for piece in arrived] + relayed)
+    late = packed(late_at, [], 0, late)
     late_other = swapped(late, "blk", 1)
     gram = gram_of(late, gram)
     gram = gram_of(early_other, gram)

time: 59.4 us -> 56 us (0.943)
  the two profiles are of different devices: /device:TPU:0 before, /device:TPU:9 now
where the time goes in v2:
time: 56 us; the launch traced here: 55.2 us
  waiting for transfers between devices  23.4 us (42%)
  starting transfers between devices  22.7 us (41%)
  Pallas kernels  7.69 us (14%)
  between operations  0.76 us (1%)
  other arithmetic  0.56 us (1%)
    ppermute x11, waiting for transfers between devices, swapped(): lax.ppermute(value, axis, [(source, source ^ bits) for source in range(co...  23.4 us
    ppermute x11, starting transfers between devices, swapped(): lax.ppermute(value, axis, [(source, source ^ bits) for source in range(co...  15.8 us
    all_to_all x1, starting transfers between devices, two_blocks(): lax.all_to_all(late, 'cluster', split_axis=0, concat_axis=0, tiled=True)  6.84 us
    pallas_call x1, Pallas kernels, exchange(): pl.pallas_call(kernel, out_shape=jax.ShapeDtypeStruct((points, width), jn...  3.03 us
    pallas_call x1, Pallas kernels, outgoing(): pl.pallas_call(kernel, out_shape=[jax.ShapeDtypeStruct(intersection.shape...  2.61 us
    pallas_call x2, Pallas kernels, packed(): pl.pallas_call(kernel, out_shape=jax.ShapeDtypeStruct((list_len, num_func...  1.19 us
  transfers between devices with their start and end apart: 12, of which 10 were waited for; matrix products, arithmetic and copies ran while one was open for 1% of the time, Pallas kernels for 8%

profile of v2, /device:TPU:9, one launch (start us, length us, event | category | flops | bytes accessed | tf_op | source)
XLA Modules:
  0.0 55.2 jit_solution(13335936447066539261)
XLA Ops:
  0.0 1.2 %collective-permute-start = (bf16[256,256]{1,0:T(8,128)(2,1)}, bf16[256,256]{1,0:T(8,128)(2,1)S(1)}, u32[]{:S(2)}, u32[]{:S(2)}) collective-permute-start(bf16[256,256]{1,0:T(8,128)(2,1)} %refs_1_.1), channel_id=1, source_target_pairs={{0,1},{1,0},{2,3},{3,2},{4,5},{5,4},{6,7},{7,6},{8,9},{9,8},{10,11... | collective-permute-start | bytes 393224 | tf_op jit(solution)/shard_map/ppermute | solution.py:25
  1.2 2.6 %outgoing.1 = (s32[16,32]{1,0:T(8,128)S(1)}, bf16[64,8,384]{2,1,0:T(8,128)(2,1)}, bf16[8,8,640]{2,1,0:T(8,128)(2,1)S(1)}, bf16[8,8,640]{2,1,0:T(8,128)(2,1)S(1)}...) custom-call(s32[1]{0:T(128)} %bitcast.8.me_ref, ...), custom_call_target="tpu_custom_call" | custom-call | tf_op jit(solution)/shard_map/outgoing/pallas_call | solution.py:177
  3.9 6.8 %all-to-all-start = ((bf16[16,4,8,384]{3,2,1,0:T(8,128)(2,1)}), bf16[16,4,8,384]{3,2,1,0:T(8,128)(2,1)S(1)}, u32[]{:S(2)}, u32[]{:S(2)}) async-start(bf16[16,4,8,384]{3,2,1,0:T(8,128)(2,1)} %bitcast.12), calls=%async_computation | async-start | bytes 786432 | tf_op jit(solution)/shard_map/all_to_all | solution.py:247
  10.7 1.2 %collective-permute-start.1 = (bf16[8,8,640]{2,1,0:T(8,128)(2,1)S(1)}, bf16[8,8,640]{2,1,0:T(8,128)(2,1)S(1)}, u32[]{:S(2)}, u32[]{:S(2)}) collective-permute-start(bf16[8,8,640]{2,1,0:T(8,128)(2,1)S(1)} %get-tuple-element.17), channel_id=1, source_target_pairs={{0,4},{2,6},{4,0},{6,2},{8,12},{10,14},{12,8},{14,10},{16,20},{18,... | collective-permute-start | bytes 245768 | tf_op jit(solution)/shard_map/ppermute | solution.py:25
  11.9 0.3 collective-permute-start.2
  12.2 1.2 %collective-permute-start.3 = (bf16[8,8,640]{2,1,0:T(8,128)(2,1)S(1)}, bf16[8,8,640]{2,1,0:T(8,128)(2,1)S(1)}, u32[]{:S(2)}, u32[]{:S(2)}) collective-permute-start(bf16[8,8,640]{2,1,0:T(8,128)(2,1)S(1)} %get-tuple-element.19), channel_id=1, source_target_pairs={{0,12},{2,14},{4,8},{6,10},{8,4},{10,6},{12,0},{14,2},{16,28},{18,... | collective-permute-start | bytes 245768 | tf_op jit(solution)/shard_map/ppermute | solution.py:25
  13.3 2.1 %collective-permute-start.4 = (bf16[8,8,640]{2,1,0:T(8,128)(2,1)S(1)}, bf16[8,8,640]{2,1,0:T(8,128)(2,1)S(1)}, u32[]{:S(2)}, u32[]{:S(2)}) collective-permute-start(bf16[8,8,640]{2,1,0:T(8,128)(2,1)S(1)} %get-tuple-element.20), channel_id=1, source_target_pairs={{0,16},{2,18},{4,20},{6,22},{8,24},{10,26},{12,28},{14,30},{16,0},... | collective-permute-start | bytes 245768 | tf_op jit(solution)/shard_map/ppermute | solution.py:25
  15.5 0.2 convert_reduce_fusion
  15.7 0.8 %collective-permute-done.1.rest_1_ = bf16[8,8,640]{2,1,0:T(8,128)(2,1)S(1)} collective-permute-done((bf16[8,8,640]{2,1,0:T(8,128)(2,1)S(1)}, bf16[8,8,640]{2,1,0:T(8,128)(2,1)S(1)}, u32[]{:S(2)}, u32[]{:S(2)}) %collective-permute-start.1) | collective-permute-done | bytes 81952 | tf_op jit(solution)/shard_map/ppermute | solution.py:25
  16.4 3.3 %collective-permute-start.5 = (bf16[8,8,640]{2,1,0:T(8,128)(2,1)S(1)}, bf16[8,8,640]{2,1,0:T(8,128)(2,1)S(1)}, u32[]{:S(2)}, u32[]{:S(2)}) collective-permute-start(bf16[8,8,640]{2,1,0:T(8,128)(2,1)S(1)} %get-tuple-element.21), channel_id=1, source_target_pairs={{0,20},{2,22},{4,16},{6,18},{8,28},{10,30},{12,24},{14,26},{16,4},... | collective-permute-start | bytes 245768 | tf_op jit(solution)/shard_map/ppermute | solution.py:25
  19.7 0.5 collective-permute-done.2.rest_2_
  20.2 1.8 %collective-permute-start.6 = (bf16[8,8,640]{2,1,0:T(8,128)(2,1)S(1)}, bf16[8,8,640]{2,1,0:T(8,128)(2,1)S(1)}, u32[]{:S(2)}, u32[]{:S(2)}) collective-permute-start(bf16[8,8,640]{2,1,0:T(8,128)(2,1)S(1)} %get-tuple-element.22), channel_id=1, source_target_pairs={{0,24},{2,26},{4,28},{6,30},{8,16},{10,18},{12,20},{14,22},{16,8},... | collective-permute-start | bytes 245768 | tf_op jit(solution)/shard_map/ppermute | solution.py:25
  22.1 0.5 collective-permute-done.3.rest_3_
  22.6 2.1 %collective-permute-start.7 = (bf16[8,8,640]{2,1,0:T(8,128)(2,1)S(1)}, bf16[8,8,640]{2,1,0:T(8,128)(2,1)S(1)}, u32[]{:S(2)}, u32[]{:S(2)}) collective-permute-start(bf16[8,8,640]{2,1,0:T(8,128)(2,1)S(1)} %get-tuple-element.23), channel_id=1, source_target_pairs={{0,28},{2,30},{4,24},{6,26},{8,20},{10,22},{12,16},{14,18},{16,12}... | collective-permute-start | bytes 245768 | tf_op jit(solution)/shard_map/ppermute | solution.py:25
  24.7 0.6 %collective-permute-done.4.rest_4_ = bf16[8,8,640]{2,1,0:T(8,128)(2,1)S(1)} collective-permute-done((bf16[8,8,640]{2,1,0:T(8,128)(2,1)S(1)}, bf16[8,8,640]{2,1,0:T(8,128)(2,1)S(1)}, u32[]{:S(2)}, u32[]{:S(2)}) %collective-permute-start.4) | collective-permute-done | bytes 81952 | tf_op jit(solution)/shard_map/ppermute | solution.py:25
  25.3 2.7 %collective-permute-done.5.rest_5_ = bf16[8,8,640]{2,1,0:T(8,128)(2,1)S(1)} collective-permute-done((bf16[8,8,640]{2,1,0:T(8,128)(2,1)S(1)}, bf16[8,8,640]{2,1,0:T(8,128)(2,1)S(1)}, u32[]{:S(2)}, u32[]{:S(2)}) %collective-permute-start.5) | collective-permute-done | bytes 81952 | tf_op jit(solution)/shard_map/ppermute | solution.py:25
  28.0 5.4 %collective-permute-done.6.rest_6_ = bf16[8,8,640]{2,1,0:T(8,128)(2,1)S(1)} collective-permute-done((bf16[8,8,640]{2,1,0:T(8,128)(2,1)S(1)}, bf16[8,8,640]{2,1,0:T(8,128)(2,1)S(1)}, u32[]{:S(2)}, u32[]{:S(2)}) %collective-permute-start.6) | collective-permute-done | bytes 81952 | tf_op jit(solution)/shard_map/ppermute | solution.py:25
  33.5 2.6 %collective-permute-done.7.rest_7_ = bf16[8,8,640]{2,1,0:T(8,128)(2,1)S(1)} collective-permute-done((bf16[8,8,640]{2,1,0:T(8,128)(2,1)S(1)}, bf16[8,8,640]{2,1,0:T(8,128)(2,1)S(1)}, u32[]{:S(2)}, u32[]{:S(2)}) %collective-permute-start.7) | collective-permute-done | bytes 81952 | tf_op jit(solution)/shard_map/ppermute | solution.py:25
  36.1 1.0 %collective-permute-start.8 = (bf16[32,8,640]{2,1,0:T(8,128)(2,1)S(1)}, bf16[32,8,640]{2,1,0:T(8,128)(2,1)S(1)}, u32[]{:S(2)}, u32[]{:S(2)}) collective-permute-start(bf16[32,8,640]{2,1,0:T(8,128)(2,1)S(1)} %slice_dynamic-update-slice_fusion), channel_id=1, source_target_pairs={{0,2},{2,0},{4,6},{6,4},{8,10},{10,8},{12,14},{14,12},{16,18},{18,... | collective-permute-start | bytes 983048 | tf_op jit(solution)/shard_map/ppermute | solution.py:25
  37.1 0.1 pad_add_fusion
  37.2 1.2 %collective-permute-done.8.rest_8_ = bf16[32,8,640]{2,1,0:T(8,128)(2,1)S(1)} collective-permute-done((bf16[32,8,640]{2,1,0:T(8,128)(2,1)S(1)}, bf16[32,8,640]{2,1,0:T(8,128)(2,1)S(1)}, u32[]{:S(2)}, u32[]{:S(2)}) %collective-permute-start.8) | collective-permute-done | bytes 327712 | tf_op jit(solution)/shard_map/ppermute | solution.py:25
  38.4 0.0 copy-start.1
  38.4 0.6 %packed.2 = bf16[32,8,640]{2,1,0:T(8,128)(2,1)S(1)} custom-call(s32[32]{0:T(128)S(1)} %get-tuple-element.28.position_ref, bf16[8,8,640]{2,1,0:T(8,128)(2,1)S(1)} %get-tuple-element.16.rest_0_, bf16[8,8,640]{2,1,0:T(8,128)(2,1)S(1)} %collective-permute-done.1.rest_1_, bf16[8,8,640]{2,1,0:T(8,128)(2,1)S(1)} %collective-permute-done.2.rest_2_, ...), custom_call_target="tpu_custom_call" | custom-call | tf_op jit(solution)/shard_map/packed/pallas_call | solution.py:211
  39.0 0.3 collective-permute-start.9
  39.3 0.1 broadcast_add_fusion
  40.0 0.1 add.69.refs_0_
  40.1 0.0 all-to-all-done
  40.1 0.6 %packed.3 = bf16[32,8,384]{2,1,0:T(8,128)(2,1)S(1)} custom-call(s32[32]{0:T(128)S(1)} %get-tuple-element.27.position_ref, bf16[64,8,384]{2,1,0:T(8,128)(2,1)S(1)} %bitcast.33), custom_call_target="tpu_custom_call" | custom-call | tf_op jit(solution)/shard_map/packed/pallas_call | solution.py:211
  40.7 1.3 %collective-permute-start.10 = (bf16[256,384]{1,0:T(8,128)(2,1)S(1)}, bf16[256,384]{1,0:T(8,128)(2,1)S(1)}, u32[]{:S(2)}, u32[]{:S(2)}) collective-permute-start(bf16[256,384]{1,0:T(8,128)(2,1)S(1)} %bitcast.30), channel_id=1, source_target_pairs={{0,1},{1,0},{2,3},{3,2},{4,5},{5,4},{6,7},{7,6},{8,9},{9,8},{10,11... | collective-permute-start | bytes 589832 | tf_op jit(solution)/shard_map/ppermute | solution.py:25
  42.0 0.0 copy-done.1
  42.0 0.2 multiply_bitcast_fusion
  42.2 0.3 gram_of.3.refs_1_
  42.5 0.3 gram_of.4.refs_1_
  42.7 0.0 copy-start
  42.8 5.2 %collective-permute-done.9.refs_0_.refs_7_ = bf16[256,640]{1,0:T(8,128)(2,1)S(1)} collective-permute-done((bf16[256,640]{1,0:T(8,128)(2,1)S(1)}, bf16[256,640]{1,0:T(8,128)(2,1)S(1)}, u32[]{:S(2)}, u32[]{:S(2)}) %collective-permute-start.9) | collective-permute-done | bytes 327712 | tf_op jit(solution)/shard_map/ppermute | solution.py:25
  48.0 0.3 gram_of.5.refs_5_
  48.3 0.0 collective-permute-done.refs_2_
  48.3 3.9 %collective-permute-done.10.refs_9_ = bf16[256,384]{1,0:T(8,128)(2,1)S(1)} collective-permute-done((bf16[256,384]{1,0:T(8,128)(2,1)S(1)}, bf16[256,384]{1,0:T(8,128)(2,1)S(1)}, u32[]{:S(2)}, u32[]{:S(2)}) %collective-permute-start.10) | collective-permute-done | bytes 196640 | tf_op jit(solution)/shard_map/ppermute | solution.py:25
  52.2 0.0 copy-done
  52.2 3.0 %exchange.1 = bf16[256,2048]{1,0:T(8,128)(2,1)} custom-call(s32[4]{0:T(128)S(1)} %add.69.refs_0_, bf16[256,256]{1,0:T(8,128)(2,1)S(1)} %copy-done, bf16[256,256]{1,0:T(8,128)(2,1)S(1)} %collective-permute-done.refs_2_, f32[256,256]{1,0:T(8,128)S(1)} %get-tuple-element.26.refs_3_, f32[256,256]{1,0:T(8,128)S(1)} %get-tuple-element.25.refs_4_, ...), custom_call_target="tpu_custom_call" | custom-call | tf_op jit(solution)/shard_map/exchange/pallas_call | solution.py:90
  (11 shorter events, 0.1 us)
Async XLA Ops:
  0.0 48.3 %collective-permute-start = (bf16[256,256]{1,0:T(8,128)(2,1)}, bf16[256,256]{1,0:T(8,128)(2,1)S(1)}, u32[]{:S(2)}, u32[]{:S(2)}) collective-permute-start(bf16[256,256]{1,0:T(8,128)(2,1)} %refs_1_.1), channel_id=1, source_target_pairs={{0,1},{1,0},{2,3},{3,2},{4,5},{5,4},{6,7},{7,6},{8,9},{9,8},{10,11... | collective-permute-start | bytes 393224 | tf_op jit(solution)/shard_map/ppermute | solution.py:25
  3.9 36.2 %all-to-all-start = ((bf16[16,4,8,384]{3,2,1,0:T(8,128)(2,1)}), bf16[16,4,8,384]{3,2,1,0:T(8,128)(2,1)S(1)}, u32[]{:S(2)}, u32[]{:S(2)}) async-start(bf16[16,4,8,384]{3,2,1,0:T(8,128)(2,1)} %bitcast.12), calls=%async_computation | async-start | bytes 786432 | tf_op jit(solution)/shard_map/all_to_all | solution.py:247
  10.7 5.7 %collective-permute-start.1 = (bf16[8,8,640]{2,1,0:T(8,128)(2,1)S(1)}, bf16[8,8,640]{2,1,0:T(8,128)(2,1)S(1)}, u32[]{:S(2)}, u32[]{:S(2)}) collective-permute-start(bf16[8,8,640]{2,1,0:T(8,128)(2,1)S(1)} %get-tuple-element.17), channel_id=1, source_target_pairs={{0,4},{2,6},{4,0},{6,2},{8,12},{10,14},{12,8},{14,10},{16,20},{18,... | collective-permute-start | bytes 245768 | tf_op jit(solution)/shard_map/ppermute | solution.py:25
  11.9 8.3 %collective-permute-start.2 = (bf16[8,8,640]{2,1,0:T(8,128)(2,1)S(1)}, bf16[8,8,640]{2,1,0:T(8,128)(2,1)S(1)}, u32[]{:S(2)}, u32[]{:S(2)}) collective-permute-start(bf16[8,8,640]{2,1,0:T(8,128)(2,1)S(1)} %get-tuple-element.18), channel_id=1, source_target_pairs={{0,8},{2,10},{4,12},{6,14},{8,0},{10,2},{12,4},{14,6},{16,24},{18,... | collective-permute-start | bytes 245768 | tf_op jit(solution)/shard_map/ppermute | solution.py:25
  12.2 10.4 %collective-permute-start.3 = (bf16[8,8,640]{2,1,0:T(8,128)(2,1)S(1)}, bf16[8,8,640]{2,1,0:T(8,128)(2,1)S(1)}, u32[]{:S(2)}, u32[]{:S(2)}) collective-permute-start(bf16[8,8,640]{2,1,0:T(8,128)(2,1)S(1)} %get-tuple-element.19), channel_id=1, source_target_pairs={{0,12},{2,14},{4,8},{6,10},{8,4},{10,6},{12,0},{14,2},{16,28},{18,... | collective-permute-start | bytes 245768 | tf_op jit(solution)/shard_map/ppermute | solution.py:25
  13.3 11.9 %collective-permute-start.4 = (bf16[8,8,640]{2,1,0:T(8,128)(2,1)S(1)}, bf16[8,8,640]{2,1,0:T(8,128)(2,1)S(1)}, u32[]{:S(2)}, u32[]{:S(2)}) collective-permute-start(bf16[8,8,640]{2,1,0:T(8,128)(2,1)S(1)} %get-tuple-element.20), channel_id=1, source_target_pairs={{0,16},{2,18},{4,20},{6,22},{8,24},{10,26},{12,28},{14,30},{16,0},... | collective-permute-start | bytes 245768 | tf_op jit(solution)/shard_map/ppermute | solution.py:25
  16.4 11.6 %collective-permute-start.5 = (bf16[8,8,640]{2,1,0:T(8,128)(2,1)S(1)}, bf16[8,8,640]{2,1,0:T(8,128)(2,1)S(1)}, u32[]{:S(2)}, u32[]{:S(2)}) collective-permute-start(bf16[8,8,640]{2,1,0:T(8,128)(2,1)S(1)} %get-tuple-element.21), channel_id=1, source_target_pairs={{0,20},{2,22},{4,16},{6,18},{8,28},{10,30},{12,24},{14,26},{16,4},... | collective-permute-start | bytes 245768 | tf_op jit(solution)/shard_map/ppermute | solution.py:25
  20.2 13.2 %collective-permute-start.6 = (bf16[8,8,640]{2,1,0:T(8,128)(2,1)S(1)}, bf16[8,8,640]{2,1,0:T(8,128)(2,1)S(1)}, u32[]{:S(2)}, u32[]{:S(2)}) collective-permute-start(bf16[8,8,640]{2,1,0:T(8,128)(2,1)S(1)} %get-tuple-element.22), channel_id=1, source_target_pairs={{0,24},{2,26},{4,28},{6,30},{8,16},{10,18},{12,20},{14,22},{16,8},... | collective-permute-start | bytes 245768 | tf_op jit(solution)/shard_map/ppermute | solution.py:25
  22.6 13.5 %collective-permute-start.7 = (bf16[8,8,640]{2,1,0:T(8,128)(2,1)S(1)}, bf16[8,8,640]{2,1,0:T(8,128)(2,1)S(1)}, u32[]{:S(2)}, u32[]{:S(2)}) collective-permute-start(bf16[8,8,640]{2,1,0:T(8,128)(2,1)S(1)} %get-tuple-element.23), channel_id=1, source_target_pairs={{0,28},{2,30},{4,24},{6,26},{8,20},{10,22},{12,16},{14,18},{16,12}... | collective-permute-start | bytes 245768 | tf_op jit(solution)/shard_map/ppermute | solution.py:25
  36.1 2.2 %collective-permute-start.8 = (bf16[32,8,640]{2,1,0:T(8,128)(2,1)S(1)}, bf16[32,8,640]{2,1,0:T(8,128)(2,1)S(1)}, u32[]{:S(2)}, u32[]{:S(2)}) collective-permute-start(bf16[32,8,640]{2,1,0:T(8,128)(2,1)S(1)} %slice_dynamic-update-slice_fusion), channel_id=1, source_target_pairs={{0,2},{2,0},{4,6},{6,4},{8,10},{10,8},{12,14},{14,12},{16,18},{18,... | collective-permute-start | bytes 983048 | tf_op jit(solution)/shard_map/ppermute | solution.py:25
  38.4 3.6 %copy-start.1 = (bf16[256,7,256]{2,0,1:T(8,128)(2,1)S(1)}, bf16[256,7,256]{2,0,1:T(8,128)(2,1)}, u32[]{:S(2)}) copy-start(bf16[256,7,256]{2,0,1:T(8,128)(2,1)} %param.9) | copy-start | bytes 2752516
  39.0 9.0 %collective-permute-start.9 = (bf16[256,640]{1,0:T(8,128)(2,1)S(1)}, bf16[256,640]{1,0:T(8,128)(2,1)S(1)}, u32[]{:S(2)}, u32[]{:S(2)}) collective-permute-start(bf16[256,640]{1,0:T(8,128)(2,1)S(1)} %bitcast.27), channel_id=1, source_target_pairs={{0,1},{1,0},{2,3},{3,2},{4,5},{5,4},{6,7},{7,6},{8,9},{9,8},{10,11... | collective-permute-start | bytes 983048 | tf_op jit(solution)/shard_map/ppermute | solution.py:25
  40.7 11.5 %collective-permute-start.10 = (bf16[256,384]{1,0:T(8,128)(2,1)S(1)}, bf16[256,384]{1,0:T(8,128)(2,1)S(1)}, u32[]{:S(2)}, u32[]{:S(2)}) collective-permute-start(bf16[256,384]{1,0:T(8,128)(2,1)S(1)} %bitcast.30), channel_id=1, source_target_pairs={{0,1},{1,0},{2,3},{3,2},{4,5},{5,4},{6,7},{7,6},{8,9},{9,8},{10,11... | collective-permute-start | bytes 589832 | tf_op jit(solution)/shard_map/ppermute | solution.py:25
  42.7 9.4 %copy-start = (bf16[256,256]{1,0:T(8,128)(2,1)S(1)}, bf16[256,256]{1,0:T(8,128)(2,1)}, u32[]{:S(2)}) copy-start(bf16[256,256]{1,0:T(8,128)(2,1)} %refs_1_.1) | copy-start | bytes 393220

commit v3 on v2

v3 whole, which is shorter than its diff:
```python
import jax
import jax.numpy as jnp
from jax import lax
from jax.experimental import pallas as pl
from jax.experimental.pallas import tpu as pltpu
from jax.sharding import PartitionSpec as P


EARLY_PARTS = 5

VMEM = pl.BlockSpec(memory_space=pltpu.VMEM)
SMEM = pl.BlockSpec(memory_space=pltpu.SMEM)
HBM = pl.BlockSpec(memory_space=pltpu.HBM)
PARAMS = pltpu.CompilerParams(vmem_limit_bytes=12 * 2**20)


def passed_along(value, axis, steps):
    count = lax.axis_size(axis)
    pairs = [(source, (source + steps) % count) for source in range(count)]
    return lax.ppermute(value, axis, pairs)


def swapped(value, axis, bits):
    count = lax.axis_size(axis)
    return lax.ppermute(value, axis, [(source, source ^ bits) for source in range(count)])


def dot_nn(a, b):
    return lax.dot_general(a, b, (((1,), (0,)), ((), ())), preferred_element_type=jnp.float32)


def dot_nt(a, b):
    return lax.dot_general(a, b, (((1,), (1,)), ((), ())), preferred_element_type=jnp.float32)


def orbital_block(basis_refs, values):
    return jnp.concatenate([dot_nn(ref[...], values).astype(jnp.bfloat16) for ref in basis_refs], axis=0)


def orbitals_of(sources, values, density=None):
    num_sources = len(sources)
    points = sources[0].shape[0]

    def kernel(*refs):
        orbitals = orbital_block(refs[:num_sources], refs[num_sources][...])
        orbital_ref, density_ref = refs[-2:]
        orbital_ref[...] = orbitals
        total = dot_nt(orbitals[:points], orbitals)
        density_ref[...] = total if density is None else total + refs[num_sources + 1][...]

    operands = [*sources, values]
    if density is not None:
        operands.append(density)
    return pl.pallas_call(
        kernel,
        out_shape=[
            jax.ShapeDtypeStruct((num_sources * points, values.shape[1]), jnp.bfloat16),
            jax.ShapeDtypeStruct((points, num_sources * points), jnp.float32),
        ],
        in_specs=[VMEM] * len(operands),
        out_specs=[VMEM, VMEM],
        compiler_params=PARAMS,
        name="orbitals_of",
    )(*operands)


def exchange(starts, sources, factors, density, orbitals, values, width):
    num_sources = len(sources)
    num_known = len(orbitals)
    points = sources[0].shape[0]
    widths = [block.shape[1] for block in orbitals] + [values.shape[1]]

    def kernel(*refs):
        start_ref = refs[0]
        basis_refs = refs[1 : 1 + num_sources]
        factor_refs = refs[1 + num_sources : 1 + 2 * num_sources]
        rest = list(refs[1 + 2 * num_sources :])
        total = rest.pop(0)[...] if density is not None else None
        known_refs = rest[:num_known]
        value_ref, out_ref = rest[num_known : num_known + 2]
        held_refs = rest[num_known + 2 : -2]
        last_ref, sems = rest[-2:]
        last_ref[...] = orbital_block(basis_refs, value_ref[...])
        term = dot_nt(last_ref[:points], last_ref[...])
        total = term if total is None else total + term
        tiles = []
        for source in range(num_sources):
            part = total[:, source * points : (source + 1) * points]
            tiles.append((part * factor_refs[source][...]).astype(jnp.bfloat16))
        tiles = jnp.concatenate(tiles, axis=1)
        copies = []
        for at, ref in enumerate([*known_refs, last_ref]):
            held_refs[at][...] = dot_nn(tiles, ref[...]).astype(out_ref.dtype)
            start = pl.multiple_of(start_ref[at] * 128, 128)
            copy = pltpu.make_async_copy(held_refs[at], out_ref.at[:, pl.ds(start, widths[at])], sems.at[at])
            copy.start()
            copies.append(copy)
        for copy in copies:
            copy.wait()

    operands = [starts, *sources, *factors]
    if density is not None:
        operands.append(density)
    operands.extend([*orbitals, values])
    return pl.pallas_call(
        kernel,
        out_shape=jax.ShapeDtypeStruct((points, width), jnp.bfloat16),
        in_specs=[SMEM] + [VMEM] * (len(operands) - 1),
        out_specs=HBM,
        scratch_shapes=[pltpu.VMEM((points, columns), jnp.bfloat16) for columns in widths]
        + [pltpu.VMEM((num_sources * points, widths[-1]), jnp.bfloat16), pltpu.SemaphoreType.DMA((len(widths),))],
        compiler_params=PARAMS if num_sources == 2 else pltpu.CompilerParams(vmem_limit_bytes=32 * 2**20),
        name="exchange",
    )(*operands)


def second_halves(blocks):
    rows = blocks[0].shape[0]
    half = rows // 2

    def kernel(*refs):
        for at, ref in enumerate(refs[:-1]):
            refs[-1][at * half : (at + 1) * half] = ref[half:]

    return pl.pallas_call(
        kernel,
        out_shape=jax.ShapeDtypeStruct((len(blocks) * half,) + blocks[0].shape[1:], blocks[0].dtype),
        in_specs=[VMEM] * len(blocks),
        out_specs=VMEM,
        compiler_params=PARAMS,
        name="second_halves",
    )(*blocks)


def outgoing(coeff, intersection, my_cluster, capacity, split):
    num_clusters, list_len = intersection.shape
    atom_count, num_funcs, columns = coeff.shape
    slots = num_clusters * capacity
    lanes = 128

    def kernel(me_ref, list_ref, coeff_ref, list_held, late_ref, *rest):
        early_refs = rest[: num_clusters // 2]
        coeff_held, late_held, source_held, source_read, sems = rest[num_clusters // 2 :]
        coeff_copy = pltpu.make_async_copy(coeff_ref, coeff_held, sems.at[0])
        list_copy = pltpu.make_async_copy(list_ref, list_held, sems.at[1])
        late_copy = pltpu.make_async_copy(late_held, late_ref, sems.at[2])
        source_copy = pltpu.make_async_copy(source_held, source_read, sems.at[3])
        list_copy.start()
        coeff_copy.start()
        me = me_ref[0]
        ks = lax.broadcasted_iota(jnp.int32, (list_len, list_len), 0)
        ls = lax.broadcasted_iota(jnp.int32, (list_len, list_len), 1)
        earlier = jnp.where(ks < ls, 1.0, 0.0).astype(jnp.bfloat16)
        list_copy.wait()
        local = list_held[...] - me * atom_count
        mine = jnp.logical_and(local >= 0, local < atom_count)
        rank = dot_nn(jnp.where(mine, 1.0, 0.0).astype(jnp.bfloat16), earlier)
        lane = lax.broadcasted_iota(jnp.int32, (num_clusters, lanes), 1)
        source = jnp.zeros((num_clusters, lanes), jnp.int32)
        for slot in range(capacity):
            chosen = jnp.where(jnp.logical_and(mine, rank == slot), local, 0)
            source = jnp.where(lane == slot, jnp.sum(chosen, axis=1, keepdims=True), source)
        source_held[...] = source
        source_copy.start()
        source_copy.wait()
        coeff_copy.wait()
        for cluster in range(num_clusters):
            for slot in range(capacity):
                late_held[cluster * capacity + slot] = coeff_held[source_read[cluster, slot], :, split:]
        late_copy.start()
        for turn in range(num_clusters):
            cluster = jnp.bitwise_xor(me, turn)
            for slot in range(capacity):
                values = coeff_held[source_read[cluster, slot], :, :split]
                early_refs[turn // 2][turn % 2 * capacity + slot] = values
        late_copy.wait()

    count = num_clusters // 2
    late = jax.ShapeDtypeStruct((slots, num_funcs, columns - split), coeff.dtype)
    early = jax.ShapeDtypeStruct((2 * capacity, num_funcs, split), coeff.dtype)
    return pl.pallas_call(
        kernel,
        out_shape=[jax.ShapeDtypeStruct(intersection.shape, jnp.int32), late] + [early] * count,
        in_specs=[SMEM, HBM, HBM],
        out_specs=[VMEM, HBM] + [VMEM] * count,
        scratch_shapes=[
            pltpu.VMEM(coeff.shape, coeff.dtype),
            pltpu.VMEM((slots, num_funcs, columns - split), coeff.dtype),
            pltpu.VMEM((num_clusters, lanes), jnp.int32),
            pltpu.SMEM((num_clusters, lanes), jnp.int32),
            pltpu.SemaphoreType.DMA((4,)),
        ],
        compiler_params=PARAMS,
        name="outgoing",
    )(
        my_cluster.reshape(1),
        pltpu.with_memory_space_constraint(intersection, pltpu.HBM),
        pltpu.with_memory_space_constraint(coeff, pltpu.HBM),
    )


def packed(positions, blocks, taken, last):
    list_len = positions.shape[0]
    num_funcs, columns = last.shape[1:]
    slots = len(blocks) * taken + last.shape[0]

    def kernel(position_ref, *rest):
        last_ref, out_ref, held_ref = rest[len(blocks) :]
        for at, ref in enumerate(rest[: len(blocks)]):
            held_ref[at * taken : (at + 1) * taken] = ref[:taken]
        held_ref[len(blocks) * taken :] = last_ref[...]
        for k in range(list_len):
            out_ref[k] = held_ref[position_ref[k]]

    return pl.pallas_call(
        kernel,
        out_shape=jax.ShapeDtypeStruct((list_len, num_funcs, columns), last.dtype),
        in_specs=[SMEM] + [VMEM] * (len(blocks) + 1),
        out_specs=VMEM,
        scratch_shapes=[pltpu.VMEM((slots, num_funcs, columns), last.dtype)],
        compiler_params=PARAMS,
        name="packed",
    )(positions, *blocks, last).reshape(list_len * num_funcs, columns)


def screened_factors(coulomb, reach, by_step, norm_factor):
    half_stops = (coulomb.shape[1] - 1) // 2
    points = coulomb.shape[0]
    my_reach = reach[0]
    factors = []
    for step in sorted(by_step):
        total = jnp.zeros((points, coulomb.shape[2]), jnp.float32)
        for offset in by_step[step]:
            tile = coulomb[:, offset + half_stops, :].astype(jnp.float32)
            total = total + jnp.where(abs(offset) <= my_reach, tile, jnp.float32(0.0))
        factors.append(total * norm_factor)
    return factors


def two_blocks(coeff, intersection, basis_vals, factors, capacity):
    num_clusters, list_len = intersection.shape
    atom_count, num_funcs, columns = coeff.shape
    my_cluster = lax.axis_index("cluster")
    my_block = lax.axis_index("blk")
    split = max(columns * EARLY_PARTS // 8 // 128, 1) * 128
    listed, late, *pieces = outgoing(coeff, intersection, my_cluster, capacity, split)
    arrived = [pieces[0]]
    for m in range(1, len(pieces)):
        arrived.append(swapped(pieces[m], "cluster", 2 * m))
    late = late.reshape(num_clusters, capacity, num_funcs, columns - split)
    late = lax.all_to_all(late, "cluster", split_axis=0, concat_axis=0, tiled=True)
    late = late.reshape(num_clusters * capacity, num_funcs, columns - split)
    relayed = swapped(second_halves(arrived), "cluster", 1)
    sources = [basis_vals, swapped(basis_vals, "blk", 1)]

    my_row = lax.dynamic_index_in_dim(listed, my_cluster, 0, keepdims=False)
    owner = my_row // atom_count
    same = jnp.logical_and(owner[:, None] == owner[None, :], jnp.arange(list_len)[:, None] > jnp.arange(list_len)[None, :])
    rank = jnp.sum(same.astype(jnp.int32), axis=1)
    turn = jnp.bitwise_xor(owner, my_cluster)
    early_at = turn // 2 * capacity + rank + jnp.where(turn % 2 == 1, num_clusters // 2 * capacity, 0)
    late_at = owner * capacity + rank

    func = jnp.arange(list_len * num_funcs) % num_funcs
    late_row = jnp.repeat(late_at * num_funcs, num_funcs) + func
    late_order = late_row[:, None] == jnp.arange(num_clusters * capacity * num_funcs)[None, :]
    late_order = lax.optimization_barrier(late_order.astype(jnp.bfloat16))

    early = packed(early_at, arrived, capacity, relayed)
    early_other = swapped(early, "blk", 1)
    early_orbitals, density = orbitals_of(sources, early)
    late = dot_nn(late_order, late.reshape(-1, columns - split)).astype(jnp.bfloat16)
    late_other = swapped(late, "blk", 1)
    late_orbitals, density = orbitals_of(sources, late, density)
    early_other_orbitals, density = orbitals_of(sources, early_other, density)
    lanes = columns // 128
    begin = jnp.stack([my_block * lanes, (1 - my_block) * lanes])
    starts = (begin[None, :] + jnp.array([0, split // 128])[:, None]).reshape(-1)
    known = [early_orbitals, early_other_orbitals, late_orbitals]
    return exchange(starts, sources, factors, density, known, late_other, 2 * columns)


def many_blocks(coeff, intersection, basis_vals, factors, capacity, steps):
    num_clusters, list_len = intersection.shape
    atom_count, num_funcs, columns = coeff.shape
    my_cluster = lax.axis_index("cluster")
    num_blocks = lax.axis_size("blk")
    local_atom = intersection - my_cluster * atom_count
    mine = jnp.logical_and(local_atom >= 0, local_atom < atom_count)
    earlier = jnp.arange(list_len)[:, None] < jnp.arange(list_len)[None, :]
    rank = dot_nn(mine.astype(jnp.bfloat16), earlier.astype(jnp.bfloat16)).astype(jnp.int32)
    matches = jnp.logical_and(mine[:, None, :], rank[:, None, :] == jnp.arange(capacity)[None, :, None])
    source_rows = jnp.sum(jnp.where(matches, local_atom[:, None, :], 0), axis=2)
    outgoing = coeff.at[source_rows.reshape(-1)].get(mode="promise_in_bounds")
    outgoing = outgoing.reshape(num_clusters, capacity, num_funcs, columns)
    incoming = lax.all_to_all(outgoing, "cluster", split_axis=0, concat_axis=0, tiled=True)
    my_row = lax.dynamic_index_in_dim(intersection, my_cluster, 0, keepdims=False)
    my_owners = my_row // atom_count
    same = jnp.logical_and(my_owners[:, None] == my_owners[None, :], earlier.T)
    positions = my_owners * capacity + jnp.sum(same.astype(jnp.int32), axis=1)
    needed = incoming.reshape(num_clusters * capacity, num_funcs, columns)
    needed = needed.at[positions].get(mode="promise_in_bounds")
    needed = needed.reshape(list_len * num_funcs, columns)
    all_columns = lax.all_gather(needed, "blk", axis=1, tiled=True)
    sources = [basis_vals if step == 0 else passed_along(basis_vals, "blk", -step) for step in steps]
    starts = jnp.zeros((1,), jnp.int32)
    return exchange(starts, sources, factors, None, [], all_columns, num_blocks * columns)


def on_device(coeff, intersection, basis_vals, coulomb, reach):
    num_clusters = lax.axis_size("cluster")
    num_blocks = lax.axis_size("blk")
    list_len = intersection.shape[1]
    capacity = 2 * list_len // num_clusters
    half_stops = (coulomb.shape[1] - 1) // 2
    by_step = {}
    for offset in range(-half_stops, half_stops + 1):
        by_step.setdefault(offset % num_blocks, []).append(offset)
    factors = screened_factors(coulomb, reach, by_step, (coeff.shape[2] * num_blocks) ** (-0.5))
    if takes_two_blocks(num_clusters, num_blocks):
        return two_blocks(coeff, intersection, basis_vals, factors, capacity)
    return many_blocks(coeff, intersection, basis_vals, factors, capacity, sorted(by_step))


def takes_two_blocks(num_clusters, num_blocks):
    return num_blocks == 2 and num_clusters >= 16 and num_clusters & (num_clusters - 1) == 0


def solution(mesh):
    return jax.shard_map(
        on_device,
        mesh=mesh,
        in_specs=(
            P("cluster", None, "blk"),
            P(),
            P(("cluster", "blk"), None),
            P(("cluster", "blk"), None, None),
            P(("cluster", "blk")),
        ),
        out_specs=P(("cluster", "blk"), None),
        check_vma=False,
    )
```

time: 56 us -> 54 us (0.964)
  starting transfers between devices: 22.7 us -> 20.5 us
    ppermute x11, starting transfers between devices: 15.8 us -> 13.8 us  [swapped(): lax.ppermute(value, axis, [(source, source ^ bits) for source in range(co...]
    pallas_call x3 -> x4, Pallas kernels: 0.86 us -> 1.79 us  [the longest x3 1.77 us: orbitals_of(): pl.pallas_call(kernel, out_shape=[jax.ShapeDtypeStruct((num_sources * poi...]
    pallas_call x2 -> x1, Pallas kernels: 1.19 us -> 0.62 us  [packed(): pl.pallas_call(kernel, out_shape=jax.ShapeDtypeStruct((list_len, num_func...]
  transfers between devices with their start and end apart: 12 -> 12, of which waited for: 10 -> 8; matrix products, arithmetic and copies ran while one was open for 1% -> 2% of each run, Pallas kernels for 8% -> 5%
where the time goes in v3:
time: 54 us; the launch traced here: 53.2 us
  waiting for transfers between devices  23.3 us (43%)
  starting transfers between devices  20.5 us (38%)
  Pallas kernels  7.34 us (14%)
  between operations  0.78 us (1%)
  other arithmetic  0.68 us (1%)
    ppermute x11, waiting for transfers between devices, swapped(): lax.ppermute(value, axis, [(source, source ^ bits) for source in range(co...  23.3 us
    ppermute x11, starting transfers between devices, swapped(): lax.ppermute(value, axis, [(source, source ^ bits) for source in range(co...  13.8 us
    all_to_all x1, starting transfers between devices, two_blocks(): lax.all_to_all(late, 'cluster', split_axis=0, concat_axis=0, tiled=True)  6.69 us
    pallas_call x1, Pallas kernels, exchange(): pl.pallas_call(kernel, out_shape=jax.ShapeDtypeStruct((points, width), jn...  2.49 us
    pallas_call x1, Pallas kernels, outgoing(): pl.pallas_call(kernel, out_shape=[jax.ShapeDtypeStruct(intersection.shape...  2.43 us
    pallas_call x3, Pallas kernels, orbitals_of(): pl.pallas_call(kernel, out_shape=[jax.ShapeDtypeStruct((num_sources * poi...  1.77 us
  transfers between devices with their start and end apart: 12, of which 8 were waited for; matrix products, arithmetic and copies ran while one was open for 2% of the time, Pallas kernels for 5%

profile of v3, /device:TPU:9, one launch (start us, length us, event | category | flops | bytes accessed | tf_op | source)
XLA Modules:
  0.0 53.2 jit_solution(15417742139210860481)
XLA Ops:
  0.0 2.4 %outgoing.1 = (s32[16,32]{1,0:T(8,128)S(1)}, bf16[64,8,384]{2,1,0:T(8,128)(2,1)}, bf16[8,8,640]{2,1,0:T(8,128)(2,1)S(1)}, bf16[8,8,640]{2,1,0:T(8,128)(2,1)S(1)}...) custom-call(s32[1]{0:T(128)} %bitcast.8.me_ref, ...), custom_call_target="tpu_custom_call" | custom-call | tf_op jit(solution)/shard_map/outgoing/pallas_call | solution.py:181
  2.4 0.0 copy-start
  2.4 6.7 %all-to-all-start = ((bf16[16,4,8,384]{3,2,1,0:T(8,128)(2,1)}), bf16[16,4,8,384]{3,2,1,0:T(8,128)(2,1)S(1)}, u32[]{:S(2)}, u32[]{:S(2)}) async-start(bf16[16,4,8,384]{3,2,1,0:T(8,128)(2,1)} %bitcast.12), calls=%async_computation | async-start | bytes 786432 | tf_op jit(solution)/shard_map/all_to_all | solution.py:251
  9.1 1.2 %collective-permute-start.1 = (bf16[8,8,640]{2,1,0:T(8,128)(2,1)S(1)}, bf16[8,8,640]{2,1,0:T(8,128)(2,1)S(1)}, u32[]{:S(2)}, u32[]{:S(2)}) collective-permute-start(bf16[8,8,640]{2,1,0:T(8,128)(2,1)S(1)} %get-tuple-element.23), channel_id=1, source_target_pairs={{0,4},{2,6},{4,0},{6,2},{8,12},{10,14},{12,8},{14,10},{16,20},{18,... | collective-permute-start | bytes 245768 | tf_op jit(solution)/shard_map/ppermute | solution.py:25
  10.3 0.3 collective-permute-start.2
  10.6 1.2 %collective-permute-start.3 = (bf16[8,8,640]{2,1,0:T(8,128)(2,1)S(1)}, bf16[8,8,640]{2,1,0:T(8,128)(2,1)S(1)}, u32[]{:S(2)}, u32[]{:S(2)}) collective-permute-start(bf16[8,8,640]{2,1,0:T(8,128)(2,1)S(1)} %get-tuple-element.25), channel_id=1, source_target_pairs={{0,12},{2,14},{4,8},{6,10},{8,4},{10,6},{12,0},{14,2},{16,28},{18,... | collective-permute-start | bytes 245768 | tf_op jit(solution)/shard_map/ppermute | solution.py:25
  11.8 2.1 %collective-permute-start.4 = (bf16[8,8,640]{2,1,0:T(8,128)(2,1)S(1)}, bf16[8,8,640]{2,1,0:T(8,128)(2,1)S(1)}, u32[]{:S(2)}, u32[]{:S(2)}) collective-permute-start(bf16[8,8,640]{2,1,0:T(8,128)(2,1)S(1)} %get-tuple-element.26), channel_id=1, source_target_pairs={{0,16},{2,18},{4,20},{6,22},{8,24},{10,26},{12,28},{14,30},{16,0},... | collective-permute-start | bytes 245768 | tf_op jit(solution)/shard_map/ppermute | solution.py:25
  13.9 1.2 %collective-permute-start.5 = (bf16[8,8,640]{2,1,0:T(8,128)(2,1)S(1)}, bf16[8,8,640]{2,1,0:T(8,128)(2,1)S(1)}, u32[]{:S(2)}, u32[]{:S(2)}) collective-permute-start(bf16[8,8,640]{2,1,0:T(8,128)(2,1)S(1)} %get-tuple-element.27), channel_id=1, source_target_pairs={{0,20},{2,22},{4,16},{6,18},{8,28},{10,30},{12,24},{14,26},{16,4},... | collective-permute-start | bytes 245768 | tf_op jit(solution)/shard_map/ppermute | solution.py:25
  15.1 0.2 convert_reduce_fusion
  15.3 0.1 broadcast_in_dim.26
  15.4 0.1 reshape.102
  15.5 0.0 collective-permute-done.1.refs_1_.rest_1_
  15.5 1.3 %collective-permute-start.6 = (bf16[8,8,640]{2,1,0:T(8,128)(2,1)S(1)}, bf16[8,8,640]{2,1,0:T(8,128)(2,1)S(1)}, u32[]{:S(2)}, u32[]{:S(2)}) collective-permute-start(bf16[8,8,640]{2,1,0:T(8,128)(2,1)S(1)} %get-tuple-element.28), channel_id=1, source_target_pairs={{0,24},{2,26},{4,28},{6,30},{8,16},{10,18},{12,20},{14,22},{16,8},... | collective-permute-start | bytes 245768 | tf_op jit(solution)/shard_map/ppermute | solution.py:25
  16.8 1.9 %collective-permute-done.2.refs_2_.rest_2_ = bf16[8,8,640]{2,1,0:T(8,128)(2,1)S(1)} collective-permute-done((bf16[8,8,640]{2,1,0:T(8,128)(2,1)S(1)}, bf16[8,8,640]{2,1,0:T(8,128)(2,1)S(1)}, u32[]{:S(2)}, u32[]{:S(2)}) %collective-permute-start.2) | collective-permute-done | bytes 81952 | tf_op jit(solution)/shard_map/ppermute | solution.py:25
  18.7 2.7 %collective-permute-start.7 = (bf16[8,8,640]{2,1,0:T(8,128)(2,1)S(1)}, bf16[8,8,640]{2,1,0:T(8,128)(2,1)S(1)}, u32[]{:S(2)}, u32[]{:S(2)}) collective-permute-start(bf16[8,8,640]{2,1,0:T(8,128)(2,1)S(1)} %get-tuple-element.29), channel_id=1, source_target_pairs={{0,28},{2,30},{4,24},{6,26},{8,20},{10,22},{12,16},{14,18},{16,12}... | collective-permute-start | bytes 245768 | tf_op jit(solution)/shard_map/ppermute | solution.py:25
  21.4 0.1 pad_add_fusion
  21.5 0.0 collective-permute-done.3.refs_3_.rest_3_
  21.5 0.0 copy-done
  21.5 1.2 %collective-permute-start = (bf16[256,256]{1,0:T(8,128)(2,1)S(1)}, bf16[256,256]{1,0:T(8,128)(2,1)S(1)}, u32[]{:S(2)}, u32[]{:S(2)}) collective-permute-start(bf16[256,256]{1,0:T(8,128)(2,1)S(1)} %copy-done), channel_id=1, source_target_pairs={{0,1},{1,0},{2,3},{3,2},{4,5},{5,4},{6,7},{7,6},{8,9},{9,8},{10,11... | collective-permute-start | bytes 393224 | tf_op jit(solution)/shard_map/ppermute | solution.py:25
  22.7 1.0 %collective-permute-done.4.refs_4_.rest_4_ = bf16[8,8,640]{2,1,0:T(8,128)(2,1)S(1)} collective-permute-done((bf16[8,8,640]{2,1,0:T(8,128)(2,1)S(1)}, bf16[8,8,640]{2,1,0:T(8,128)(2,1)S(1)}, u32[]{:S(2)}, u32[]{:S(2)}) %collective-permute-start.4) | collective-permute-done | bytes 81952 | tf_op jit(solution)/shard_map/ppermute | solution.py:25
  23.7 4.5 %collective-permute-done.5.refs_5_.rest_5_ = bf16[8,8,640]{2,1,0:T(8,128)(2,1)S(1)} collective-permute-done((bf16[8,8,640]{2,1,0:T(8,128)(2,1)S(1)}, bf16[8,8,640]{2,1,0:T(8,128)(2,1)S(1)}, u32[]{:S(2)}, u32[]{:S(2)}) %collective-permute-start.5) | collective-permute-done | bytes 81952 | tf_op jit(solution)/shard_map/ppermute | solution.py:25
  28.2 3.7 %collective-permute-done.6.refs_6_.rest_6_ = bf16[8,8,640]{2,1,0:T(8,128)(2,1)S(1)} collective-permute-done((bf16[8,8,640]{2,1,0:T(8,128)(2,1)S(1)}, bf16[8,8,640]{2,1,0:T(8,128)(2,1)S(1)}, u32[]{:S(2)}, u32[]{:S(2)}) %collective-permute-start.6) | collective-permute-done | bytes 81952 | tf_op jit(solution)/shard_map/ppermute | solution.py:25
  31.9 2.7 %collective-permute-done.7.refs_7_.rest_7_ = bf16[8,8,640]{2,1,0:T(8,128)(2,1)S(1)} collective-permute-done((bf16[8,8,640]{2,1,0:T(8,128)(2,1)S(1)}, bf16[8,8,640]{2,1,0:T(8,128)(2,1)S(1)}, u32[]{:S(2)}, u32[]{:S(2)}) %collective-permute-start.7) | collective-permute-done | bytes 81952 | tf_op jit(solution)/shard_map/ppermute | solution.py:25
  34.6 1.0 %collective-permute-start.8 = (bf16[32,8,640]{2,1,0:T(8,128)(2,1)S(1)}, bf16[32,8,640]{2,1,0:T(8,128)(2,1)S(1)}, u32[]{:S(2)}, u32[]{:S(2)}) collective-permute-start(bf16[32,8,640]{2,1,0:T(8,128)(2,1)S(1)} %second_halves.1), channel_id=1, source_target_pairs={{0,2},{2,0},{4,6},{6,4},{8,10},{10,8},{12,14},{14,12},{16,18},{18,... | collective-permute-start | bytes 983048 | tf_op jit(solution)/shard_map/ppermute | solution.py:25
  35.6 0.1 broadcast_add_fusion
  36.4 0.1 add.86.refs_0_
  36.4 0.1 fusion
  36.6 0.3 collective-permute-done.8.rest_8_
  36.9 0.0 copy-start.1
  36.9 0.6 %packed.1 = bf16[32,8,640]{2,1,0:T(8,128)(2,1)S(1)} custom-call(s32[32]{0:T(128)S(1)} %get-tuple-element.40.position_ref, bf16[8,8,640]{2,1,0:T(8,128)(2,1)S(1)} %get-tuple-element.22.refs_0_.rest_0_, bf16[8,8,640]{2,1,0:T(8,128)(2,1)S(1)} %collective-permute-done.1.refs_1_.rest_1_, bf16[8,8,640]{2,1,0:T(8,128)(2,1)S(1)} %collective-permute-done.2.refs_2_.rest_2_, ...), custom_call_target="tpu_custom_call" | custom-call | tf_op jit(solution)/shard_map/packed/pallas_call | solution.py:215
  37.5 1.3 %collective-permute-start.9 = (bf16[256,640]{1,0:T(8,128)(2,1)S(1)}, bf16[256,640]{1,0:T(8,128)(2,1)S(1)}, u32[]{:S(2)}, u32[]{:S(2)}) collective-permute-start(bf16[256,640]{1,0:T(8,128)(2,1)S(1)} %bitcast.28), channel_id=1, source_target_pairs={{0,1},{1,0},{2,3},{3,2},{4,5},{5,4},{6,7},{7,6},{8,9},{9,8},{10,11... | collective-permute-start | bytes 983048 | tf_op jit(solution)/shard_map/ppermute | solution.py:25
  38.8 0.0 all-to-all-done
  38.8 0.3 convolution_convert_fusion.refs_2_
  39.1 0.3 collective-permute-start.10
  39.4 0.0 copy-done.1
  39.4 0.2 multiply_bitcast_fusion
  39.6 0.0 collective-permute-done.refs_1_.refs_2_
  39.6 0.6 %orbitals_of.3 = (bf16[512,640]{1,0:T(8,128)(2,1)S(1)}, f32[256,512]{1,0:T(8,128)S(1)}) custom-call(bf16[256,256]{1,0:T(8,128)(2,1)S(1)} %copy-done, bf16[256,256]{1,0:T(8,128)(2,1)S(1)} %collective-permute-done.refs_1_.refs_2_, bf16[256,640]{1,0:T(8,128)(2,1)S(1)} %bitcast.29), custom_call_target="tpu_custom_call" | custom-call | tf_op jit(solution)/shard_map/orbitals_of/pallas_call | solution.py:54
  40.2 0.5 orbitals_of.4
  40.8 5.7 %collective-permute-done.9.refs_2_ = bf16[256,640]{1,0:T(8,128)(2,1)S(1)} collective-permute-done((bf16[256,640]{1,0:T(8,128)(2,1)S(1)}, bf16[256,640]{1,0:T(8,128)(2,1)S(1)}, u32[]{:S(2)}, u32[]{:S(2)}) %collective-permute-start.9) | collective-permute-done | bytes 327712 | tf_op jit(solution)/shard_map/ppermute | solution.py:25
  46.5 0.6 %orbitals_of.5 = (bf16[512,640]{1,0:T(8,128)(2,1)S(1)}, f32[256,512]{1,0:T(8,128)S(1)}) custom-call(bf16[256,256]{1,0:T(8,128)(2,1)S(1)} %copy-done, bf16[256,256]{1,0:T(8,128)(2,1)S(1)} %collective-permute-done.refs_1_.refs_2_, bf16[256,640]{1,0:T(8,128)(2,1)S(1)} %collective-permute-done.9.refs_2_, f32[256,512]{1,0:T(8,128)S(1)} %get-tuple-element.32.refs_3_), custom_call_target="tpu_custom_call" | custom-call | tf_op jit(solution)/shard_map/orbitals_of/pallas_call | solution.py:54
  47.1 3.6 %collective-permute-done.10.refs_9_ = bf16[256,384]{1,0:T(8,128)(2,1)S(1)} collective-permute-done((bf16[256,384]{1,0:T(8,128)(2,1)S(1)}, bf16[256,384]{1,0:T(8,128)(2,1)S(1)}, u32[]{:S(2)}, u32[]{:S(2)}) %collective-permute-start.10) | collective-permute-done | bytes 196640 | tf_op jit(solution)/shard_map/ppermute | solution.py:25
  50.7 2.5 %exchange.1 = bf16[256,2048]{1,0:T(8,128)(2,1)} custom-call(s32[4]{0:T(128)S(1)} %add.86.refs_0_, bf16[256,256]{1,0:T(8,128)(2,1)S(1)} %copy-done, bf16[256,256]{1,0:T(8,128)(2,1)S(1)} %collective-permute-done.refs_1_.refs_2_, f32[256,256]{1,0:T(8,128)S(1)} %get-tuple-element.38.refs_3_, f32[256,256]{1,0:T(8,128)S(1)} %get-tuple-element.37.refs_4_, ...), custom_call_target="tpu_custom_call" | custom-call | tf_op jit(solution)/shard_map/exchange/pallas_call | solution.py:105
  (5 shorter events, 0.1 us)
Async XLA Ops:
  2.4 19.0 %copy-start = (bf16[256,256]{1,0:T(8,128)(2,1)S(1)}, bf16[256,256]{1,0:T(8,128)(2,1)}, u32[]{:S(2)}) copy-start(bf16[256,256]{1,0:T(8,128)(2,1)} %refs_1_.1) | copy-start | bytes 393220
  2.4 36.4 %all-to-all-start = ((bf16[16,4,8,384]{3,2,1,0:T(8,128)(2,1)}), bf16[16,4,8,384]{3,2,1,0:T(8,128)(2,1)S(1)}, u32[]{:S(2)}, u32[]{:S(2)}) async-start(bf16[16,4,8,384]{3,2,1,0:T(8,128)(2,1)} %bitcast.12), calls=%async_computation | async-start | bytes 786432 | tf_op jit(solution)/shard_map/all_to_all | solution.py:251
  9.1 6.3 %collective-permute-start.1 = (bf16[8,8,640]{2,1,0:T(8,128)(2,1)S(1)}, bf16[8,8,640]{2,1,0:T(8,128)(2,1)S(1)}, u32[]{:S(2)}, u32[]{:S(2)}) collective-permute-start(bf16[8,8,640]{2,1,0:T(8,128)(2,1)S(1)} %get-tuple-element.23), channel_id=1, source_target_pairs={{0,4},{2,6},{4,0},{6,2},{8,12},{10,14},{12,8},{14,10},{16,20},{18,... | collective-permute-start | bytes 245768 | tf_op jit(solution)/shard_map/ppermute | solution.py:25
  10.3 8.3 %collective-permute-start.2 = (bf16[8,8,640]{2,1,0:T(8,128)(2,1)S(1)}, bf16[8,8,640]{2,1,0:T(8,128)(2,1)S(1)}, u32[]{:S(2)}, u32[]{:S(2)}) collective-permute-start(bf16[8,8,640]{2,1,0:T(8,128)(2,1)S(1)} %get-tuple-element.24), channel_id=1, source_target_pairs={{0,8},{2,10},{4,12},{6,14},{8,0},{10,2},{12,4},{14,6},{16,24},{18,... | collective-permute-start | bytes 245768 | tf_op jit(solution)/shard_map/ppermute | solution.py:25
  10.6 10.9 %collective-permute-start.3 = (bf16[8,8,640]{2,1,0:T(8,128)(2,1)S(1)}, bf16[8,8,640]{2,1,0:T(8,128)(2,1)S(1)}, u32[]{:S(2)}, u32[]{:S(2)}) collective-permute-start(bf16[8,8,640]{2,1,0:T(8,128)(2,1)S(1)} %get-tuple-element.25), channel_id=1, source_target_pairs={{0,12},{2,14},{4,8},{6,10},{8,4},{10,6},{12,0},{14,2},{16,28},{18,... | collective-permute-start | bytes 245768 | tf_op jit(solution)/shard_map/ppermute | solution.py:25
  11.8 11.9 %collective-permute-start.4 = (bf16[8,8,640]{2,1,0:T(8,128)(2,1)S(1)}, bf16[8,8,640]{2,1,0:T(8,128)(2,1)S(1)}, u32[]{:S(2)}, u32[]{:S(2)}) collective-permute-start(bf16[8,8,640]{2,1,0:T(8,128)(2,1)S(1)} %get-tuple-element.26), channel_id=1, source_target_pairs={{0,16},{2,18},{4,20},{6,22},{8,24},{10,26},{12,28},{14,30},{16,0},... | collective-permute-start | bytes 245768 | tf_op jit(solution)/shard_map/ppermute | solution.py:25
  13.9 14.4 %collective-permute-start.5 = (bf16[8,8,640]{2,1,0:T(8,128)(2,1)S(1)}, bf16[8,8,640]{2,1,0:T(8,128)(2,1)S(1)}, u32[]{:S(2)}, u32[]{:S(2)}) collective-permute-start(bf16[8,8,640]{2,1,0:T(8,128)(2,1)S(1)} %get-tuple-element.27), channel_id=1, source_target_pairs={{0,20},{2,22},{4,16},{6,18},{8,28},{10,30},{12,24},{14,26},{16,4},... | collective-permute-start | bytes 245768 | tf_op jit(solution)/shard_map/ppermute | solution.py:25
  15.5 16.4 %collective-permute-start.6 = (bf16[8,8,640]{2,1,0:T(8,128)(2,1)S(1)}, bf16[8,8,640]{2,1,0:T(8,128)(2,1)S(1)}, u32[]{:S(2)}, u32[]{:S(2)}) collective-permute-start(bf16[8,8,640]{2,1,0:T(8,128)(2,1)S(1)} %get-tuple-element.28), channel_id=1, source_target_pairs={{0,24},{2,26},{4,28},{6,30},{8,16},{10,18},{12,20},{14,22},{16,8},... | collective-permute-start | bytes 245768 | tf_op jit(solution)/shard_map/ppermute | solution.py:25
  18.7 15.9 %collective-permute-start.7 = (bf16[8,8,640]{2,1,0:T(8,128)(2,1)S(1)}, bf16[8,8,640]{2,1,0:T(8,128)(2,1)S(1)}, u32[]{:S(2)}, u32[]{:S(2)}) collective-permute-start(bf16[8,8,640]{2,1,0:T(8,128)(2,1)S(1)} %get-tuple-element.29), channel_id=1, source_target_pairs={{0,28},{2,30},{4,24},{6,26},{8,20},{10,22},{12,16},{14,18},{16,12}... | collective-permute-start | bytes 245768 | tf_op jit(solution)/shard_map/ppermute | solution.py:25
  21.5 18.1 %collective-permute-start = (bf16[256,256]{1,0:T(8,128)(2,1)S(1)}, bf16[256,256]{1,0:T(8,128)(2,1)S(1)}, u32[]{:S(2)}, u32[]{:S(2)}) collective-permute-start(bf16[256,256]{1,0:T(8,128)(2,1)S(1)} %copy-done), channel_id=1, source_target_pairs={{0,1},{1,0},{2,3},{3,2},{4,5},{5,4},{6,7},{7,6},{8,9},{9,8},{10,11... | collective-permute-start | bytes 393224 | tf_op jit(solution)/shard_map/ppermute | solution.py:25
  34.6 2.3 %collective-permute-start.8 = (bf16[32,8,640]{2,1,0:T(8,128)(2,1)S(1)}, bf16[32,8,640]{2,1,0:T(8,128)(2,1)S(1)}, u32[]{:S(2)}, u32[]{:S(2)}) collective-permute-start(bf16[32,8,640]{2,1,0:T(8,128)(2,1)S(1)} %second_halves.1), channel_id=1, source_target_pairs={{0,2},{2,0},{4,6},{6,4},{8,10},{10,8},{12,14},{14,12},{16,18},{18,... | collective-permute-start | bytes 983048 | tf_op jit(solution)/shard_map/ppermute | solution.py:25
  36.9 2.5 %copy-start.1 = (bf16[256,7,256]{2,0,1:T(8,128)(2,1)S(1)}, bf16[256,7,256]{2,0,1:T(8,128)(2,1)}, u32[]{:S(2)}) copy-start(bf16[256,7,256]{2,0,1:T(8,128)(2,1)} %param.9) | copy-start | bytes 2752516
  37.5 9.0 %collective-permute-start.9 = (bf16[256,640]{1,0:T(8,128)(2,1)S(1)}, bf16[256,640]{1,0:T(8,128)(2,1)S(1)}, u32[]{:S(2)}, u32[]{:S(2)}) collective-permute-start(bf16[256,640]{1,0:T(8,128)(2,1)S(1)} %bitcast.28), channel_id=1, source_target_pairs={{0,1},{1,0},{2,3},{3,2},{4,5},{5,4},{6,7},{7,6},{8,9},{9,8},{10,11... | collective-permute-start | bytes 983048 | tf_op jit(solution)/shard_map/ppermute | solution.py:25
  39.1 11.6 %collective-permute-start.10 = (bf16[256,384]{1,0:T(8,128)(2,1)S(1)}, bf16[256,384]{1,0:T(8,128)(2,1)S(1)}, u32[]{:S(2)}, u32[]{:S(2)}) collective-permute-start(bf16[256,384]{1,0:T(8,128)(2,1)S(1)} %convolution_convert_fusion.refs_2_), channel_id=1, source_target_pairs={{0,1},{1,0},{2,3},{3,2},{4,5},{5,4},{6,7},{7,6},{8,9},{9,8},{10,11... | collective-permute-start | bytes 589832 | tf_op jit(solution)/shard_map/ppermute | solution.py:25

commit v4 on v3

--- a/solution.py
+++ b/solution.py
@@ -64,17 +64,19 @@
     )(*operands)
 
 
-def exchange(starts, sources, factors, density, orbitals, values, width):
+def exchange(places, sources, factors, density, orbitals, values, width):
     num_sources = len(sources)
     num_known = len(orbitals)
     points = sources[0].shape[0]
     widths = [block.shape[1] for block in orbitals] + [values.shape[1]]
 
+    num_blocks = lax.axis_size("blk")
+
     def kernel(*refs):
-        start_ref = refs[0]
-        basis_refs = refs[1 : 1 + num_sources]
-        factor_refs = refs[1 + num_sources : 1 + 2 * num_sources]
-        rest = list(refs[1 + 2 * num_sources :])
+        basis_refs = refs[:num_sources]
+        factor_refs = refs[num_sources : 2 * num_sources]
+        rest = list(refs[2 * num_sources :])
+        my_block = lax.axis_index("blk")
         total = rest.pop(0)[...] if density is not None else None
         known_refs = rest[:num_known]
         value_ref, out_ref = rest[num_known : num_known + 2]
@@ -91,21 +93,23 @@
         copies = []
         for at, ref in enumerate([*known_refs, last_ref]):
             held_refs[at][...] = dot_nn(tiles, ref[...]).astype(out_ref.dtype)
-            start = pl.multiple_of(start_ref[at] * 128, 128)
+            turn, first = places[at]
+            start = lax.rem(my_block + turn, num_blocks) * (width // num_blocks) + first if turn is not None else first
+            start = pl.multiple_of(start, 128)
             copy = pltpu.make_async_copy(held_refs[at], out_ref.at[:, pl.ds(start, widths[at])], sems.at[at])
             copy.start()
             copies.append(copy)
         for copy in copies:
             copy.wait()
 
-    operands = [starts, *sources, *factors]
+    operands = [*sources, *factors]
     if density is not None:
         operands.append(density)
     operands.extend([*orbitals, values])
     return pl.pallas_call(
         kernel,
         out_shape=jax.ShapeDtypeStruct((points, width), jnp.bfloat16),
-        in_specs=[SMEM] + [VMEM] * (len(operands) - 1),
+        in_specs=[VMEM] * len(operands),
         out_specs=HBM,
         scratch_shapes=[pltpu.VMEM((points, columns), jnp.bfloat16) for columns in widths]
         + [pltpu.VMEM((num_sources * points, widths[-1]), jnp.bfloat16), pltpu.SemaphoreType.DMA((len(widths),))],
@@ -132,22 +136,24 @@
     )(*blocks)
 
 
-def outgoing(coeff, intersection, my_cluster, capacity, split):
+def outgoing(coeff, intersection, basis_vals, capacity, split):
     num_clusters, list_len = intersection.shape
     atom_count, num_funcs, columns = coeff.shape
     slots = num_clusters * capacity
     lanes = 128
 
-    def kernel(me_ref, list_ref, coeff_ref, list_held, late_ref, *rest):
+    def kernel(list_ref, coeff_ref, basis_ref, early_at_ref, late_at_ref, basis_held, late_ref, *rest):
         early_refs = rest[: num_clusters // 2]
-        coeff_held, late_held, source_held, source_read, sems = rest[num_clusters // 2 :]
+        list_held, coeff_held, late_held, source_held, source_read, sems = rest[num_clusters // 2 :]
         coeff_copy = pltpu.make_async_copy(coeff_ref, coeff_held, sems.at[0])
         list_copy = pltpu.make_async_copy(list_ref, list_held, sems.at[1])
         late_copy = pltpu.make_async_copy(late_held, late_ref, sems.at[2])
         source_copy = pltpu.make_async_copy(source_held, source_read, sems.at[3])
+        basis_copy = pltpu.make_async_copy(basis_ref, basis_held, sems.at[4])
         list_copy.start()
         coeff_copy.start()
-        me = me_ref[0]
+        basis_copy.start()
+        me = lax.axis_index("cluster")
         ks = lax.broadcasted_iota(jnp.int32, (list_len, list_len), 0)
         ls = lax.broadcasted_iota(jnp.int32, (list_len, list_len), 1)
         earlier = jnp.where(ks < ls, 1.0, 0.0).astype(jnp.bfloat16)
@@ -162,6 +168,15 @@
             source = jnp.where(lane == slot, jnp.sum(chosen, axis=1, keepdims=True), source)
         source_held[...] = source
         source_copy.start()
+        owner = jnp.broadcast_to(list_held[pl.ds(me, 1)], (list_len, list_len)) // atom_count
+        owner_across = jnp.sum(jnp.where(ks == ls, owner, 0), axis=1, keepdims=True)
+        before = jnp.where(jnp.logical_and(owner == owner_across, ks < ls), 1, 0)
+        slot = jnp.sum(before, axis=0, keepdims=True)
+        owner = owner[:1]
+        turn = jnp.bitwise_xor(owner, me)
+        side = jnp.bitwise_and(turn, 1)
+        early_at_ref[...] = (turn - side) // 2 * capacity + side * (slots // 2) + slot
+        late_at_ref[...] = owner * capacity + slot
         source_copy.wait()
         coeff_copy.wait()
         for cluster in range(num_clusters):
@@ -174,33 +189,41 @@
                 values = coeff_held[source_read[cluster, slot], :, :split]
                 early_refs[turn // 2][turn % 2 * capacity + slot] = values
         late_copy.wait()
+        basis_copy.wait()
 
     count = num_clusters // 2
     late = jax.ShapeDtypeStruct((slots, num_funcs, columns - split), coeff.dtype)
     early = jax.ShapeDtypeStruct((2 * capacity, num_funcs, split), coeff.dtype)
     return pl.pallas_call(
         kernel,
-        out_shape=[jax.ShapeDtypeStruct(intersection.shape, jnp.int32), late] + [early] * count,
-        in_specs=[SMEM, HBM, HBM],
-        out_specs=[VMEM, HBM] + [VMEM] * count,
+        out_shape=[
+            jax.ShapeDtypeStruct((1, list_len), jnp.int32),
+            jax.ShapeDtypeStruct((1, list_len), jnp.int32),
+            jax.ShapeDtypeStruct(basis_vals.shape, basis_vals.dtype),
+            late,
+        ]
+        + [early] * count,
+        in_specs=[HBM] * 3,
+        out_specs=[VMEM, VMEM, VMEM, HBM] + [VMEM] * count,
         scratch_shapes=[
+            pltpu.VMEM(intersection.shape, jnp.int32),
             pltpu.VMEM(coeff.shape, coeff.dtype),
             pltpu.VMEM((slots, num_funcs, columns - split), coeff.dtype),
             pltpu.VMEM((num_clusters, lanes), jnp.int32),
             pltpu.SMEM((num_clusters, lanes), jnp.int32),
-            pltpu.SemaphoreType.DMA((4,)),
+            pltpu.SemaphoreType.DMA((5,)),
         ],
         compiler_params=PARAMS,
         name="outgoing",
     )(
-        my_cluster.reshape(1),
         pltpu.with_memory_space_constraint(intersection, pltpu.HBM),
         pltpu.with_memory_space_constraint(coeff, pltpu.HBM),
+        pltpu.with_memory_space_constraint(basis_vals, pltpu.HBM),
     )
 
 
 def packed(positions, blocks, taken, last):
-    list_len = positions.shape[0]
+    list_len = positions.shape[1]
     num_funcs, columns = last.shape[1:]
     slots = len(blocks) * taken + last.shape[0]
 
@@ -210,7 +233,7 @@
             held_ref[at * taken : (at + 1) * taken] = ref[:taken]
         held_ref[len(blocks) * taken :] = last_ref[...]
         for k in range(list_len):
-            out_ref[k] = held_ref[position_ref[k]]
+            out_ref[k] = held_ref[position_ref[0, k]]
 
     return pl.pallas_call(
         kernel,
@@ -239,11 +262,9 @@
 
 def two_blocks(coeff, intersection, basis_vals, factors, capacity):
     num_clusters, list_len = intersection.shape
-    atom_count, num_funcs, columns = coeff.shape
-    my_cluster = lax.axis_index("cluster")
-    my_block = lax.axis_index("blk")
+    _, num_funcs, columns = coeff.shape
     split = max(columns * EARLY_PARTS // 8 // 128, 1) * 128
-    listed, late, *pieces = outgoing(coeff, intersection, my_cluster, capacity, split)
+    early_at, late_at, basis, late, *pieces = outgoing(coeff, intersection, basis_vals, capacity, split)
     arrived = [pieces[0]]
     for m in range(1, len(pieces)):
         arrived.append(swapped(pieces[m], "cluster", 2 * m))
@@ -251,18 +272,11 @@
     late = lax.all_to_all(late, "cluster", split_axis=0, concat_axis=0, tiled=True)
     late = late.reshape(num_clusters * capacity, num_funcs, columns - split)
     relayed = swapped(second_halves(arrived), "cluster", 1)
-    sources = [basis_vals, swapped(basis_vals, "blk", 1)]
-
-    my_row = lax.dynamic_index_in_dim(listed, my_cluster, 0, keepdims=False)
-    owner = my_row // atom_count
-    same = jnp.logical_and(owner[:, None] == owner[None, :], jnp.arange(list_len)[:, None] > jnp.arange(list_len)[None, :])
-    rank = jnp.sum(same.astype(jnp.int32), axis=1)
-    turn = jnp.bitwise_xor(owner, my_cluster)
-    early_at = turn // 2 * capacity + rank + jnp.where(turn % 2 == 1, num_clusters // 2 * capacity, 0)
-    late_at = owner * capacity + rank
+    sources = [basis, swapped(basis, "blk", 1)]
 
     func = jnp.arange(list_len * num_funcs) % num_funcs
-    late_row = jnp.repeat(late_at * num_funcs, num_funcs) + func
+    late_row = jnp.repeat(late_at.reshape(-1) * num_funcs, num_funcs) + func
+    late_row = lax.optimization_barrier(late_row)
     late_order = late_row[:, None] == jnp.arange(num_clusters * capacity * num_funcs)[None, :]
     late_order = lax.optimization_barrier(late_order.astype(jnp.bfloat16))
 
@@ -273,11 +287,9 @@
     late_other = swapped(late, "blk", 1)
     late_orbitals, density = orbitals_of(sources, late, density)
     early_other_orbitals, density = orbitals_of(sources, early_other, density)
-    lanes = columns // 128
-    begin = jnp.stack([my_block * lanes, (1 - my_block) * lanes])
-    starts = (begin[None, :] + jnp.array([0, split // 128])[:, None]).reshape(-1)
+    places = [(0, 0), (1, 0), (0, split), (1, split)]
     known = [early_orbitals, early_other_orbitals, late_orbitals]
-    return exchange(starts, sources, factors, density, known, late_other, 2 * columns)
+    return exchange(places, sources, factors, density, known, late_other, 2 * columns)
 
 
 def many_blocks(coeff, intersection, basis_vals, factors, capacity, steps):
@@ -303,8 +315,7 @@
     needed = needed.reshape(list_len * num_funcs, columns)
     all_columns = lax.all_gather(needed, "blk", axis=1, tiled=True)
     sources = [basis_vals if step == 0 else passed_along(basis_vals, "blk", -step) for step in steps]
-    starts = jnp.zeros((1,), jnp.int32)
-    return exchange(starts, sources, factors, None, [], all_columns, num_blocks * columns)
+    return exchange([(None, 0)], sources, factors, None, [], all_columns, num_blocks * columns)
 
 
 def on_device(coeff, intersection, basis_vals, coulomb, reach):

time: 54 us -> 54.5 us (level)
  waiting for transfers between devices: 23.3 us -> 27.2 us
  starting transfers between devices: 20.5 us -> 18.2 us
    ppermute x11, waiting for transfers between devices: 23.3 us -> 27.2 us  [swapped(): lax.ppermute(value, axis, [(source, source ^ bits) for source in range(co...]
    ppermute x11, starting transfers between devices: 13.8 us -> 11.9 us  [swapped(): lax.ppermute(value, axis, [(source, source ^ bits) for source in range(co...]
    pallas_call x1, Pallas kernels: 2.49 us -> 1.95 us  [exchange(): pl.pallas_call(kernel, out_shape=jax.ShapeDtypeStruct((points, width), jn...]
  transfers between devices with their start and end apart: 12 -> 12, of which waited for: 8 -> 8; matrix products, arithmetic and copies ran while one was open for 2% -> 1% of each run, Pallas kernels for 5% -> 5%
where the time goes in v4:
time: 54.5 us; the launch traced here: 53.7 us
  waiting for transfers between devices  27.2 us (50%)
  starting transfers between devices  18.2 us (33%)
  Pallas kernels  6.8 us (12%)
  between operations  0.74 us (1%)
    ppermute x11, waiting for transfers between devices, swapped(): lax.ppermute(value, axis, [(source, source ^ bits) for source in range(co...  27.2 us
    ppermute x11, starting transfers between devices, swapped(): lax.ppermute(value, axis, [(source, source ^ bits) for source in range(co...  11.9 us
    all_to_all x1, starting transfers between devices, two_blocks(): lax.all_to_all(late, 'cluster', split_axis=0, concat_axis=0, tiled=True)  6.3 us
    pallas_call x1, Pallas kernels, outgoing(): pl.pallas_call(kernel, out_shape=[jax.ShapeDtypeStruct((1, list_len), jnp...  2.44 us
    pallas_call x1, Pallas kernels, exchange(): pl.pallas_call(kernel, out_shape=jax.ShapeDtypeStruct((points, width), jn...  1.95 us
    pallas_call x3, Pallas kernels, orbitals_of(): pl.pallas_call(kernel, out_shape=[jax.ShapeDtypeStruct((num_sources * poi...  1.77 us
  transfers between devices with their start and end apart: 12, of which 8 were waited for; matrix products, arithmetic and copies ran while one was open for 1% of the time, Pallas kernels for 5%

profile of v4, /device:TPU:9, one launch (start us, length us, event | category | flops | bytes accessed | tf_op | source)
XLA Modules:
  0.0 53.7 jit_solution(3407283375776312882)
XLA Ops:
  0.0 2.4 %outgoing.1 = (s32[1,32]{1,0:T(1,128)S(1)}, s32[1,32]{1,0:T(1,128)S(1)}, bf16[256,256]{1,0:T(8,128)(2,1)S(1)}, bf16[64,8,384]{2,1,0:T(8,128)(2,1)}, bf16[8,8,640...) custom-call(s32[16,32]{1,0:T(8,128)} %list_ref.1, ...), custom_call_target="tpu_custom_call" | custom-call | tf_op jit(solution)/shard_map/outgoing/pallas_call | solution.py:197
  2.4 1.3 %collective-permute-start.1 = (bf16[8,8,640]{2,1,0:T(8,128)(2,1)S(1)}, bf16[8,8,640]{2,1,0:T(8,128)(2,1)S(1)}, u32[]{:S(2)}, u32[]{:S(2)}) collective-permute-start(bf16[8,8,640]{2,1,0:T(8,128)(2,1)S(1)} %get-tuple-element.26), channel_id=1, source_target_pairs={{0,4},{2,6},{4,0},{6,2},{8,12},{10,14},{12,8},{14,10},{16,20},{18,... | collective-permute-start | bytes 245768 | tf_op jit(solution)/shard_map/ppermute | solution.py:25
  3.7 0.2 collective-permute-start.2
  3.9 6.3 %all-to-all-start = ((bf16[16,4,8,384]{3,2,1,0:T(8,128)(2,1)}), bf16[16,4,8,384]{3,2,1,0:T(8,128)(2,1)S(1)}, u32[]{:S(2)}, u32[]{:S(2)}) async-start(bf16[16,4,8,384]{3,2,1,0:T(8,128)(2,1)} %bitcast.8), calls=%async_computation | async-start | bytes 786432 | tf_op jit(solution)/shard_map/all_to_all | solution.py:272
  10.2 1.2 %collective-permute-start.3 = (bf16[8,8,640]{2,1,0:T(8,128)(2,1)S(1)}, bf16[8,8,640]{2,1,0:T(8,128)(2,1)S(1)}, u32[]{:S(2)}, u32[]{:S(2)}) collective-permute-start(bf16[8,8,640]{2,1,0:T(8,128)(2,1)S(1)} %get-tuple-element.28), channel_id=1, source_target_pairs={{0,12},{2,14},{4,8},{6,10},{8,4},{10,6},{12,0},{14,2},{16,28},{18,... | collective-permute-start | bytes 245768 | tf_op jit(solution)/shard_map/ppermute | solution.py:25
  11.4 2.1 %collective-permute-start.4 = (bf16[8,8,640]{2,1,0:T(8,128)(2,1)S(1)}, bf16[8,8,640]{2,1,0:T(8,128)(2,1)S(1)}, u32[]{:S(2)}, u32[]{:S(2)}) collective-permute-start(bf16[8,8,640]{2,1,0:T(8,128)(2,1)S(1)} %get-tuple-element.29), channel_id=1, source_target_pairs={{0,16},{2,18},{4,20},{6,22},{8,24},{10,26},{12,28},{14,30},{16,0},... | collective-permute-start | bytes 245768 | tf_op jit(solution)/shard_map/ppermute | solution.py:25
  13.5 0.1 collective-permute-start.5
  13.6 0.0 collective-permute-done.1.refs_1_.rest_1_
  13.6 2.3 %collective-permute-start.6 = (bf16[8,8,640]{2,1,0:T(8,128)(2,1)S(1)}, bf16[8,8,640]{2,1,0:T(8,128)(2,1)S(1)}, u32[]{:S(2)}, u32[]{:S(2)}) collective-permute-start(bf16[8,8,640]{2,1,0:T(8,128)(2,1)S(1)} %get-tuple-element.31), channel_id=1, source_target_pairs={{0,24},{2,26},{4,28},{6,30},{8,16},{10,18},{12,20},{14,22},{16,8},... | collective-permute-start | bytes 245768 | tf_op jit(solution)/shard_map/ppermute | solution.py:25
  15.8 0.0 collective-permute-done.2.refs_2_.rest_2_
  15.8 1.0 %collective-permute-start.7 = (bf16[8,8,640]{2,1,0:T(8,128)(2,1)S(1)}, bf16[8,8,640]{2,1,0:T(8,128)(2,1)S(1)}, u32[]{:S(2)}, u32[]{:S(2)}) collective-permute-start(bf16[8,8,640]{2,1,0:T(8,128)(2,1)S(1)} %get-tuple-element.32), channel_id=1, source_target_pairs={{0,28},{2,30},{4,24},{6,26},{8,20},{10,22},{12,16},{14,18},{16,12}... | collective-permute-start | bytes 245768 | tf_op jit(solution)/shard_map/ppermute | solution.py:25
  16.8 0.1 broadcast_in_dim.16
  16.9 0.1 reshape.54
  17.0 3.4 %collective-permute-done.3.refs_3_.rest_3_ = bf16[8,8,640]{2,1,0:T(8,128)(2,1)S(1)} collective-permute-done((bf16[8,8,640]{2,1,0:T(8,128)(2,1)S(1)}, bf16[8,8,640]{2,1,0:T(8,128)(2,1)S(1)}, u32[]{:S(2)}, u32[]{:S(2)}) %collective-permute-start.3) | collective-permute-done | bytes 81952 | tf_op jit(solution)/shard_map/ppermute | solution.py:25
  20.4 1.2 %collective-permute-start = (bf16[256,256]{1,0:T(8,128)(2,1)S(1)}, bf16[256,256]{1,0:T(8,128)(2,1)S(1)}, u32[]{:S(2)}, u32[]{:S(2)}) collective-permute-start(bf16[256,256]{1,0:T(8,128)(2,1)S(1)} %get-tuple-element.23.refs_0_), channel_id=1, source_target_pairs={{0,1},{1,0},{2,3},{3,2},{4,5},{5,4},{6,7},{7,6},{8,9},{9,8},{10,11... | collective-permute-start | bytes 393224 | tf_op jit(solution)/shard_map/ppermute | solution.py:25
  21.6 5.9 %collective-permute-done.4.refs_4_.rest_4_ = bf16[8,8,640]{2,1,0:T(8,128)(2,1)S(1)} collective-permute-done((bf16[8,8,640]{2,1,0:T(8,128)(2,1)S(1)}, bf16[8,8,640]{2,1,0:T(8,128)(2,1)S(1)}, u32[]{:S(2)}, u32[]{:S(2)}) %collective-permute-start.4) | collective-permute-done | bytes 81952 | tf_op jit(solution)/shard_map/ppermute | solution.py:25
  27.5 1.8 %collective-permute-done.5.refs_5_.rest_5_ = bf16[8,8,640]{2,1,0:T(8,128)(2,1)S(1)} collective-permute-done((bf16[8,8,640]{2,1,0:T(8,128)(2,1)S(1)}, bf16[8,8,640]{2,1,0:T(8,128)(2,1)S(1)}, u32[]{:S(2)}, u32[]{:S(2)}) %collective-permute-start.5) | collective-permute-done | bytes 81952 | tf_op jit(solution)/shard_map/ppermute | solution.py:25
  29.3 3.7 %collective-permute-done.6.refs_6_.rest_6_ = bf16[8,8,640]{2,1,0:T(8,128)(2,1)S(1)} collective-permute-done((bf16[8,8,640]{2,1,0:T(8,128)(2,1)S(1)}, bf16[8,8,640]{2,1,0:T(8,128)(2,1)S(1)}, u32[]{:S(2)}, u32[]{:S(2)}) %collective-permute-start.6) | collective-permute-done | bytes 81952 | tf_op jit(solution)/shard_map/ppermute | solution.py:25
  33.0 2.7 %collective-permute-done.7.refs_7_.rest_7_ = bf16[8,8,640]{2,1,0:T(8,128)(2,1)S(1)} collective-permute-done((bf16[8,8,640]{2,1,0:T(8,128)(2,1)S(1)}, bf16[8,8,640]{2,1,0:T(8,128)(2,1)S(1)}, u32[]{:S(2)}, u32[]{:S(2)}) %collective-permute-start.7) | collective-permute-done | bytes 81952 | tf_op jit(solution)/shard_map/ppermute | solution.py:25
  35.6 1.0 %collective-permute-start.8 = (bf16[32,8,640]{2,1,0:T(8,128)(2,1)S(1)}, bf16[32,8,640]{2,1,0:T(8,128)(2,1)S(1)}, u32[]{:S(2)}, u32[]{:S(2)}) collective-permute-start(bf16[32,8,640]{2,1,0:T(8,128)(2,1)S(1)} %second_halves.1), channel_id=1, source_target_pairs={{0,2},{2,0},{4,6},{6,4},{8,10},{10,8},{12,14},{14,12},{16,18},{18,... | collective-permute-start | bytes 983048 | tf_op jit(solution)/shard_map/ppermute | solution.py:25
  37.3 0.1 fusion
  37.5 0.5 collective-permute-done.8.rest_8_
  37.9 0.0 copy-start
  37.9 0.6 %packed.1 = bf16[32,8,640]{2,1,0:T(8,128)(2,1)S(1)} custom-call(s32[1,32]{1,0:T(1,128)S(1)} %get-tuple-element.24.position_ref, bf16[8,8,640]{2,1,0:T(8,128)(2,1)S(1)} %get-tuple-element.25.refs_0_.rest_0_, bf16[8,8,640]{2,1,0:T(8,128)(2,1)S(1)} %collective-permute-done.1.refs_1_.rest_1_, bf16[8,8,640]{2,1,0:T(8,128)(2,1)S(1)} %collective-permute-done.2.refs_2_.rest_2_, ...), custom_call_target="tpu_custom_call" | custom-call | tf_op jit(solution)/shard_map/packed/pallas_call | solution.py:238
  38.6 1.3 %collective-permute-start.9 = (bf16[256,640]{1,0:T(8,128)(2,1)S(1)}, bf16[256,640]{1,0:T(8,128)(2,1)S(1)}, u32[]{:S(2)}, u32[]{:S(2)}) collective-permute-start(bf16[256,640]{1,0:T(8,128)(2,1)S(1)} %bitcast.15), channel_id=1, source_target_pairs={{0,1},{1,0},{2,3},{3,2},{4,5},{5,4},{6,7},{7,6},{8,9},{9,8},{10,11... | collective-permute-start | bytes 983048 | tf_op jit(solution)/shard_map/ppermute | solution.py:25
  39.9 0.0 all-to-all-done
  39.9 0.3 convolution_convert_fusion.refs_2_
  40.2 0.3 collective-permute-start.10
  40.5 0.0 copy-done
  40.5 0.2 multiply_bitcast_fusion
  40.7 0.0 collective-permute-done.refs_1_
  40.7 0.6 %orbitals_of.3 = (bf16[512,640]{1,0:T(8,128)(2,1)S(1)}, f32[256,512]{1,0:T(8,128)S(1)}) custom-call(bf16[256,256]{1,0:T(8,128)(2,1)S(1)} %get-tuple-element.23.refs_0_, bf16[256,256]{1,0:T(8,128)(2,1)S(1)} %collective-permute-done.refs_1_, bf16[256,640]{1,0:T(8,128)(2,1)S(1)} %bitcast.16), custom_call_target="tpu_custom_call" | custom-call | tf_op jit(solution)/shard_map/orbitals_of/pallas_call | solution.py:54
  41.3 0.5 orbitals_of.4
  41.8 5.7 %collective-permute-done.9.refs_2_ = bf16[256,640]{1,0:T(8,128)(2,1)S(1)} collective-permute-done((bf16[256,640]{1,0:T(8,128)(2,1)S(1)}, bf16[256,640]{1,0:T(8,128)(2,1)S(1)}, u32[]{:S(2)}, u32[]{:S(2)}) %collective-permute-start.9) | collective-permute-done | bytes 327712 | tf_op jit(solution)/shard_map/ppermute | solution.py:25
  47.5 0.6 %orbitals_of.5 = (bf16[512,640]{1,0:T(8,128)(2,1)S(1)}, f32[256,512]{1,0:T(8,128)S(1)}) custom-call(bf16[256,256]{1,0:T(8,128)(2,1)S(1)} %get-tuple-element.23.refs_0_, bf16[256,256]{1,0:T(8,128)(2,1)S(1)} %collective-permute-done.refs_1_, bf16[256,640]{1,0:T(8,128)(2,1)S(1)} %collective-permute-done.9.refs_2_, f32[256,512]{1,0:T(8,128)S(1)} %get-tuple-element.36.refs_3_), custom_call_target="tpu_custom_call" | custom-call | tf_op jit(solution)/shard_map/orbitals_of/pallas_call | solution.py:54
  48.2 3.6 %collective-permute-done.10.refs_8_ = bf16[256,384]{1,0:T(8,128)(2,1)S(1)} collective-permute-done((bf16[256,384]{1,0:T(8,128)(2,1)S(1)}, bf16[256,384]{1,0:T(8,128)(2,1)S(1)}, u32[]{:S(2)}, u32[]{:S(2)}) %collective-permute-start.10) | collective-permute-done | bytes 196640 | tf_op jit(solution)/shard_map/ppermute | solution.py:25
  51.7 1.9 %exchange.1 = bf16[256,2048]{1,0:T(8,128)(2,1)} custom-call(bf16[256,256]{1,0:T(8,128)(2,1)S(1)} %get-tuple-element.23.refs_0_, bf16[256,256]{1,0:T(8,128)(2,1)S(1)} %collective-permute-done.refs_1_, f32[256,256]{1,0:T(8,128)S(1)} %get-tuple-element.42.refs_2_, f32[256,256]{1,0:T(8,128)S(1)} %get-tuple-element.41.refs_3_, ...), custom_call_target="tpu_custom_call" | custom-call | tf_op jit(solution)/shard_map/exchange/pallas_call | solution.py:109
  (3 shorter events, 0.0 us)
Async XLA Ops:
  2.4 11.1 %collective-permute-start.1 = (bf16[8,8,640]{2,1,0:T(8,128)(2,1)S(1)}, bf16[8,8,640]{2,1,0:T(8,128)(2,1)S(1)}, u32[]{:S(2)}, u32[]{:S(2)}) collective-permute-start(bf16[8,8,640]{2,1,0:T(8,128)(2,1)S(1)} %get-tuple-element.26), channel_id=1, source_target_pairs={{0,4},{2,6},{4,0},{6,2},{8,12},{10,14},{12,8},{14,10},{16,20},{18,... | collective-permute-start | bytes 245768 | tf_op jit(solution)/shard_map/ppermute | solution.py:25
  3.7 12.1 %collective-permute-start.2 = (bf16[8,8,640]{2,1,0:T(8,128)(2,1)S(1)}, bf16[8,8,640]{2,1,0:T(8,128)(2,1)S(1)}, u32[]{:S(2)}, u32[]{:S(2)}) collective-permute-start(bf16[8,8,640]{2,1,0:T(8,128)(2,1)S(1)} %get-tuple-element.27), channel_id=1, source_target_pairs={{0,8},{2,10},{4,12},{6,14},{8,0},{10,2},{12,4},{14,6},{16,24},{18,... | collective-permute-start | bytes 245768 | tf_op jit(solution)/shard_map/ppermute | solution.py:25
  3.9 36.0 %all-to-all-start = ((bf16[16,4,8,384]{3,2,1,0:T(8,128)(2,1)}), bf16[16,4,8,384]{3,2,1,0:T(8,128)(2,1)S(1)}, u32[]{:S(2)}, u32[]{:S(2)}) async-start(bf16[16,4,8,384]{3,2,1,0:T(8,128)(2,1)} %bitcast.8), calls=%async_computation | async-start | bytes 786432 | tf_op jit(solution)/shard_map/all_to_all | solution.py:272
  10.2 10.2 %collective-permute-start.3 = (bf16[8,8,640]{2,1,0:T(8,128)(2,1)S(1)}, bf16[8,8,640]{2,1,0:T(8,128)(2,1)S(1)}, u32[]{:S(2)}, u32[]{:S(2)}) collective-permute-start(bf16[8,8,640]{2,1,0:T(8,128)(2,1)S(1)} %get-tuple-element.28), channel_id=1, source_target_pairs={{0,12},{2,14},{4,8},{6,10},{8,4},{10,6},{12,0},{14,2},{16,28},{18,... | collective-permute-start | bytes 245768 | tf_op jit(solution)/shard_map/ppermute | solution.py:25
  11.4 16.2 %collective-permute-start.4 = (bf16[8,8,640]{2,1,0:T(8,128)(2,1)S(1)}, bf16[8,8,640]{2,1,0:T(8,128)(2,1)S(1)}, u32[]{:S(2)}, u32[]{:S(2)}) collective-permute-start(bf16[8,8,640]{2,1,0:T(8,128)(2,1)S(1)} %get-tuple-element.29), channel_id=1, source_target_pairs={{0,16},{2,18},{4,20},{6,22},{8,24},{10,26},{12,28},{14,30},{16,0},... | collective-permute-start | bytes 245768 | tf_op jit(solution)/shard_map/ppermute | solution.py:25
  13.5 15.8 %collective-permute-start.5 = (bf16[8,8,640]{2,1,0:T(8,128)(2,1)S(1)}, bf16[8,8,640]{2,1,0:T(8,128)(2,1)S(1)}, u32[]{:S(2)}, u32[]{:S(2)}) collective-permute-start(bf16[8,8,640]{2,1,0:T(8,128)(2,1)S(1)} %get-tuple-element.30), channel_id=1, source_target_pairs={{0,20},{2,22},{4,16},{6,18},{8,28},{10,30},{12,24},{14,26},{16,4},... | collective-permute-start | bytes 245768 | tf_op jit(solution)/shard_map/ppermute | solution.py:25
  13.6 19.4 %collective-permute-start.6 = (bf16[8,8,640]{2,1,0:T(8,128)(2,1)S(1)}, bf16[8,8,640]{2,1,0:T(8,128)(2,1)S(1)}, u32[]{:S(2)}, u32[]{:S(2)}) collective-permute-start(bf16[8,8,640]{2,1,0:T(8,128)(2,1)S(1)} %get-tuple-element.31), channel_id=1, source_target_pairs={{0,24},{2,26},{4,28},{6,30},{8,16},{10,18},{12,20},{14,22},{16,8},... | collective-permute-start | bytes 245768 | tf_op jit(solution)/shard_map/ppermute | solution.py:25
  15.8 19.8 %collective-permute-start.7 = (bf16[8,8,640]{2,1,0:T(8,128)(2,1)S(1)}, bf16[8,8,640]{2,1,0:T(8,128)(2,1)S(1)}, u32[]{:S(2)}, u32[]{:S(2)}) collective-permute-start(bf16[8,8,640]{2,1,0:T(8,128)(2,1)S(1)} %get-tuple-element.32), channel_id=1, source_target_pairs={{0,28},{2,30},{4,24},{6,26},{8,20},{10,22},{12,16},{14,18},{16,12}... | collective-permute-start | bytes 245768 | tf_op jit(solution)/shard_map/ppermute | solution.py:25
  20.4 20.3 %collective-permute-start = (bf16[256,256]{1,0:T(8,128)(2,1)S(1)}, bf16[256,256]{1,0:T(8,128)(2,1)S(1)}, u32[]{:S(2)}, u32[]{:S(2)}) collective-permute-start(bf16[256,256]{1,0:T(8,128)(2,1)S(1)} %get-tuple-element.23.refs_0_), channel_id=1, source_target_pairs={{0,1},{1,0},{2,3},{3,2},{4,5},{5,4},{6,7},{7,6},{8,9},{9,8},{10,11... | collective-permute-start | bytes 393224 | tf_op jit(solution)/shard_map/ppermute | solution.py:25
  35.6 2.3 %collective-permute-start.8 = (bf16[32,8,640]{2,1,0:T(8,128)(2,1)S(1)}, bf16[32,8,640]{2,1,0:T(8,128)(2,1)S(1)}, u32[]{:S(2)}, u32[]{:S(2)}) collective-permute-start(bf16[32,8,640]{2,1,0:T(8,128)(2,1)S(1)} %second_halves.1), channel_id=1, source_target_pairs={{0,2},{2,0},{4,6},{6,4},{8,10},{10,8},{12,14},{14,12},{16,18},{18,... | collective-permute-start | bytes 983048 | tf_op jit(solution)/shard_map/ppermute | solution.py:25
  37.9 2.5 %copy-start = (bf16[256,7,256]{2,0,1:T(8,128)(2,1)S(1)}, bf16[256,7,256]{2,0,1:T(8,128)(2,1)}, u32[]{:S(2)}) copy-start(bf16[256,7,256]{2,0,1:T(8,128)(2,1)} %param.8) | copy-start | bytes 2752516
  38.6 9.0 %collective-permute-start.9 = (bf16[256,640]{1,0:T(8,128)(2,1)S(1)}, bf16[256,640]{1,0:T(8,128)(2,1)S(1)}, u32[]{:S(2)}, u32[]{:S(2)}) collective-permute-start(bf16[256,640]{1,0:T(8,128)(2,1)S(1)} %bitcast.15), channel_id=1, source_target_pairs={{0,1},{1,0},{2,3},{3,2},{4,5},{5,4},{6,7},{7,6},{8,9},{9,8},{10,11... | collective-permute-start | bytes 983048 | tf_op jit(solution)/shard_map/ppermute | solution.py:25
  40.2 11.6 %collective-permute-start.10 = (bf16[256,384]{1,0:T(8,128)(2,1)S(1)}, bf16[256,384]{1,0:T(8,128)(2,1)S(1)}, u32[]{:S(2)}, u32[]{:S(2)}) collective-permute-start(bf16[256,384]{1,0:T(8,128)(2,1)S(1)} %convolution_convert_fusion.refs_2_), channel_id=1, source_target_pairs={{0,1},{1,0},{2,3},{3,2},{4,5},{5,4},{6,7},{7,6},{8,9},{9,8},{10,11... | collective-permute-start | bytes 589832 | tf_op jit(solution)/shard_map/ppermute | solution.py:25

commit v5 on v4

--- a/solution.py
+++ b/solution.py
@@ -64,13 +64,13 @@
     )(*operands)
 
 
-def exchange(places, sources, factors, density, orbitals, values, width):
+def exchange(sides, sources, factors, density, orbitals, values, width):
     num_sources = len(sources)
     num_known = len(orbitals)
     points = sources[0].shape[0]
-    widths = [block.shape[1] for block in orbitals] + [values.shape[1]]
-
-    num_blocks = lax.axis_size("blk")
+    side_width = width // len(sides)
+    step = side_width // 2 if side_width % 512 == 0 else side_width
+    num_pieces = width // step
 
     def kernel(*refs):
         basis_refs = refs[:num_sources]
@@ -91,14 +91,20 @@
             tiles.append((part * factor_refs[source][...]).astype(jnp.bfloat16))
         tiles = jnp.concatenate(tiles, axis=1)
         copies = []
-        for at, ref in enumerate([*known_refs, last_ref]):
-            held_refs[at][...] = dot_nn(tiles, ref[...]).astype(out_ref.dtype)
-            turn, first = places[at]
-            start = lax.rem(my_block + turn, num_blocks) * (width // num_blocks) + first if turn is not None else first
-            start = pl.multiple_of(start, 128)
-            copy = pltpu.make_async_copy(held_refs[at], out_ref.at[:, pl.ds(start, widths[at])], sems.at[at])
-            copy.start()
-            copies.append(copy)
+        all_refs = [*known_refs, last_ref]
+        for turn, members in enumerate(sides):
+            blocks = [all_refs[at] for at in members]
+            for begin in range(0, side_width, step):
+                at = turn * (side_width // step) + begin // step
+                held_ref = held_refs[at]
+                held_ref[...] = dot_nn(tiles, columns_of(blocks, begin, begin + step)).astype(out_ref.dtype)
+                start = begin
+                if len(sides) > 1:
+                    start = lax.rem(my_block + turn, len(sides)) * side_width + begin
+                start = pl.multiple_of(start, 128)
+                copy = pltpu.make_async_copy(held_ref, out_ref.at[:, pl.ds(start, step)], sems.at[at])
+                copy.start()
+                copies.append(copy)
         for copy in copies:
             copy.wait()
 
@@ -111,11 +117,23 @@
         out_shape=jax.ShapeDtypeStruct((points, width), jnp.bfloat16),
         in_specs=[VMEM] * len(operands),
         out_specs=HBM,
-        scratch_shapes=[pltpu.VMEM((points, columns), jnp.bfloat16) for columns in widths]
-        + [pltpu.VMEM((num_sources * points, widths[-1]), jnp.bfloat16), pltpu.SemaphoreType.DMA((len(widths),))],
-        compiler_params=PARAMS if num_sources == 2 else pltpu.CompilerParams(vmem_limit_bytes=32 * 2**20),
+        scratch_shapes=[pltpu.VMEM((points, step), jnp.bfloat16)] * num_pieces
+        + [pltpu.VMEM((num_sources * points, values.shape[1]), jnp.bfloat16), pltpu.SemaphoreType.DMA((num_pieces,))],
+        compiler_params=pltpu.CompilerParams(vmem_limit_bytes=12 * 2**20) if num_sources == 2 else pltpu.CompilerParams(vmem_limit_bytes=32 * 2**20),
         name="exchange",
     )(*operands)
+
+
+def columns_of(blocks, begin, end):
+    found = []
+    first = 0
+    for block in blocks:
+        width = block.shape[1]
+        low, high = max(begin - first, 0), min(end - first, width)
+        if low < high:
+            found.append(block[:, low:high])
+        first += width
+    return found[0] if len(found) == 1 else jnp.concatenate(found, axis=1)
 
 
 def second_halves(blocks):
@@ -287,9 +305,8 @@
     late_other = swapped(late, "blk", 1)
     late_orbitals, density = orbitals_of(sources, late, density)
     early_other_orbitals, density = orbitals_of(sources, early_other, density)
-    places = [(0, 0), (1, 0), (0, split), (1, split)]
     known = [early_orbitals, early_other_orbitals, late_orbitals]
-    return exchange(places, sources, factors, density, known, late_other, 2 * columns)
+    return exchange([(0, 2), (1, 3)], sources, factors, density, known, late_other, 2 * columns)
 
 
 def many_blocks(coeff, intersection, basis_vals, factors, capacity, steps):
@@ -315,7 +332,7 @@
     needed = needed.reshape(list_len * num_funcs, columns)
     all_columns = lax.all_gather(needed, "blk", axis=1, tiled=True)
     sources = [basis_vals if step == 0 else passed_along(basis_vals, "blk", -step) for step in steps]
-    return exchange([(None, 0)], sources, factors, None, [], all_columns, num_blocks * columns)
+    return exchange([(0,)], sources, factors, None, [], all_columns, num_blocks * columns)
 
 
 def on_device(coeff, intersection, basis_vals, coulomb, reach):

time: 54.5 us -> 54.4 us (level)
  no operation moved by 1% of the time
where the time goes in v5:
time: 54.4 us; the launch traced here: 53.6 us
  waiting for transfers between devices  27.2 us (50%)
  starting transfers between devices  18.2 us (33%)
  Pallas kernels  6.73 us (12%)
  between operations  0.74 us (1%)
    ppermute x11, waiting for transfers between devices, swapped(): lax.ppermute(value, axis, [(source, source ^ bits) for source in range(co...  27.2 us
    ppermute x11, starting transfers between devices, swapped(): lax.ppermute(value, axis, [(source, source ^ bits) for source in range(co...  11.9 us
    all_to_all x1, starting transfers between devices, two_blocks(): lax.all_to_all(late, 'cluster', split_axis=0, concat_axis=0, tiled=True)  6.3 us
    pallas_call x1, Pallas kernels, outgoing(): pl.pallas_call(kernel, out_shape=[jax.ShapeDtypeStruct((1, list_len), jnp...  2.44 us
    pallas_call x1, Pallas kernels, exchange(): pl.pallas_call(kernel, out_shape=jax.ShapeDtypeStruct((points, width), jn...  1.87 us
    pallas_call x3, Pallas kernels, orbitals_of(): pl.pallas_call(kernel, out_shape=[jax.ShapeDtypeStruct((num_sources * poi...  1.77 us
  transfers between devices with their start and end apart: 12, of which 8 were waited for; matrix products, arithmetic and copies ran while one was open for 1% of the time, Pallas kernels for 5%

profile of v5, /device:TPU:9, one launch (start us, length us, event | category | flops | bytes accessed | tf_op | source)
XLA Modules:
  0.0 53.6 jit_solution(15872357880078298374)
XLA Ops:
  0.0 2.4 %outgoing.1 = (s32[1,32]{1,0:T(1,128)S(1)}, s32[1,32]{1,0:T(1,128)S(1)}, bf16[256,256]{1,0:T(8,128)(2,1)S(1)}, bf16[64,8,384]{2,1,0:T(8,128)(2,1)}, bf16[8,8,640...) custom-call(s32[16,32]{1,0:T(8,128)} %list_ref.1, ...), custom_call_target="tpu_custom_call" | custom-call | tf_op jit(solution)/shard_map/outgoing/pallas_call | solution.py:215
  2.4 1.3 %collective-permute-start.1 = (bf16[8,8,640]{2,1,0:T(8,128)(2,1)S(1)}, bf16[8,8,640]{2,1,0:T(8,128)(2,1)S(1)}, u32[]{:S(2)}, u32[]{:S(2)}) collective-permute-start(bf16[8,8,640]{2,1,0:T(8,128)(2,1)S(1)} %get-tuple-element.26), channel_id=1, source_target_pairs={{0,4},{2,6},{4,0},{6,2},{8,12},{10,14},{12,8},{14,10},{16,20},{18,... | collective-permute-start | bytes 245768 | tf_op jit(solution)/shard_map/ppermute | solution.py:25
  3.7 0.2 collective-permute-start.2
  3.9 6.3 %all-to-all-start = ((bf16[16,4,8,384]{3,2,1,0:T(8,128)(2,1)}), bf16[16,4,8,384]{3,2,1,0:T(8,128)(2,1)S(1)}, u32[]{:S(2)}, u32[]{:S(2)}) async-start(bf16[16,4,8,384]{3,2,1,0:T(8,128)(2,1)} %bitcast.8), calls=%async_computation | async-start | bytes 786432 | tf_op jit(solution)/shard_map/all_to_all | solution.py:290
  10.2 1.2 %collective-permute-start.3 = (bf16[8,8,640]{2,1,0:T(8,128)(2,1)S(1)}, bf16[8,8,640]{2,1,0:T(8,128)(2,1)S(1)}, u32[]{:S(2)}, u32[]{:S(2)}) collective-permute-start(bf16[8,8,640]{2,1,0:T(8,128)(2,1)S(1)} %get-tuple-element.28), channel_id=1, source_target_pairs={{0,12},{2,14},{4,8},{6,10},{8,4},{10,6},{12,0},{14,2},{16,28},{18,... | collective-permute-start | bytes 245768 | tf_op jit(solution)/shard_map/ppermute | solution.py:25
  11.4 2.1 %collective-permute-start.4 = (bf16[8,8,640]{2,1,0:T(8,128)(2,1)S(1)}, bf16[8,8,640]{2,1,0:T(8,128)(2,1)S(1)}, u32[]{:S(2)}, u32[]{:S(2)}) collective-permute-start(bf16[8,8,640]{2,1,0:T(8,128)(2,1)S(1)} %get-tuple-element.29), channel_id=1, source_target_pairs={{0,16},{2,18},{4,20},{6,22},{8,24},{10,26},{12,28},{14,30},{16,0},... | collective-permute-start | bytes 245768 | tf_op jit(solution)/shard_map/ppermute | solution.py:25
  13.5 0.1 collective-permute-start.5
  13.6 0.0 collective-permute-done.1.refs_1_.rest_1_
  13.6 2.3 %collective-permute-start.6 = (bf16[8,8,640]{2,1,0:T(8,128)(2,1)S(1)}, bf16[8,8,640]{2,1,0:T(8,128)(2,1)S(1)}, u32[]{:S(2)}, u32[]{:S(2)}) collective-permute-start(bf16[8,8,640]{2,1,0:T(8,128)(2,1)S(1)} %get-tuple-element.31), channel_id=1, source_target_pairs={{0,24},{2,26},{4,28},{6,30},{8,16},{10,18},{12,20},{14,22},{16,8},... | collective-permute-start | bytes 245768 | tf_op jit(solution)/shard_map/ppermute | solution.py:25
  15.8 0.0 collective-permute-done.2.refs_2_.rest_2_
  15.8 1.0 %collective-permute-start.7 = (bf16[8,8,640]{2,1,0:T(8,128)(2,1)S(1)}, bf16[8,8,640]{2,1,0:T(8,128)(2,1)S(1)}, u32[]{:S(2)}, u32[]{:S(2)}) collective-permute-start(bf16[8,8,640]{2,1,0:T(8,128)(2,1)S(1)} %get-tuple-element.32), channel_id=1, source_target_pairs={{0,28},{2,30},{4,24},{6,26},{8,20},{10,22},{12,16},{14,18},{16,12}... | collective-permute-start | bytes 245768 | tf_op jit(solution)/shard_map/ppermute | solution.py:25
  16.8 0.1 broadcast_in_dim.16
  16.9 0.1 reshape.54
  17.0 3.4 %collective-permute-done.3.refs_3_.rest_3_ = bf16[8,8,640]{2,1,0:T(8,128)(2,1)S(1)} collective-permute-done((bf16[8,8,640]{2,1,0:T(8,128)(2,1)S(1)}, bf16[8,8,640]{2,1,0:T(8,128)(2,1)S(1)}, u32[]{:S(2)}, u32[]{:S(2)}) %collective-permute-start.3) | collective-permute-done | bytes 81952 | tf_op jit(solution)/shard_map/ppermute | solution.py:25
  20.4 1.2 %collective-permute-start = (bf16[256,256]{1,0:T(8,128)(2,1)S(1)}, bf16[256,256]{1,0:T(8,128)(2,1)S(1)}, u32[]{:S(2)}, u32[]{:S(2)}) collective-permute-start(bf16[256,256]{1,0:T(8,128)(2,1)S(1)} %get-tuple-element.23.refs_0_), channel_id=1, source_target_pairs={{0,1},{1,0},{2,3},{3,2},{4,5},{5,4},{6,7},{7,6},{8,9},{9,8},{10,11... | collective-permute-start | bytes 393224 | tf_op jit(solution)/shard_map/ppermute | solution.py:25
  21.6 5.9 %collective-permute-done.4.refs_4_.rest_4_ = bf16[8,8,640]{2,1,0:T(8,128)(2,1)S(1)} collective-permute-done((bf16[8,8,640]{2,1,0:T(8,128)(2,1)S(1)}, bf16[8,8,640]{2,1,0:T(8,128)(2,1)S(1)}, u32[]{:S(2)}, u32[]{:S(2)}) %collective-permute-start.4) | collective-permute-done | bytes 81952 | tf_op jit(solution)/shard_map/ppermute | solution.py:25
  27.5 1.8 %collective-permute-done.5.refs_5_.rest_5_ = bf16[8,8,640]{2,1,0:T(8,128)(2,1)S(1)} collective-permute-done((bf16[8,8,640]{2,1,0:T(8,128)(2,1)S(1)}, bf16[8,8,640]{2,1,0:T(8,128)(2,1)S(1)}, u32[]{:S(2)}, u32[]{:S(2)}) %collective-permute-start.5) | collective-permute-done | bytes 81952 | tf_op jit(solution)/shard_map/ppermute | solution.py:25
  29.3 3.7 %collective-permute-done.6.refs_6_.rest_6_ = bf16[8,8,640]{2,1,0:T(8,128)(2,1)S(1)} collective-permute-done((bf16[8,8,640]{2,1,0:T(8,128)(2,1)S(1)}, bf16[8,8,640]{2,1,0:T(8,128)(2,1)S(1)}, u32[]{:S(2)}, u32[]{:S(2)}) %collective-permute-start.6) | collective-permute-done | bytes 81952 | tf_op jit(solution)/shard_map/ppermute | solution.py:25
  33.0 2.7 %collective-permute-done.7.refs_7_.rest_7_ = bf16[8,8,640]{2,1,0:T(8,128)(2,1)S(1)} collective-permute-done((bf16[8,8,640]{2,1,0:T(8,128)(2,1)S(1)}, bf16[8,8,640]{2,1,0:T(8,128)(2,1)S(1)}, u32[]{:S(2)}, u32[]{:S(2)}) %collective-permute-start.7) | collective-permute-done | bytes 81952 | tf_op jit(solution)/shard_map/ppermute | solution.py:25
  35.6 1.0 %collective-permute-start.8 = (bf16[32,8,640]{2,1,0:T(8,128)(2,1)S(1)}, bf16[32,8,640]{2,1,0:T(8,128)(2,1)S(1)}, u32[]{:S(2)}, u32[]{:S(2)}) collective-permute-start(bf16[32,8,640]{2,1,0:T(8,128)(2,1)S(1)} %second_halves.1), channel_id=1, source_target_pairs={{0,2},{2,0},{4,6},{6,4},{8,10},{10,8},{12,14},{14,12},{16,18},{18,... | collective-permute-start | bytes 983048 | tf_op jit(solution)/shard_map/ppermute | solution.py:25
  37.3 0.1 fusion
  37.5 0.5 collective-permute-done.8.rest_8_
  37.9 0.0 copy-start
  37.9 0.6 %packed.1 = bf16[32,8,640]{2,1,0:T(8,128)(2,1)S(1)} custom-call(s32[1,32]{1,0:T(1,128)S(1)} %get-tuple-element.24.position_ref, bf16[8,8,640]{2,1,0:T(8,128)(2,1)S(1)} %get-tuple-element.25.refs_0_.rest_0_, bf16[8,8,640]{2,1,0:T(8,128)(2,1)S(1)} %collective-permute-done.1.refs_1_.rest_1_, bf16[8,8,640]{2,1,0:T(8,128)(2,1)S(1)} %collective-permute-done.2.refs_2_.rest_2_, ...), custom_call_target="tpu_custom_call" | custom-call | tf_op jit(solution)/shard_map/packed/pallas_call | solution.py:256
  38.6 1.3 %collective-permute-start.9 = (bf16[256,640]{1,0:T(8,128)(2,1)S(1)}, bf16[256,640]{1,0:T(8,128)(2,1)S(1)}, u32[]{:S(2)}, u32[]{:S(2)}) collective-permute-start(bf16[256,640]{1,0:T(8,128)(2,1)S(1)} %bitcast.15), channel_id=1, source_target_pairs={{0,1},{1,0},{2,3},{3,2},{4,5},{5,4},{6,7},{7,6},{8,9},{9,8},{10,11... | collective-permute-start | bytes 983048 | tf_op jit(solution)/shard_map/ppermute | solution.py:25
  39.9 0.0 all-to-all-done
  39.9 0.3 convolution_convert_fusion.refs_2_
  40.2 0.3 collective-permute-start.10
  40.5 0.0 copy-done
  40.5 0.2 multiply_bitcast_fusion
  40.7 0.0 collective-permute-done.refs_1_
  40.7 0.6 %orbitals_of.3 = (bf16[512,640]{1,0:T(8,128)(2,1)S(1)}, f32[256,512]{1,0:T(8,128)S(1)}) custom-call(bf16[256,256]{1,0:T(8,128)(2,1)S(1)} %get-tuple-element.23.refs_0_, bf16[256,256]{1,0:T(8,128)(2,1)S(1)} %collective-permute-done.refs_1_, bf16[256,640]{1,0:T(8,128)(2,1)S(1)} %bitcast.16), custom_call_target="tpu_custom_call" | custom-call | tf_op jit(solution)/shard_map/orbitals_of/pallas_call | solution.py:54
  41.3 0.5 orbitals_of.4
  41.8 5.7 %collective-permute-done.9.refs_2_ = bf16[256,640]{1,0:T(8,128)(2,1)S(1)} collective-permute-done((bf16[256,640]{1,0:T(8,128)(2,1)S(1)}, bf16[256,640]{1,0:T(8,128)(2,1)S(1)}, u32[]{:S(2)}, u32[]{:S(2)}) %collective-permute-start.9) | collective-permute-done | bytes 327712 | tf_op jit(solution)/shard_map/ppermute | solution.py:25
  47.5 0.6 %orbitals_of.5 = (bf16[512,640]{1,0:T(8,128)(2,1)S(1)}, f32[256,512]{1,0:T(8,128)S(1)}) custom-call(bf16[256,256]{1,0:T(8,128)(2,1)S(1)} %get-tuple-element.23.refs_0_, bf16[256,256]{1,0:T(8,128)(2,1)S(1)} %collective-permute-done.refs_1_, bf16[256,640]{1,0:T(8,128)(2,1)S(1)} %collective-permute-done.9.refs_2_, f32[256,512]{1,0:T(8,128)S(1)} %get-tuple-element.36.refs_3_), custom_call_target="tpu_custom_call" | custom-call | tf_op jit(solution)/shard_map/orbitals_of/pallas_call | solution.py:54
  48.2 3.6 %collective-permute-done.10.refs_8_ = bf16[256,384]{1,0:T(8,128)(2,1)S(1)} collective-permute-done((bf16[256,384]{1,0:T(8,128)(2,1)S(1)}, bf16[256,384]{1,0:T(8,128)(2,1)S(1)}, u32[]{:S(2)}, u32[]{:S(2)}) %collective-permute-start.10) | collective-permute-done | bytes 196640 | tf_op jit(solution)/shard_map/ppermute | solution.py:25
  51.7 1.9 %exchange.1 = bf16[256,2048]{1,0:T(8,128)(2,1)} custom-call(bf16[256,256]{1,0:T(8,128)(2,1)S(1)} %get-tuple-element.23.refs_0_, bf16[256,256]{1,0:T(8,128)(2,1)S(1)} %collective-permute-done.refs_1_, f32[256,256]{1,0:T(8,128)S(1)} %get-tuple-element.42.refs_2_, f32[256,256]{1,0:T(8,128)S(1)} %get-tuple-element.41.refs_3_, ...), custom_call_target="tpu_custom_call" | custom-call | tf_op jit(solution)/shard_map/exchange/pallas_call | solution.py:115
  (3 shorter events, 0.0 us)
Async XLA Ops:
  2.4 11.1 %collective-permute-start.1 = (bf16[8,8,640]{2,1,0:T(8,128)(2,1)S(1)}, bf16[8,8,640]{2,1,0:T(8,128)(2,1)S(1)}, u32[]{:S(2)}, u32[]{:S(2)}) collective-permute-start(bf16[8,8,640]{2,1,0:T(8,128)(2,1)S(1)} %get-tuple-element.26), channel_id=1, source_target_pairs={{0,4},{2,6},{4,0},{6,2},{8,12},{10,14},{12,8},{14,10},{16,20},{18,... | collective-permute-start | bytes 245768 | tf_op jit(solution)/shard_map/ppermute | solution.py:25
  3.7 12.1 %collective-permute-start.2 = (bf16[8,8,640]{2,1,0:T(8,128)(2,1)S(1)}, bf16[8,8,640]{2,1,0:T(8,128)(2,1)S(1)}, u32[]{:S(2)}, u32[]{:S(2)}) collective-permute-start(bf16[8,8,640]{2,1,0:T(8,128)(2,1)S(1)} %get-tuple-element.27), channel_id=1, source_target_pairs={{0,8},{2,10},{4,12},{6,14},{8,0},{10,2},{12,4},{14,6},{16,24},{18,... | collective-permute-start | bytes 245768 | tf_op jit(solution)/shard_map/ppermute | solution.py:25
  3.9 36.0 %all-to-all-start = ((bf16[16,4,8,384]{3,2,1,0:T(8,128)(2,1)}), bf16[16,4,8,384]{3,2,1,0:T(8,128)(2,1)S(1)}, u32[]{:S(2)}, u32[]{:S(2)}) async-start(bf16[16,4,8,384]{3,2,1,0:T(8,128)(2,1)} %bitcast.8), calls=%async_computation | async-start | bytes 786432 | tf_op jit(solution)/shard_map/all_to_all | solution.py:290
  10.2 10.2 %collective-permute-start.3 = (bf16[8,8,640]{2,1,0:T(8,128)(2,1)S(1)}, bf16[8,8,640]{2,1,0:T(8,128)(2,1)S(1)}, u32[]{:S(2)}, u32[]{:S(2)}) collective-permute-start(bf16[8,8,640]{2,1,0:T(8,128)(2,1)S(1)} %get-tuple-element.28), channel_id=1, source_target_pairs={{0,12},{2,14},{4,8},{6,10},{8,4},{10,6},{12,0},{14,2},{16,28},{18,... | collective-permute-start | bytes 245768 | tf_op jit(solution)/shard_map/ppermute | solution.py:25
  11.4 16.2 %collective-permute-start.4 = (bf16[8,8,640]{2,1,0:T(8,128)(2,1)S(1)}, bf16[8,8,640]{2,1,0:T(8,128)(2,1)S(1)}, u32[]{:S(2)}, u32[]{:S(2)}) collective-permute-start(bf16[8,8,640]{2,1,0:T(8,128)(2,1)S(1)} %get-tuple-element.29), channel_id=1, source_target_pairs={{0,16},{2,18},{4,20},{6,22},{8,24},{10,26},{12,28},{14,30},{16,0},... | collective-permute-start | bytes 245768 | tf_op jit(solution)/shard_map/ppermute | solution.py:25
  13.5 15.8 %collective-permute-start.5 = (bf16[8,8,640]{2,1,0:T(8,128)(2,1)S(1)}, bf16[8,8,640]{2,1,0:T(8,128)(2,1)S(1)}, u32[]{:S(2)}, u32[]{:S(2)}) collective-permute-start(bf16[8,8,640]{2,1,0:T(8,128)(2,1)S(1)} %get-tuple-element.30), channel_id=1, source_target_pairs={{0,20},{2,22},{4,16},{6,18},{8,28},{10,30},{12,24},{14,26},{16,4},... | collective-permute-start | bytes 245768 | tf_op jit(solution)/shard_map/ppermute | solution.py:25
  13.6 19.4 %collective-permute-start.6 = (bf16[8,8,640]{2,1,0:T(8,128)(2,1)S(1)}, bf16[8,8,640]{2,1,0:T(8,128)(2,1)S(1)}, u32[]{:S(2)}, u32[]{:S(2)}) collective-permute-start(bf16[8,8,640]{2,1,0:T(8,128)(2,1)S(1)} %get-tuple-element.31), channel_id=1, source_target_pairs={{0,24},{2,26},{4,28},{6,30},{8,16},{10,18},{12,20},{14,22},{16,8},... | collective-permute-start | bytes 245768 | tf_op jit(solution)/shard_map/ppermute | solution.py:25
  15.8 19.8 %collective-permute-start.7 = (bf16[8,8,640]{2,1,0:T(8,128)(2,1)S(1)}, bf16[8,8,640]{2,1,0:T(8,128)(2,1)S(1)}, u32[]{:S(2)}, u32[]{:S(2)}) collective-permute-start(bf16[8,8,640]{2,1,0:T(8,128)(2,1)S(1)} %get-tuple-element.32), channel_id=1, source_target_pairs={{0,28},{2,30},{4,24},{6,26},{8,20},{10,22},{12,16},{14,18},{16,12}... | collective-permute-start | bytes 245768 | tf_op jit(solution)/shard_map/ppermute | solution.py:25
  20.4 20.3 %collective-permute-start = (bf16[256,256]{1,0:T(8,128)(2,1)S(1)}, bf16[256,256]{1,0:T(8,128)(2,1)S(1)}, u32[]{:S(2)}, u32[]{:S(2)}) collective-permute-start(bf16[256,256]{1,0:T(8,128)(2,1)S(1)} %get-tuple-element.23.refs_0_), channel_id=1, source_target_pairs={{0,1},{1,0},{2,3},{3,2},{4,5},{5,4},{6,7},{7,6},{8,9},{9,8},{10,11... | collective-permute-start | bytes 393224 | tf_op jit(solution)/shard_map/ppermute | solution.py:25
  35.6 2.3 %collective-permute-start.8 = (bf16[32,8,640]{2,1,0:T(8,128)(2,1)S(1)}, bf16[32,8,640]{2,1,0:T(8,128)(2,1)S(1)}, u32[]{:S(2)}, u32[]{:S(2)}) collective-permute-start(bf16[32,8,640]{2,1,0:T(8,128)(2,1)S(1)} %second_halves.1), channel_id=1, source_target_pairs={{0,2},{2,0},{4,6},{6,4},{8,10},{10,8},{12,14},{14,12},{16,18},{18,... | collective-permute-start | bytes 983048 | tf_op jit(solution)/shard_map/ppermute | solution.py:25
  37.9 2.5 %copy-start = (bf16[256,7,256]{2,0,1:T(8,128)(2,1)S(1)}, bf16[256,7,256]{2,0,1:T(8,128)(2,1)}, u32[]{:S(2)}) copy-start(bf16[256,7,256]{2,0,1:T(8,128)(2,1)} %param.8) | copy-start | bytes 2752516
  38.6 9.0 %collective-permute-start.9 = (bf16[256,640]{1,0:T(8,128)(2,1)S(1)}, bf16[256,640]{1,0:T(8,128)(2,1)S(1)}, u32[]{:S(2)}, u32[]{:S(2)}) collective-permute-start(bf16[256,640]{1,0:T(8,128)(2,1)S(1)} %bitcast.15), channel_id=1, source_target_pairs={{0,1},{1,0},{2,3},{3,2},{4,5},{5,4},{6,7},{7,6},{8,9},{9,8},{10,11... | collective-permute-start | bytes 983048 | tf_op jit(solution)/shard_map/ppermute | solution.py:25
  40.2 11.6 %collective-permute-start.10 = (bf16[256,384]{1,0:T(8,128)(2,1)S(1)}, bf16[256,384]{1,0:T(8,128)(2,1)S(1)}, u32[]{:S(2)}, u32[]{:S(2)}) collective-permute-start(bf16[256,384]{1,0:T(8,128)(2,1)S(1)} %convolution_convert_fusion.refs_2_), channel_id=1, source_target_pairs={{0,1},{1,0},{2,3},{3,2},{4,5},{5,4},{6,7},{7,6},{8,9},{9,8},{10,11... | collective-permute-start | bytes 589832 | tf_op jit(solution)/shard_map/ppermute | solution.py:25
